TPU v7x, 32 devices: a whole 2x2x4 slice. The times are simulated.
32 devices in a mesh: rep: 4 (over z), fsdp: 8 (over y, x, core).
Axes of the slice: x: 2, y: 2, z: 4, core: 2. Of those that a mesh axis runs over, the one named last changes fastest.
Arguments:
- tokens: bfloat16 [4, 2048, 1024], P('rep', 'fsdp'), may hold values from -6 to 6
- segment_ids: int32 [4, 2048], P('rep'), may hold values from 0 to 7, never falling along the last dimension, each value on 1 to 1280 neighbouring positions
- qkv_weight: bfloat16 [1024, 3072], P('fsdp'), may hold values from -0.1875 to 0.1875
- out_weight: bfloat16 [1024, 1024], P('fsdp'), may hold values from -1.5 to 1.5
- up_weight: bfloat16 [1024, 4096], P('fsdp'), may hold values from -0.1875 to 0.1875
- down_weight: bfloat16 [4096, 1024], P('fsdp'), may hold values from -0.09375 to 0.09375
- proj_bias: float32 [4, 1024], replicated, may hold values from -1.2 to 1.2
- hidden_bias: float32 [4096], replicated, may hold values from -1.2 to 1.2
- norm_gain: float32 [2, 1024], replicated, may hold values from 0.5 to 1.5
- norm_shift: float32 [2, 1024], replicated, may hold values from -1.2 to 1.2
- cotangent: bfloat16 [4, 2048, 1024], P('rep', 'fsdp'), may hold values from -6 to 6
Outputs:
- output: bfloat16 [4, 2048, 1024], P('rep', 'fsdp')
- input_grad: bfloat16 [4, 2048, 1024], P('rep', 'fsdp')
- qkv_grad: float32 [1024, 3072], P('fsdp')
- out_grad: float32 [1024, 1024], P('fsdp')
- up_grad: float32 [1024, 4096], P('fsdp')
- down_grad: float32 [4096, 1024], P('fsdp')
- proj_bias_grad: float32 [4, 1024], replicated
- hidden_bias_grad: float32 [4096], replicated
- gain_grad: float32 [2, 1024], replicated
- shift_grad: float32 [2, 1024], replicated
Inputs may be any that keep to these rules, and one draw needn't show every extreme that they name: `segment_ids`: in each sequence documents are numbered 0 to 7 in order, each 1 to 1280 tokens long, one exactly 1280.
All inputs are finite; a program needn't handle non-finite values.
Results may differ from a plain program's by a relative error of at most 0.018.
Values may be sent and summed in bfloat16 or wider, within the bound.
A program may use at most 192 MiB of HBM per device.

v0:
```python
import math

import jax
import jax.numpy as jnp
from jax import lax
from jax.sharding import PartitionSpec as P

HEADS = 16


NEGATIVE = -1e30


def normalize(hidden, gain, shift):
    center = hidden - jnp.mean(hidden, axis=-1, keepdims=True)
    spread = jnp.mean(center * center, axis=-1, keepdims=True)
    return center * lax.rsqrt(spread + 1e-05) * gain + shift


def exact_gelu(value):
    return jax.nn.gelu(value, approximate=False)


def gather_attention(qkv_weight, out_weight):
    return (
        lax.all_gather(qkv_weight, "fsdp", axis=0, tiled=True),
        lax.all_gather(out_weight, "fsdp", axis=0, tiled=True),
    )


def gather_feedforward(up_weight, down_weight):
    return (
        lax.all_gather(up_weight, "fsdp", axis=0, tiled=True),
        lax.all_gather(down_weight, "fsdp", axis=0, tiled=True),
    )


def block_plan(row_count):
    block_rows = math.gcd(row_count, 1024)
    return (block_rows, row_count // block_rows)


def split_heads(matrix):
    return matrix.reshape(matrix.shape[0], HEADS, matrix.shape[1] // HEADS)


def join_heads(stacked):
    return jnp.transpose(stacked, (1, 0, 2)).reshape(
        stacked.shape[1], stacked.shape[0] * stacked.shape[2]
    )


def local(
    tokens,
    segment_ids,
    qkv_weight,
    out_weight,
    up_weight,
    down_weight,
    proj_bias,
    hidden_bias,
    norm_gain,
    norm_shift,
    cotangent,
):
    inputs = tokens[0]
    tok_count, model_width = inputs.shape
    head_dim = model_width // HEADS
    score_scale = head_dim ** (-0.5)
    doc_ids = segment_ids[0]
    own_index = lax.axis_index("fsdp")
    own_docs = lax.dynamic_slice_in_dim(doc_ids, own_index * tok_count, tok_count)
    qkv_full, out_full = gather_attention(qkv_weight, out_weight)
    projected = jnp.dot(inputs, qkv_full, preferred_element_type=jnp.float32)
    queries = (projected[:, :model_width] + proj_bias[0]).astype(jnp.bfloat16)
    key_rows = projected[:, model_width : 2 * model_width].astype(jnp.bfloat16)
    value_rows = (projected[:, 2 * model_width :] + proj_bias[1]).astype(jnp.bfloat16)
    query_heads = split_heads(queries)
    key_own = split_heads(key_rows)
    value_own = split_heads(value_rows)
    initial = (
        jnp.zeros((HEADS, tok_count, head_dim), jnp.float32),
        jnp.full((HEADS, tok_count), NEGATIVE, jnp.float32),
        jnp.zeros((HEADS, tok_count), jnp.float32),
    )
    key_piece = lax.all_gather(key_rows, "fsdp", axis=0, tiled=True)
    value_piece = lax.all_gather(value_rows, "fsdp", axis=0, tiled=True)
    block_rows, blocks = block_plan(key_piece.shape[0])

    def forward_advance(block_index, running_state):
        weighted, running, denominator = running_state
        offset = block_index * block_rows
        key_block = split_heads(lax.dynamic_slice_in_dim(key_piece, offset, block_rows))
        value_block = split_heads(lax.dynamic_slice_in_dim(value_piece, offset, block_rows))
        block_docs = lax.dynamic_slice_in_dim(doc_ids, offset, block_rows)
        scores = (
            jnp.einsum("qhd,khd->hqk", query_heads, key_block, preferred_element_type=jnp.float32)
            * score_scale
        )
        same_doc = (own_docs[:, None] == block_docs[None, :])[None]
        highest = jnp.maximum(running, jnp.max(jnp.where(same_doc, scores, NEGATIVE), axis=2))
        factor = jnp.exp(running - highest)
        weights = jnp.where(same_doc, jnp.exp(scores - highest[:, :, None]), 0.0)
        denominator = denominator * factor + jnp.sum(weights, axis=2)
        weighted = weighted * factor[:, :, None] + jnp.einsum(
            "hqk,khd->hqd",
            weights.astype(jnp.bfloat16),
            value_block,
            preferred_element_type=jnp.float32,
        )
        return (weighted, highest, denominator)

    weighted, running, denominator = lax.fori_loop(0, blocks, forward_advance, initial)
    attended_heads = weighted / denominator[:, :, None]
    log_total = running + jnp.log(denominator)
    attended_low = join_heads(attended_heads).astype(jnp.bfloat16)
    branch = jnp.dot(attended_low, out_full, preferred_element_type=jnp.float32) + proj_bias[2]
    first_norm, norm_one_back = jax.vjp(
        normalize, inputs.astype(jnp.float32) + branch, norm_gain[0], norm_shift[0]
    )
    first_low = first_norm.astype(jnp.bfloat16)
    up_full, down_full = gather_feedforward(up_weight, down_weight)
    hidden_pre = jnp.dot(first_low, up_full, preferred_element_type=jnp.float32) + hidden_bias
    activated, gelu_back = jax.vjp(exact_gelu, hidden_pre)
    activated_low = activated.astype(jnp.bfloat16)
    second = jnp.dot(activated_low, down_full, preferred_element_type=jnp.float32) + proj_bias[3]
    output, norm_two_back = jax.vjp(normalize, first_norm + second, norm_gain[1], norm_shift[1])
    up_back, down_back = gather_feedforward(up_weight, down_weight)
    qkv_back, out_back = gather_attention(qkv_weight, out_weight)
    grad_second, gain_two, shift_two = norm_two_back(cotangent[0].astype(jnp.float32))
    second_low = grad_second.astype(jnp.bfloat16)
    down_term = jnp.einsum(
        "tf,td->fd", activated_low, second_low, preferred_element_type=jnp.float32
    )
    activated_grad = jnp.einsum(
        "td,fd->tf", second_low, down_back, preferred_element_type=jnp.float32
    )
    (pre_grad,) = gelu_back(activated_grad)
    pre_low = pre_grad.astype(jnp.bfloat16)
    up_term = jnp.einsum("td,tf->df", first_low, pre_low, preferred_element_type=jnp.float32)
    first_grad = grad_second + jnp.einsum(
        "tf,df->td", pre_low, up_back, preferred_element_type=jnp.float32
    )
    branch_grad, gain_one, shift_one = norm_one_back(first_grad)
    branch_low = branch_grad.astype(jnp.bfloat16)
    out_term = jnp.einsum("te,td->ed", attended_low, branch_low, preferred_element_type=jnp.float32)
    attended_grad = jnp.einsum(
        "td,ed->te", branch_low, out_back, preferred_element_type=jnp.float32
    ).astype(jnp.bfloat16)
    grad_heads = split_heads(attended_grad)
    correction = jnp.einsum("qhd,hqd->hq", grad_heads.astype(jnp.float32), attended_heads)
    lse_all, correction_all = (
        lax.all_gather(log_total, "fsdp", axis=1, tiled=True),
        lax.all_gather(correction, "fsdp", axis=1, tiled=True),
    )
    query_key_piece = lax.all_gather(key_rows, "fsdp", axis=0, tiled=True)
    query_value_piece = lax.all_gather(value_rows, "fsdp", axis=0, tiled=True)
    query_block_rows, blocks = block_plan(query_key_piece.shape[0])

    def query_advance(block_index, query_state):
        offset = block_index * query_block_rows
        key_block = split_heads(lax.dynamic_slice_in_dim(query_key_piece, offset, query_block_rows))
        value_block = split_heads(
            lax.dynamic_slice_in_dim(query_value_piece, offset, query_block_rows)
        )
        block_docs = lax.dynamic_slice_in_dim(doc_ids, offset, query_block_rows)
        scores = (
            jnp.einsum("qhd,khd->hqk", query_heads, key_block, preferred_element_type=jnp.float32)
            * score_scale
        )
        same_doc = (own_docs[:, None] == block_docs[None, :])[None]
        probabilities = jnp.where(same_doc, jnp.exp(scores - log_total[:, :, None]), 0.0)
        prob_grad = jnp.einsum(
            "qhd,khd->hqk", grad_heads, value_block, preferred_element_type=jnp.float32
        )
        score_grad = (probabilities * (prob_grad - correction[:, :, None])).astype(jnp.bfloat16)
        return query_state + jnp.einsum(
            "hqk,khd->hqd", score_grad, key_block, preferred_element_type=jnp.float32
        )

    query_acc = lax.fori_loop(
        0, blocks, query_advance, jnp.zeros((HEADS, tok_count, head_dim), jnp.float32)
    )
    query_grad = (join_heads(query_acc) * score_scale).astype(jnp.bfloat16)
    empty_heads = jnp.zeros((HEADS, tok_count, head_dim), jnp.float32)
    query_piece = lax.all_gather(queries, "fsdp", axis=0, tiled=True)
    grad_piece = lax.all_gather(attended_grad, "fsdp", axis=0, tiled=True)
    key_block_rows, blocks = block_plan(query_piece.shape[0])

    def key_advance(block_index, key_state):
        key_acc, value_acc = key_state
        offset = block_index * key_block_rows
        query_block = split_heads(lax.dynamic_slice_in_dim(query_piece, offset, key_block_rows))
        grad_block = split_heads(lax.dynamic_slice_in_dim(grad_piece, offset, key_block_rows))
        block_docs = lax.dynamic_slice_in_dim(doc_ids, offset, key_block_rows)
        lse_block = lax.dynamic_slice_in_dim(lse_all, offset, key_block_rows, axis=1)
        corr_block = lax.dynamic_slice_in_dim(correction_all, offset, key_block_rows, axis=1)
        scores = (
            jnp.einsum("qhd,khd->hqk", query_block, key_own, preferred_element_type=jnp.float32)
            * score_scale
        )
        same_doc = (block_docs[:, None] == own_docs[None, :])[None]
        probabilities = jnp.where(same_doc, jnp.exp(scores - lse_block[:, :, None]), 0.0)
        value_acc = value_acc + jnp.einsum(
            "hqk,qhd->hkd",
            probabilities.astype(jnp.bfloat16),
            grad_block,
            preferred_element_type=jnp.float32,
        )
        prob_grad = jnp.einsum(
            "qhd,khd->hqk", grad_block, value_own, preferred_element_type=jnp.float32
        )
        score_grad = (probabilities * (prob_grad - corr_block[:, :, None])).astype(jnp.bfloat16)
        key_acc = key_acc + jnp.einsum(
            "hqk,qhd->hkd", score_grad, query_block, preferred_element_type=jnp.float32
        )
        return (key_acc, value_acc)

    key_acc, value_acc = lax.fori_loop(0, blocks, key_advance, (empty_heads, empty_heads))
    key_grad = (join_heads(key_acc) * score_scale).astype(jnp.bfloat16)
    value_grad = join_heads(value_acc).astype(jnp.bfloat16)
    qkv_grad_low = jnp.concatenate([query_grad, key_grad, value_grad], axis=1)
    qkv_term = jnp.einsum("td,te->de", inputs, qkv_grad_low, preferred_element_type=jnp.float32)
    input_grad = branch_grad + jnp.einsum(
        "te,de->td", qkv_grad_low, qkv_back, preferred_element_type=jnp.float32
    )
    bias_term = jnp.stack(
        [
            jnp.sum(query_grad.astype(jnp.float32), axis=0),
            jnp.sum(value_grad.astype(jnp.float32), axis=0),
            jnp.sum(branch_low.astype(jnp.float32), axis=0),
            jnp.sum(second_low.astype(jnp.float32), axis=0),
        ]
    )
    hidden_term = jnp.sum(pre_low.astype(jnp.float32), axis=0)
    gain_term = jnp.stack([gain_one, gain_two])
    shift_term = jnp.stack([shift_one, shift_two])
    bias_total, hidden_total, gain_total, shift_total = lax.psum(
        (bias_term, hidden_term, gain_term, shift_term), ("rep", "fsdp")
    )
    up_sum, down_sum = (
        lax.psum_scatter(up_term, "fsdp", scatter_dimension=0, tiled=True),
        lax.psum_scatter(down_term, "fsdp", scatter_dimension=0, tiled=True),
    )
    qkv_sum, out_sum = (
        lax.psum_scatter(qkv_term, "fsdp", scatter_dimension=0, tiled=True),
        lax.psum_scatter(out_term, "fsdp", scatter_dimension=0, tiled=True),
    )
    qkv_total, out_total, up_total, down_total = lax.psum(
        (qkv_sum, out_sum, up_sum, down_sum), "rep"
    )
    grad_scale = (tok_count * lax.axis_size("fsdp") * lax.axis_size("rep")) ** (-0.5)
    return (
        output.astype(jnp.bfloat16)[None],
        input_grad.astype(jnp.bfloat16)[None],
        qkv_total * grad_scale,
        out_total * grad_scale,
        up_total * grad_scale,
        down_total * grad_scale,
        bias_total * grad_scale,
        hidden_total * grad_scale,
        gain_total * grad_scale,
        shift_total * grad_scale,
    )


def solution(mesh):
    return jax.shard_map(
        local,
        mesh=mesh,
        in_specs=(
            P("rep", "fsdp", None),
            P("rep", None),
            P("fsdp", None),
            P("fsdp", None),
            P("fsdp", None),
            P("fsdp", None),
            P(),
            P(),
            P(),
            P(),
            P("rep", "fsdp", None),
        ),
        out_specs=(
            P("rep", "fsdp", None),
            P("rep", "fsdp", None),
            P("fsdp", None),
            P("fsdp", None),
            P("fsdp", None),
            P("fsdp", None),
            P(),
            P(),
            P(),
            P(),
        ),
        check_vma=False,
    )
```

profile of v0, /device:TPU:0, one launch (start us, length us, event | category | flops | bytes accessed | tf_op | source)
XLA Modules:
  0.0 996.0 jit_solution(13008734010927375678)
XLA Ops:
  8.8 49.3 %all-gather.9.cloned.1.call-done = bf16[1024,3072]{1,0:T(8,128)(2,1)} async-done(((bf16[128,3072]{1,0:T(8,128)(2,1)}), bf16[1024,3072]{1,0:T(8,128)(2,1)}) %all-gather.9.cloned.1.call-update) | async-done | bytes 6291472 | tf_op jit(solution)/shard_map/all_gather | solution.py:26
  70.8 31.7 %all-gather.13.cloned.1.call-done = bf16[2048,1024]{1,0:T(8,128)(2,1)} async-done(((bf16[256,1024]{1,0:T(8,128)(2,1)}), bf16[2048,1024]{1,0:T(8,128)(2,1)}) %all-gather.13.cloned.1.call-update) | async-done | bytes 4194320 | tf_op jit(solution)/shard_map/all_gather | solution.py:87
  109.0 32.8 %all-gather.11.cloned.1.call-done = bf16[2048,1024]{1,0:T(8,128)(2,1)} async-done(((bf16[256,1024]{1,0:T(8,128)(2,1)}), bf16[2048,1024]{1,0:T(8,128)(2,1)}) %all-gather.11.cloned.1.call-update) | async-done | bytes 4194320 | tf_op jit(solution)/shard_map/all_gather | solution.py:86
  148.2 59.9 %while.48 = (s32[]{:T(128)}, f32[16,256,64]{1,2,0:T(8,128)}, f32[16,256]{1,0:T(8,128)S(1)}, f32[16,256]{1,0:T(8,128)S(1)}, s32[256]{0:T(256)S(1)}, /*index=5*/s3...) while((s32[]{:T(128)}, f32[16,256,64]{1,2,0:T(8,128)}, ...), condition=%wide.region_3.4_spmd.clone, body=%wide.region_0.3_spmd.clone.sunk | while | flops 1120948224 | bytes 75248888 | solution.py:113
  159.3 9.5 fusion.140
  188.9 9.2 fusion.140
  198.1 9.0 fusion.142
  212.4 15.2 %all-gather.17.cloned.1.call-done = bf16[1024,4096]{1,0:T(8,128)(2,1)} async-done(((bf16[128,4096]{1,0:T(8,128)(2,1)}), bf16[1024,4096]{1,0:T(8,128)(2,1)}) %all-gather.17.cloned.1.call-update) | async-done | bytes 8388624 | tf_op jit(solution)/shard_map/all_gather | solution.py:33
  227.6 16.2 %multiply_convert_fusion.1 = (bf16[256,4096]{1,0:T(8,128)(2,1)}, f32[256,4096]{1,0:T(8,128)}, f32[256,4096]{1,0:T(8,128)}) fusion(f32[4096]{0:T(1024)S(1)} %copy-done.39, bf16[1024,4096]{1,0:T(8,128)(2,1)} %all-gather.17.cloned.1.call-done, f32[256,1024]{1,0:T(8,128)S(1)} %get-tuple-element.818, f32[1024]{0:T(1024)S(1)} %bitcast.204, ...), kind=kOutput, calls=%fused_computation.57 | convolution fusion | flops 2218000384 | bytes 19949568 | tf_op jit(solution)/shard_map/dot_general | solution.py:123
  243.8 39.9 %all-gather.19.cloned.1.call-done = bf16[4096,1024]{1,0:T(8,128)(2,1)} async-done(((bf16[512,1024]{1,0:T(8,128)(2,1)}), bf16[4096,1024]{1,0:T(8,128)(2,1)}) %all-gather.19.cloned.1.call-update) | async-done | bytes 8388624 | tf_op jit(solution)/shard_map/all_gather | solution.py:34
  293.7 12.6 %convert_reduce_fusion = (f32[4096]{0:T(1024)}, bf16[256,4096]{1,0:T(8,128)(2,1)S(1)}) fusion(f32[256,4096]{1,0:T(8,128)} %get-tuple-element.795, f32[256,4096]{1,0:T(8,128)} %get-tuple-element.819, bf16[256,1024]{1,0:T(8,128)(2,1)S(1)} %get-tuple-element.789, bf16[4096,1024]{1,0:T(8,128)(2,1)} %all-gather.19.cloned.1.call-done), kind=kOutput, calls=%fused_computation.55 | convolution fusion | flops 2164256768 | bytes 19415040 | tf_op jit(solution)/shard_map/td,fd->tf/dot_general | solution.py:135
  316.3 9.9 fusion.67
  327.7 8.4 fusion.80
  345.1 9.6 all_gather.45
  356.1 10.0 %all_gather.43 = f32[16,2048]{1,0:T(8,128)} all-gather(f32[16,256]{1,0:T(8,128)} %log_add_fusion), channel_id=1, replica_groups=mesh['rep'=4,'fsdp'=8] {'fsdp'}, dimensions={1}, use_global_device_ids=true | all-gather | bytes 147456 | tf_op jit(solution)/shard_map/all_gather | solution.py:153
  366.1 53.6 %while.49 = (s32[]{:T(128)}, f32[16,256,64]{1,2,0:T(8,128)}, s32[256]{0:T(256)}, s32[2048]{0:T(1024)}, bf16[2048,1024]{0,1:T(8,128)(2,1)}, /*index=5*/bf16[256,1...) while((s32[]{:T(128)}, f32[16,256,64]{1,2,0:T(8,128)}, ...), condition=%wide.region_13.14_spmd.clone, body=%wide.region_12.13_spmd.clone.sunk | while | flops 1636564992 | bytes 51954912 | solution.py:181
  370.1 9.4 fusion.148
  380.4 13.0 %fusion.149 = f32[16,256,64]{1,2,0:T(8,128)} fusion(bf16[1024,16,64]{0,2,1:T(8,128)(2,1)S(1)} %bitcast.178, f32[16,1024,256]{1,2,0:T(8,128)} %fusion.148, bf16[1024,16,64]{0,2,1:T(8,128)(2,1)} %bitcast.185, f32[16,256]{1,0:T(8,128)} %get-tuple-element.1154, f32[16,256]{1,0:T(8,128)} %get-tuple-element.1151, ...), kind=kOutput, calls=%fused_computation.24.clone.1 | convolution fusion | flops 1099431936 | bytes 23887872 | tf_op jit(solution)/shard_map/while/body/eval_jaxpr/hqk,khd->hqd/dot_general | solution.py:177
  397.4 8.1 fusion.148
  406.3 13.3 %fusion.149 = f32[16,256,64]{1,2,0:T(8,128)} fusion(bf16[1024,16,64]{0,2,1:T(8,128)(2,1)S(1)} %bitcast.178, f32[16,1024,256]{1,2,0:T(8,128)} %fusion.148, bf16[1024,16,64]{0,2,1:T(8,128)(2,1)} %bitcast.185, f32[16,256]{1,0:T(8,128)} %get-tuple-element.1154, f32[16,256]{1,0:T(8,128)} %get-tuple-element.1151, ...), kind=kOutput, calls=%fused_computation.24.clone.1 | convolution fusion | flops 1099431936 | bytes 23887872 | tf_op jit(solution)/shard_map/while/body/eval_jaxpr/hqk,khd->hqd/dot_general | solution.py:177
  421.8 90.0 %while.50 = (s32[]{:T(128)}, f32[16,256,64]{1,2,0:T(8,128)}, f32[16,256,64]{1,2,0:T(8,128)}, s32[2048]{0:T(1024)}, s32[256]{0:T(256)}, /*index=5*/bf16[2048,1024...) while((s32[]{:T(128)}, f32[16,256,64]{1,2,0:T(8,128)}, ...), condition=%wide.region_15.16_spmd.clone, body=%wide.region_14.15_spmd.clone.sunk | while | flops 2190737408 | bytes 84624672 | solution.py:219
  429.7 11.4 %fusion.157 = f32[16,1024,256]{2,1,0:T(8,128)} fusion(bf16[1024,16,64]{0,2,1:T(8,128)(2,1)S(1)} %bitcast.179, bf16[256,16,64]{0,2,1:T(8,128)(2,1)S(1)} %copy-done.2), kind=kOutput, calls=%fused_computation.152.clone.1 | convolution fusion | flops 536870912 | bytes 19398656 | tf_op jit(solution)/shard_map/while/body/eval_jaxpr/qhd,khd->hqk/dot_general | solution.py:199
  446.3 9.3 fusion.159
  455.6 12.7 %fusion.158 = f32[16,256,64]{1,2,0:T(8,128)} fusion(bf16[1024,16,64]{0,2,1:T(8,128)(2,1)S(1)} %bitcast.180, f32[16,1024,256]{2,1,0:T(8,128)} %fusion.157, bf16[1024,16,64]{0,2,1:T(8,128)(2,1)} %bitcast.183, f32[16,1024]{1,0:T(8,128)S(1)} %get-tuple-element.1031, f32[16,1024]{1,0:T(8,128)S(1)} %get-tuple-element.1032, ...), kind=kOutput, calls=%fused_computation.40.clone.1 | convolution fusion | flops 1099431936 | bytes 23986176 | tf_op jit(solution)/shard_map/while/body/eval_jaxpr/hqk,qhd->hkd/dot_general | solution.py:214
  476.0 8.5 fusion.157
  489.5 9.9 fusion.159
  499.5 12.3 %fusion.158 = f32[16,256,64]{1,2,0:T(8,128)} fusion(bf16[1024,16,64]{0,2,1:T(8,128)(2,1)S(1)} %bitcast.180, f32[16,1024,256]{2,1,0:T(8,128)} %fusion.157, bf16[1024,16,64]{0,2,1:T(8,128)(2,1)} %bitcast.183, f32[16,1024]{1,0:T(8,128)S(1)} %get-tuple-element.1031, f32[16,1024]{1,0:T(8,128)S(1)} %get-tuple-element.1032, ...), kind=kOutput, calls=%fused_computation.40.clone.1 | convolution fusion | flops 1099431936 | bytes 23986176 | tf_op jit(solution)/shard_map/while/body/eval_jaxpr/hqk,qhd->hkd/dot_general | solution.py:214
  521.9 14.2 %reduce-scatter.9.cloned.1.call-done = f32[128,4096]{1,0:T(8,128)} async-done(((f32[1024,4096]{1,0:T(8,128)}), f32[128,4096]{1,0:T(8,128)}) %reduce-scatter.9.cloned.1.call-update) | async-done | bytes 2097168 | tf_op jit(solution)/shard_map/reduce_scatter | solution.py:242
  536.2 120.0 %reduce-scatter.11.cloned.1.call-done = f32[512,1024]{1,0:T(8,128)} async-done(((f32[4096,1024]{1,0:T(8,128)}), f32[512,1024]{1,0:T(8,128)}) %reduce-scatter.11.cloned.1.call-update) | async-done | bytes 2097168 | tf_op jit(solution)/shard_map/reduce_scatter | solution.py:243
  656.1 96.2 %reduce-scatter.5.cloned.1.call-done = f32[128,3072]{0,1:T(8,128)} async-done(((f32[1024,3072]{0,1:T(8,128)}), f32[128,3072]{0,1:T(8,128)}) %reduce-scatter.5.cloned.1.call-update) | async-done | bytes 1572880 | tf_op jit(solution)/shard_map/reduce_scatter | solution.py:246
  752.7 48.6 %all-reduce = (f32[4,1024]{1,0:T(4,128)S(1)}, f32[4096]{0:T(1024)S(1)}, f32[2,1024]{1,0:T(2,128)S(1)}, f32[2,1024]{1,0:T(2,128)S(1)}) all-reduce(f32[4,1024]{1,0:T(4,128)S(1)} %pad_maximum_fusion.3, f32[4096]{0:T(1024)S(1)} %copy-done.32, f32[2,1024]{1,0:T(2,128)S(1)} %get-tuple-element.824, ...), channel_id=1, replica_groups=mesh['rep'=4,'fsdp'=8] {'rep','fsdp'}, use_global_device_ids=true, to_apply=%region_28.29 | all-reduce | flops 12288 | bytes 98304 | tf_op jit(solution)/shard_map/psum | solution.py:238
  809.2 170.8 %all-reduce.4.cloned.1.call-done = (f32[128,3072]{0,1:T(8,128)}, f32[128,1024]{1,0:T(8,128)}, f32[128,4096]{1,0:T(8,128)}, f32[512,1024]{1,0:T(8,128)}) async-done(((f32[128,3072]{0,1:T(8,128)}, f32[128,1024]{1,0:T(8,128)}, f32[128,4096]{1,0:T(8,128)}, f32[512,1024]{1,0:T(8,128)}), (f32[128,3072]{0,1:T(8,128)}, f32[128,1024]{1,0:T(8,128)}, f32[128,4096]{1,0:T(8,128)}, ...) | async-done | bytes 6291472 | tf_op jit(solution)/shard_map/psum | solution.py:249
  (223 shorter events, 159.8 us)
Async XLA Ops:
  7.2 51.0 %all-gather.9.cloned.1.call-start = ((), (), s32[]{:S(2)}) async-start(), calls=%async_computation.4 | async-start | bytes 7077888 | tf_op jit(solution)/shard_map/all_gather | solution.py:26
  7.9 94.6 %all-gather.13.cloned.1.call-start = ((), (), s32[]{:S(2)}) async-start(), calls=%async_computation.6 | async-start | bytes 4718592 | tf_op jit(solution)/shard_map/all_gather | solution.py:87
  65.7 76.1 %all-gather.11.cloned.1.call-start = ((), (), s32[]{:S(2)}) async-start(), calls=%async_computation.5 | async-start | bytes 4718592 | tf_op jit(solution)/shard_map/all_gather | solution.py:86
  68.0 141.7 %all-gather.15.cloned.1.call-start = ((), (), s32[]{:S(2)}) async-start(), calls=%async_computation.7 | async-start | bytes 2359296 | tf_op jit(solution)/shard_map/all_gather | solution.py:27
  68.5 159.0 %all-gather.17.cloned.1.call-start = ((), (), s32[]{:S(2)}) async-start(), calls=%async_computation.8 | async-start | bytes 9437184 | tf_op jit(solution)/shard_map/all_gather | solution.py:33
  69.1 214.6 %all-gather.19.cloned.1.call-start = ((), (), s32[]{:S(2)}) async-start(), calls=%async_computation.9 | async-start | bytes 9437184 | tf_op jit(solution)/shard_map/all_gather | solution.py:34
  69.7 352.1 %all-gather.21.cloned.1.call-start = ((), (), s32[]{:S(2)}) async-start(), calls=%async_computation.10 | async-start | bytes 4718592 | tf_op jit(solution)/shard_map/all_gather | solution.py:186
  70.8 351.0 %all-gather.23.cloned.1.call-start = ((), (), s32[]{:S(2)}) async-start(), calls=%async_computation.11 | async-start | bytes 4718592 | tf_op jit(solution)/shard_map/all_gather | solution.py:187
  148.2 61.5 %copy-start.15 = (bf16[1,256,1024]{2,1,0:T(8,128)(2,1)S(1)}, bf16[1,256,1024]{2,1,0:T(8,128)(2,1)}, u32[]{:S(2)}) copy-start(bf16[1,256,1024]{2,1,0:T(8,128)(2,1)} %param.17) | copy-start | bytes 1572868
  208.1 35.7 %copy-start = (bf16[256,16,64]{0,2,1:T(8,128)(2,1)}, bf16[256,16,64]{0,2,1:T(8,128)(2,1)S(1)}, u32[]{:S(2)}) copy-start(bf16[256,16,64]{0,2,1:T(8,128)(2,1)S(1)} %get-tuple-element.1191) | copy-start | bytes 1572868
  208.1 35.7 %copy-start.26 = (s32[256]{0:T(256)}, s32[256]{0:T(256)S(1)}, u32[]{:S(2)}) copy-start(s32[256]{0:T(256)S(1)} %get-tuple-element.1223) | copy-start | bytes 3076
  208.1 136.2 %copy-start.24 = (f32[16,256]{1,0:T(8,128)}, f32[16,256]{1,0:T(8,128)S(1)}, u32[]{:S(2)}) copy-start(f32[16,256]{1,0:T(8,128)S(1)} %get-tuple-element.521) | copy-start | bytes 49156
  208.1 19.5 %copy-start.39 = (f32[4096]{0:T(1024)S(1)}, f32[4096]{0:T(1024)}, u32[]{:S(2)}) copy-start(f32[4096]{0:T(1024)} %param.24) | copy-start | bytes 49156
  291.6 14.7 %slice-start = ((s8[8388608]{0:T(1024)(128)(4,1)}), s8[4194304]{0:T(1024)(128)(4,1)S(1)}, s32[]{:S(2)}) async-start(s8[8388608]{0:T(1024)(128)(4,1)} %bitcast.220), calls=%async_computation.17 | async-start | bytes 8388608
  293.7 12.6 %slice-start.1 = ((s8[8388608]{0:T(1024)(128)(4,1)}), s8[4194304]{0:T(1024)(128)(4,1)S(1)}, s32[]{:S(2)}) async-start(s8[8388608]{0:T(1024)(128)(4,1)} %bitcast.220), calls=%async_computation.18 | async-start | bytes 8388608
  313.4 208.6 %reduce-scatter.7.cloned.1.call-start = ((), (), s32[]{:S(2)}) async-start(), calls=%async_computation.13 | async-start | bytes 4718592 | tf_op jit(solution)/shard_map/reduce_scatter | solution.py:247
  316.2 219.9 %reduce-scatter.9.cloned.1.call-start = ((), (), s32[]{:S(2)}) async-start(), calls=%async_computation.14 | async-start | bytes 18874368 | tf_op jit(solution)/shard_map/reduce_scatter | solution.py:242
  326.1 330.0 %reduce-scatter.11.cloned.1.call-start = ((), (), s32[]{:S(2)}) async-start(), calls=%async_computation.15 | async-start | bytes 18874368 | tf_op jit(solution)/shard_map/reduce_scatter | solution.py:243
  336.1 416.2 %reduce-scatter.5.cloned.1.call-start = ((), (), s32[]{:S(2)}) async-start(), calls=%async_computation.12 | async-start | bytes 14155776 | tf_op jit(solution)/shard_map/reduce_scatter | solution.py:246
  421.8 92.6 %copy-start.16 = (bf16[1,256,1024]{2,1,0:T(8,128)(2,1)S(1)}, bf16[1,256,1024]{2,1,0:T(8,128)(2,1)}, u32[]{:S(2)}) copy-start(bf16[1,256,1024]{2,1,0:T(8,128)(2,1)} %param.17) | copy-start | bytes 1572868
  521.8 230.6 %copy-start.5 = (bf16[1,256,1024]{2,1,0:T(8,128)(2,1)S(1)}, bf16[1,256,1024]{2,1,0:T(8,128)(2,1)}, u32[]{:S(2)}) copy-start(bf16[1,256,1024]{2,1,0:T(8,128)(2,1)} %param.27) | copy-start | bytes 1572868
  521.8 230.8 %copy-start.29 = (f32[1024]{0:T(1024)S(1)}, f32[1024]{0:T(1024)}, u32[]{:S(2)}) copy-start(f32[1024]{0:T(1024)} %get-tuple-element.707) | copy-start | bytes 12292
  521.8 230.7 %copy-start.35 = (f32[1024]{0:T(1024)S(1)}, f32[1024]{0:T(1024)}, u32[]{:S(2)}) copy-start(f32[1024]{0:T(1024)} %get-tuple-element.705) | copy-start | bytes 12292
  521.8 230.7 %copy-start.36 = (f32[1024]{0:T(1024)S(1)}, f32[1024]{0:T(1024)}, u32[]{:S(2)}) copy-start(f32[1024]{0:T(1024)} %get-tuple-element.709) | copy-start | bytes 12292
  521.8 230.8 %copy-start.30 = (f32[1024]{0:T(1024)S(1)}, f32[1024]{0:T(1024)}, u32[]{:S(2)}) copy-start(f32[1024]{0:T(1024)} %get-tuple-element.788) | copy-start | bytes 12292
  521.8 230.8 %copy-start.31 = (f32[1024]{0:T(1024)S(1)}, f32[1024]{0:T(1024)}, u32[]{:S(2)}) copy-start(f32[1024]{0:T(1024)} %get-tuple-element.786) | copy-start | bytes 12292
  521.8 230.8 %copy-start.32 = (f32[4096]{0:T(1024)S(1)}, f32[4096]{0:T(1024)}, u32[]{:S(2)}) copy-start(f32[4096]{0:T(1024)} %get-tuple-element.780) | copy-start | bytes 49156
  521.8 281.8 %copy-start.9 = (f32[256,1024]{1,0:T(8,128)S(1)}, f32[256,1024]{1,0:T(8,128)}, u32[]{:S(2)}) copy-start(f32[256,1024]{1,0:T(8,128)} %copy-done.8) | copy-start | bytes 3145732
  521.8 281.8 %copy-start.17 = (bf16[16,256,64]{1,2,0:T(8,128)(2,1)S(1)}, bf16[16,256,64]{1,2,0:T(8,128)(2,1)}, u32[]{:S(2)}) copy-start(bf16[16,256,64]{1,2,0:T(8,128)(2,1)} %get-tuple-element.783) | copy-start | bytes 1572868
  521.9 281.8 %copy-start.21 = (bf16[16,256,64]{1,2,0:T(8,128)(2,1)S(1)}, bf16[16,256,64]{1,2,0:T(8,128)(2,1)}, u32[]{:S(2)}) copy-start(bf16[16,256,64]{1,2,0:T(8,128)(2,1)} %copy-done.20) | copy-start | bytes 1572868
  521.9 281.8 %copy-start.38 = (f32[256]{0:T(256)S(1)}, f32[256]{0:T(256)}, u32[]{:S(2)}) copy-start(f32[256]{0:T(256)} %copy-done.37) | copy-start | bytes 3076
  521.9 458.2 %all-reduce.4.cloned.1.call-start = ((), (), s32[]{:S(2)}) async-start(), calls=%async_computation.16 | async-start | bytes 12582912 | tf_op jit(solution)/shard_map/psum | solution.py:249
  (29 other events, 127.0 us)
Sparse Core Ops, SparseCore 0:
  9.9 48.2 all-gather.8
  65.8 36.7 all-gather.12
  105.0 36.7 all-gather.10
  143.5 27.8 all-gather.14
  173.2 54.3 all-gather.16
  229.3 54.3 all-gather.18
  285.6 36.7 all-gather.20
  324.3 37.2 all-gather.22
  364.9 51.3 reduce-scatter.6
  420.2 115.9 reduce-scatter.8
  540.1 115.9 reduce-scatter.10
  659.9 92.3 reduce-scatter.4
  755.1 224.8 all-reduce.3
where the time goes:
time: 1010 us; the launch traced here: 996 us
  waiting for transfers between devices  573 us (57%)
  matrix products  220 us (22%)
  local copies, waits for them, and re-layouts  75.5 us (7%)
  blocking collectives  68.2 us (7%)
  other arithmetic  43.3 us (4%)
  between operations  14.8 us (1%)
    psum x1, waiting for transfers between devices, local(): lax.psum((qkv_sum, out_sum, up_sum, down_sum), 'rep')  171 us
    reduce_scatter x1, waiting for transfers between devices, local(): lax.psum_scatter(down_term, 'fsdp', scatter_dimension=0, tiled=True)  120 us
    reduce_scatter x1, waiting for transfers between devices, local(): lax.psum_scatter(qkv_term, 'fsdp', scatter_dimension=0, tiled=True)  96.2 us
    all_gather x1, waiting for transfers between devices, gather_attention(): lax.all_gather(qkv_weight, 'fsdp', axis=0, tiled=True)  49.3 us
    psum x1, blocking collectives, local(): lax.psum((bias_term, hidden_term, gain_term, shift_term), ('rep', 'fsdp'))  48.6 us
    all_gather x1, waiting for transfers between devices, gather_feedforward(): lax.all_gather(down_weight, 'fsdp', axis=0, tiled=True)  39.9 us
    all_gather x1, waiting for transfers between devices, local(): key_piece = lax.all_gather(key_rows, 'fsdp', axis=0, tiled=True)  32.8 us
    all_gather x1, waiting for transfers between devices, local(): value_piece = lax.all_gather(value_rows, 'fsdp', axis=0, tiled=True)  31.7 us
  transfers between devices with their start and end apart: 13, of which 9 were waited for; matrix products, arithmetic and copies ran while one was open for 32% of the time, Pallas kernels for 0%

commit v1 on v0

--- a/solution.py
+++ b/solution.py
@@ -1,14 +1,181 @@
+import functools
 import math
 
 import jax
 import jax.numpy as jnp
 from jax import lax
+from jax.experimental import pallas as pl
+from jax.experimental.pallas import tpu as pltpu
 from jax.sharding import PartitionSpec as P
 
 HEADS = 16
 
-
 NEGATIVE = -1e30
+BQ = 256
+VM = pl.BlockSpec(memory_space=pltpu.VMEM)
+SM = pl.BlockSpec(memory_space=pltpu.SMEM)
+
+
+def nt(a, b):
+    return lax.dot_general(a, b, (((1,), (1,)), ((), ())), preferred_element_type=jnp.float32)
+
+
+def nn(a, b):
+    return jnp.dot(a, b, preferred_element_type=jnp.float32)
+
+
+def block_range(seg_s, blk, i, n):
+    first = seg_s[0, i * blk]
+    last = seg_s[0, i * blk + blk - 1]
+    lo = jnp.int32(0)
+    hi = jnp.int32(0)
+    for j in range(n):
+        lo = lo + (seg_s[0, j * blk + blk - 1] < first).astype(jnp.int32)
+        hi = hi + (seg_s[0, j * blk] <= last).astype(jnp.int32)
+    return lo, hi
+
+
+def head_lanes(shape, half):
+    return lax.broadcasted_iota(jnp.int32, shape, 1) < half
+
+
+def attn_fwd_body(scale, seg_s, seg_v, q_ref, k_ref, v_ref, o_ref, a_ref, lse_ref):
+    length, width = q_ref.shape
+    half = width // 2
+    n = length // BQ
+    first = head_lanes((BQ, width), half)
+
+    @pl.loop(0, n)
+    def _(i):
+        lo, hi = block_range(seg_s, BQ, i, n)
+        rows = pl.ds(pl.multiple_of(i * BQ, BQ), BQ)
+        q = q_ref[rows, :] * jnp.bfloat16(scale)
+        zero = jnp.zeros_like(q)
+        qs = (jnp.where(first, q, zero), jnp.where(first, zero, q))
+        seg_row = seg_v[:, rows].astype(jnp.float32)
+        seg_col = jnp.transpose(jnp.broadcast_to(seg_row, (128, BQ)))
+        seg_col = jnp.concatenate([seg_col] * (BQ // 128), axis=1)
+
+        def step(j, state):
+            cols = pl.ds(pl.multiple_of(j * BQ, BQ), BQ)
+            kb = k_ref[cols, :]
+            vb = v_ref[cols, :]
+            same = seg_col == seg_v[:, cols].astype(jnp.float32)
+            out = []
+            for h in range(2):
+                m, l, acc = state[h]
+                s = jnp.where(same, nt(qs[h], kb), NEGATIVE)
+                top = jnp.maximum(m, jnp.max(s, axis=1, keepdims=True))
+                p = jnp.exp(s - top)
+                factor = jnp.exp(m - top)
+                l = l * factor + jnp.sum(p, axis=1, keepdims=True)
+                acc = acc * factor + nn(p.astype(jnp.bfloat16), vb)
+                out.append((top, l, acc))
+            return tuple(out)
+
+        one = (jnp.full((BQ, 1), NEGATIVE, jnp.float32), jnp.zeros((BQ, 1), jnp.float32), jnp.zeros((BQ, width), jnp.float32))
+        (m0, l0, acc0), (m1, l1, acc1) = lax.fori_loop(lo, hi, step, (one, one))
+        o = jnp.where(first, acc0 / l0, acc1 / l1)
+        o_ref[rows, :] = o
+        a_ref[rows, :] = o.astype(jnp.bfloat16)
+        lse_ref[0:1, rows] = jnp.transpose(jnp.broadcast_to(m0 + jnp.log(l0), (BQ, 128)))[0:1, :]
+        lse_ref[1:2, rows] = jnp.transpose(jnp.broadcast_to(m1 + jnp.log(l1), (BQ, 128)))[0:1, :]
+
+
+def attn_fwd(scale, seg, q, k, v):
+    length, width = q.shape
+    return pl.pallas_call(
+        functools.partial(attn_fwd_body, scale),
+        name="attn_fwd",
+        out_shape=(
+            jax.ShapeDtypeStruct((length, width), jnp.float32),
+            jax.ShapeDtypeStruct((length, width), jnp.bfloat16),
+            jax.ShapeDtypeStruct((8, length), jnp.float32),
+        ),
+        in_specs=[SM, VM, VM, VM, VM],
+        out_specs=(VM, VM, VM),
+        compiler_params=pltpu.CompilerParams(vmem_limit_bytes=32 << 20),
+        cost_estimate=pl.CostEstimate(flops=4 * length * length * width, bytes_accessed=6 * length * width, transcendentals=2 * length * length),
+    )(seg, seg, q, k, v)
+
+
+def attn_bwd_body(scale, seg_s, seg_v, q_ref, k_ref, v_ref, g_ref, o_ref, lse_ref, dq_ref, dk_ref, dv_ref, corr, dqt, dk_acc, dv_acc):
+    length, width = q_ref.shape
+    half = width // 2
+    n = length // BQ
+    first = head_lanes((BQ, width), half)
+
+    @pl.loop(0, n)
+    def _(i):
+        rows = pl.ds(pl.multiple_of(i * BQ, BQ), BQ)
+        prod = jnp.transpose(g_ref[rows, :].astype(jnp.float32) * o_ref[rows, :])
+        corr[0:1, rows] = jnp.sum(prod[:half], axis=0, keepdims=True)
+        corr[1:2, rows] = jnp.sum(prod[half:], axis=0, keepdims=True)
+        dqt[:, rows] = jnp.zeros((width, BQ), jnp.float32)
+
+    @pl.loop(0, n)
+    def _(j):
+        lo, hi = block_range(seg_s, BQ, j, n)
+        rows = pl.ds(pl.multiple_of(j * BQ, BQ), BQ)
+        kb = k_ref[rows, :]
+        vb = v_ref[rows, :]
+        zero = jnp.zeros_like(kb)
+        ks = (jnp.where(first, kb, zero), jnp.where(first, zero, kb))
+        vs = (jnp.where(first, vb, zero), jnp.where(first, zero, vb))
+        kt = jnp.transpose(kb)
+        seg_row = seg_v[:, rows].astype(jnp.float32)
+        seg_col = jnp.transpose(jnp.broadcast_to(seg_row, (128, BQ)))
+        seg_col = jnp.concatenate([seg_col] * (BQ // 128), axis=1)
+        dk_acc[...] = jnp.zeros_like(dk_acc)
+        dv_acc[...] = jnp.zeros_like(dv_acc)
+
+        def step(i, _):
+            cols = pl.ds(pl.multiple_of(i * BQ, BQ), BQ)
+            qb = q_ref[cols, :] * jnp.bfloat16(scale)
+            gb = g_ref[cols, :]
+            same = seg_col == seg_v[:, cols].astype(jnp.float32)
+            ps, ds = [], []
+            for h in range(2):
+                s = jnp.where(same, nt(ks[h], qb), NEGATIVE)
+                p = jnp.exp(s - lse_ref[h : h + 1, cols])
+                dp = nt(vs[h], gb)
+                d = (p * (dp - corr[h : h + 1, cols])).astype(jnp.bfloat16)
+                ps.append(p.astype(jnp.bfloat16))
+                ds.append(d)
+                dqt[h * half : (h + 1) * half, cols] += nn(kt[h * half : (h + 1) * half, :], d)
+            gz = jnp.concatenate([jnp.where(first, gb, zero), jnp.where(first, zero, gb)], axis=0)
+            qz = jnp.concatenate([jnp.where(first, qb, zero), jnp.where(first, zero, qb)], axis=0)
+            dv_acc[...] += nn(jnp.concatenate(ps, axis=1), gz)
+            dk_acc[...] += nn(jnp.concatenate(ds, axis=1), qz)
+            return 0
+
+        lax.fori_loop(lo, hi, step, 0)
+        dk_ref[rows, :] = dk_acc[...].astype(jnp.bfloat16)
+        dv_ref[rows, :] = dv_acc[...].astype(jnp.bfloat16)
+
+    @pl.loop(0, n)
+    def _(i):
+        rows = pl.ds(pl.multiple_of(i * BQ, BQ), BQ)
+        dq_ref[rows, :] = (jnp.transpose(dqt[:, rows]) * scale).astype(jnp.bfloat16)
+
+
+def attn_bwd(scale, seg, q, k, v, g, o, lse):
+    length, width = q.shape
+    return pl.pallas_call(
+        functools.partial(attn_bwd_body, scale),
+        name="attn_bwd",
+        out_shape=tuple(jax.ShapeDtypeStruct((length, width), jnp.bfloat16) for _ in range(3)),
+        in_specs=[SM, VM, VM, VM, VM, VM, VM, VM],
+        out_specs=(VM, VM, VM),
+        scratch_shapes=[
+            pltpu.VMEM((8, length), jnp.float32),
+            pltpu.VMEM((width, length), jnp.float32),
+            pltpu.VMEM((BQ, width), jnp.float32),
+            pltpu.VMEM((BQ, width), jnp.float32),
+        ],
+        compiler_params=pltpu.CompilerParams(vmem_limit_bytes=32 << 20),
+        cost_estimate=pl.CostEstimate(flops=10 * length * length * width, bytes_accessed=14 * length * width, transcendentals=2 * length * length),
+    )(seg, seg, q, k, v, g, o, lse)
 
 
 def normalize(hidden, gain, shift):
@@ -50,7 +217,7 @@
     )
 
 
-def local(
+def local_gather(
     tokens,
     segment_ids,
     qkv_weight,
@@ -264,7 +431,105 @@
     )
 
 
+def exchange(rows, parts):
+    count, width = rows.shape
+    split = jnp.transpose(rows.reshape(count, parts, width // parts), (1, 0, 2))
+    return lax.all_to_all(split, "fsdp", 0, 0).reshape(parts * count, width // parts)
+
+
+def exchange_back(rows, parts):
+    count, width = rows.shape
+    got = lax.all_to_all(rows.reshape(parts, count // parts, width), "fsdp", 0, 0)
+    return jnp.transpose(got, (1, 0, 2)).reshape(count // parts, parts * width)
+
+
+def local_tensor(tokens, segment_ids, qkv_weight, out_weight, up_weight, down_weight, proj_bias, hidden_bias, norm_gain, norm_shift, cotangent):
+    f32, bf16 = jnp.float32, jnp.bfloat16
+    inputs = tokens[0]
+    tok_count, model_width = inputs.shape
+    parts = lax.axis_size("fsdp")
+    own = lax.axis_index("fsdp")
+    head_dim = model_width // HEADS
+    scale = head_dim ** (-0.5)
+    width = model_width // parts
+    ff = hidden_bias.shape[0] // parts
+
+    def dot(spec, a, b):
+        return jnp.einsum(spec, a, b, preferred_element_type=f32)
+
+    def mine(vector, size):
+        return lax.dynamic_slice_in_dim(vector, own * size, size)
+
+    tokens_all = lax.all_gather(inputs, "fsdp", axis=0, tiled=True)
+    weight_pieces = [exchange(qkv_weight[:, i * model_width : (i + 1) * model_width], parts) for i in range(3)]
+    queries = (dot("td,de->te", tokens_all, weight_pieces[0]) + mine(proj_bias[0], width)).astype(bf16)
+    key_rows = dot("td,de->te", tokens_all, weight_pieces[1]).astype(bf16)
+    value_rows = (dot("td,de->te", tokens_all, weight_pieces[2]) + mine(proj_bias[1], width)).astype(bf16)
+    attended, attended_low_heads, lse = attn_fwd(scale, segment_ids, queries, key_rows, value_rows)
+    attended_low = exchange_back(attended_low_heads, parts)
+    out_full = lax.all_gather(out_weight, "fsdp", axis=0, tiled=True)
+    branch = dot("te,ed->td", attended_low, out_full) + proj_bias[2]
+    first_norm, norm_one_back = jax.vjp(normalize, inputs.astype(f32) + branch, norm_gain[0], norm_shift[0])
+    first_low = first_norm.astype(bf16)
+    up_mine = exchange(up_weight, parts)
+    first_all = lax.all_gather(first_low, "fsdp", axis=0, tiled=True)
+    hidden_pre = dot("td,df->tf", first_all, up_mine) + mine(hidden_bias, ff)
+    activated, gelu_back = jax.vjp(exact_gelu, hidden_pre)
+    activated_low = activated.astype(bf16)
+    second = lax.psum_scatter(dot("tf,fd->td", activated_low, down_weight).astype(bf16), "fsdp", scatter_dimension=0, tiled=True).astype(f32) + proj_bias[3]
+    output, norm_two_back = jax.vjp(normalize, first_norm + second, norm_gain[1], norm_shift[1])
+    grad_second, gain_two, shift_two = norm_two_back(cotangent[0].astype(f32))
+    second_low = grad_second.astype(bf16)
+    second_all = lax.all_gather(second_low, "fsdp", axis=0, tiled=True)
+    (pre_grad,) = gelu_back(dot("td,fd->tf", second_all, down_weight))
+    pre_low = pre_grad.astype(bf16)
+    down_sum = dot("tf,td->fd", activated_low, second_all)
+    first_grad = grad_second + lax.psum_scatter(dot("tf,df->td", pre_low, up_mine).astype(bf16), "fsdp", scatter_dimension=0, tiled=True).astype(f32)
+    up_cols = dot("td,tf->df", first_all, pre_low)
+    up_sum = exchange_back(up_cols.astype(bf16), parts)
+    branch_grad, gain_one, shift_one = norm_one_back(first_grad)
+    branch_low = branch_grad.astype(bf16)
+    attended_grad = dot("td,ed->te", branch_low, out_full).astype(bf16)
+    grad_heads = exchange(attended_grad, parts)
+    out_term = dot("te,td->ed", attended_low, branch_low)
+    out_sum = lax.psum_scatter(out_term.astype(bf16), "fsdp", scatter_dimension=0, tiled=True)
+    up_total, down_total, out_total = lax.psum((up_sum, down_sum.astype(bf16), out_sum), "rep")
+    query_grad, key_grad, value_grad = attn_bwd(scale, segment_ids, queries, key_rows, value_rows, grad_heads, attended, lse)
+    partial_input = dot("te,de->td", query_grad, weight_pieces[0]) + dot("te,de->td", key_grad, weight_pieces[1]) + dot("te,de->td", value_grad, weight_pieces[2])
+    input_grad = branch_grad + lax.psum_scatter(partial_input.astype(bf16), "fsdp", scatter_dimension=0, tiled=True).astype(f32)
+    qkv_sum = jnp.concatenate([exchange_back(dot("td,te->de", tokens_all, g).astype(bf16), parts) for g in (query_grad, key_grad, value_grad)], axis=1)
+    qkv_total = lax.psum(qkv_sum, "rep")
+
+    def placed(vector):
+        return lax.dynamic_update_slice_in_dim(jnp.zeros((vector.shape[0] * parts,), f32), vector, own * vector.shape[0], 0)
+
+    bias_term = jnp.stack([
+        placed(jnp.sum(query_grad.astype(f32), axis=0)),
+        placed(jnp.sum(value_grad.astype(f32), axis=0)),
+        jnp.sum(branch_low.astype(f32), axis=0),
+        jnp.sum(second_low.astype(f32), axis=0),
+    ])
+    hidden_term = placed(jnp.sum(pre_low.astype(f32), axis=0))
+    bias_total, hidden_total, gain_total, shift_total = lax.psum(
+        (bias_term, hidden_term, jnp.stack([gain_one, gain_two]), jnp.stack([shift_one, shift_two])), ("rep", "fsdp")
+    )
+    grad_scale = (tok_count * parts * lax.axis_size("rep")) ** (-0.5)
+    return (
+        output.astype(bf16)[None],
+        input_grad.astype(bf16)[None],
+        qkv_total.astype(f32) * grad_scale,
+        out_total.astype(f32) * grad_scale,
+        up_total.astype(f32) * grad_scale,
+        down_total.astype(f32) * grad_scale,
+        bias_total * grad_scale,
+        hidden_total * grad_scale,
+        gain_total * grad_scale,
+        shift_total * grad_scale,
+    )
+
+
 def solution(mesh):
+    local = local_tensor if HEADS == 2 * mesh.shape["fsdp"] else local_gather
     return jax.shard_map(
         local,
         mesh=mesh,

time: 1010 us -> 637 us (0.63)
  waiting for transfers between devices: 573 us -> 348 us
  matrix products: 220 us -> 68.4 us
  Pallas kernels: 0 us -> 55.5 us
  local copies, waits for them, and re-layouts: 75.5 us -> 26.8 us
  starting transfers between devices: 0.7 us -> 39.4 us
  other arithmetic: 43.3 us -> 24.2 us
  blocking collectives: 68.2 us -> 52.4 us
    dot_general x26 -> x18, matrix products: 220 us -> 68.4 us  [dot(): return jnp.einsum(spec, a, b, preferred_element_type=f32)]
    psum x1, waiting for transfers between devices: 171 us -> 69.3 us  [local_tensor(): qkv_total = lax.psum(qkv_sum, 'rep')]
    all_gather x8 -> x4, waiting for transfers between devices: 169 us -> 68.5 us  [the longest x1 36.6 us: local_tensor(): second_all = lax.all_gather(second_low, 'fsdp', axis=0, tiled=True)]
    reduce_scatter x4, waiting for transfers between devices: 230 us -> 149 us  [the longest x1 51.5 us: local_tensor(): lax.psum_scatter(dot('tf,df->td', pre_low, up_mine).astype(bf16), 'fsdp',...]
    all_to_all x0 -> x10, waiting for transfers between devices: none -> 58.9 us  [the longest x5 43 us: exchange(): lax.all_to_all(split, 'fsdp', 0, 0).reshape(parts * count, width // parts)]
    pallas_call x0 -> x2, Pallas kernels: none -> 55.5 us  [the longest x1 28 us: attn_fwd(): pl.pallas_call(functools.partial(attn_fwd_body, scale), name='attn_fwd',...]
    dynamic_slice x19 -> x1, local copies, waits for them, and re-layouts: 42.6 us -> 0.76 us  [mine(): return lax.dynamic_slice_in_dim(vector, own * size, size)]
    all_to_all x0 -> x10, starting transfers between devices: none -> 38.7 us  [the longest x5 19.7 us: exchange(): lax.all_to_all(split, 'fsdp', 0, 0).reshape(parts * count, width // parts)]
  transfers between devices with their start and end apart: 13 -> 19, of which waited for: 9 -> 15; matrix products, arithmetic and copies ran while one was open for 32% -> 9% of each run, Pallas kernels for 0% -> 9%
where the time goes in v1:
time: 637 us; the launch traced here: 630 us
  waiting for transfers between devices  348 us (55%)
  matrix products  68.4 us (11%)
  Pallas kernels  55.5 us (9%)
  blocking collectives  52.4 us (8%)
  starting transfers between devices  39.4 us (6%)
  local copies, waits for them, and re-layouts  26.8 us (4%)
  other arithmetic  24.2 us (4%)
  between operations  14.8 us (2%)
    psum x1, waiting for transfers between devices, local_tensor(): qkv_total = lax.psum(qkv_sum, 'rep')  69.3 us
    dot_general x18, matrix products, dot(): return jnp.einsum(spec, a, b, preferred_element_type=f32)  68.4 us
    psum x1, blocking collectives, local_tensor(): lax.psum((bias_term, hidden_term, jnp.stack([gain_one, gain_two]), jnp.st...  52.4 us
    reduce_scatter x1, waiting for transfers between devices, local_tensor(): lax.psum_scatter(dot('tf,df->td', pre_low, up_mine).astype(bf16), 'fsdp',...  51.5 us
    reduce_scatter x1, waiting for transfers between devices, local_tensor(): lax.psum_scatter(dot('tf,fd->td', activated_low, down_weight).astype(bf16...  51.5 us
    reduce_scatter x1, waiting for transfers between devices, local_tensor(): lax.psum_scatter(partial_input.astype(bf16), 'fsdp', scatter_dimension=0,...  46.2 us
    all_to_all x5, waiting for transfers between devices, exchange(): lax.all_to_all(split, 'fsdp', 0, 0).reshape(parts * count, width // parts)  43 us
    all_gather x1, waiting for transfers between devices, local_tensor(): second_all = lax.all_gather(second_low, 'fsdp', axis=0, tiled=True)  36.6 us
  transfers between devices with their start and end apart: 19, of which 15 were waited for; matrix products, arithmetic and copies ran while one was open for 9% of the time, Pallas kernels for 9%

profile of v1, /device:TPU:0, one launch (start us, length us, event | category | flops | bytes accessed | tf_op | source)
XLA Modules:
  0.0 629.6 jit_solution(3228046476116633254)
XLA Ops:
  10.7 5.2 all-to-all-start.2
  16.7 6.1 all-to-all-done.2
  22.8 3.4 all-to-all-start
  27.1 6.0 all-to-all-done
  33.1 3.4 all-to-all-start.1
  36.9 9.6 %all-to-all-done.1 = bf16[8,128,128]{1,2,0:T(8,128)(2,1)S(1)} async-done(((bf16[8,128,128]{1,2,0:T(8,128)(2,1)}), bf16[8,128,128]{1,2,0:T(8,128)(2,1)S(1)}, u32[]{:S(2)}, u32[]{:S(2)}) %all-to-all-start.1) | async-done | bytes 262176 | tf_op jit(solution)/shard_map/all_to_all | solution.py:437
  46.7 5.5 all-gather.12.cloned.1.call-done
  52.2 3.6 fusion.30.k_ref
  58.4 28.0 %attn_fwd.1 = (f32[2048,128]{1,0:T(8,128)S(1)}, bf16[2048,128]{1,0:T(8,128)(2,1)S(1)}, f32[8,2048]{1,0:T(8,128)S(1)}) custom-call(s32[1,2048]{1,0:T(1,128)S(1)} %copy-done.2, s32[1,2048]{1,0:T(1,128)S(1)} %copy-done.2, bf16[2048,128]{1,0:T(8,128)(2,1)S(1)} %fusion.27.q_ref, bf16[2048,128]{1,0:T(8,128)(2,1)S(1)} %fusion.30.k_ref, ...), custom_call_target="tpu_custom_call" | custom-call | flops 2147483648 | bytes 1572864 | tf_op jit(solution)/shard_map/attn_fwd/pallas_call | solution.py:87
  88.5 3.5 all-to-all-start.3
  92.1 9.5 %all-to-all-done.3 = bf16[8,256,128]{1,2,0:T(8,128)(2,1)S(1)} async-done(((bf16[8,256,128]{1,2,0:T(8,128)(2,1)}), bf16[8,256,128]{1,2,0:T(8,128)(2,1)S(1)}, u32[]{:S(2)}, u32[]{:S(2)}) %all-to-all-start.3) | async-done | bytes 524320 | tf_op jit(solution)/shard_map/all_to_all | solution.py:442
  108.7 4.2 all-to-all-start.4
  113.9 18.6 %all-to-all-done.4 = bf16[8,128,512]{1,2,0:T(8,128)(2,1)} async-done(((bf16[8,128,512]{1,2,0:T(8,128)(2,1)}), bf16[8,128,512]{1,2,0:T(8,128)(2,1)}, u32[]{:S(2)}, u32[]{:S(2)}) %all-to-all-start.4) | async-done | bytes 1048608 | tf_op jit(solution)/shard_map/all_to_all | solution.py:437
  134.8 26.4 %all-gather.8.cloned.1.call-done = bf16[2048,1024]{1,0:T(8,128)(2,1)} async-done(((bf16[256,1024]{1,0:T(8,128)(2,1)}), bf16[2048,1024]{1,0:T(8,128)(2,1)}) %all-gather.8.cloned.1.call-update) | async-done | bytes 4194320 | tf_op jit(solution)/shard_map/all_gather | solution.py:475
  161.2 14.5 %multiply_convert_fusion = (bf16[2048,512]{1,0:T(8,128)(2,1)S(1)}, f32[2048,512]{1,0:T(8,128)}, f32[2048,512]{1,0:T(8,128)}) fusion(f32[512]{0:T(512)S(1)} %dynamic_slice.11, bf16[2048,1024]{1,0:T(8,128)(2,1)} %all-gather.8.cloned.1.call-done, bf16[1024,512]{1,0:T(8,128)(2,1)} %bitcast.181), kind=kOutput, calls=%fused_computation.17 | convolution fusion | flops 2216689664 | bytes 15730688 | tf_op jit(solution)/shard_map/td,df->tf/dot_general | solution.py:458
  177.1 4.3 convolution_convert_fusion.1
  181.5 51.5 %reduce-scatter.5.cloned.1.call-done = bf16[256,1024]{1,0:T(8,128)(2,1)} async-done(((bf16[2048,1024]{1,0:T(8,128)(2,1)}), bf16[256,1024]{1,0:T(8,128)(2,1)}) %reduce-scatter.5.cloned.1.call-update) | async-done | bytes 524304 | tf_op jit(solution)/shard_map/reduce_scatter | solution.py:479
  239.7 36.6 %all-gather.10.cloned.1.call-done = bf16[2048,1024]{1,0:T(8,128)(2,1)} async-done(((bf16[256,1024]{1,0:T(8,128)(2,1)}), bf16[2048,1024]{1,0:T(8,128)(2,1)}) %all-gather.10.cloned.1.call-update) | async-done | bytes 4194320 | tf_op jit(solution)/shard_map/all_gather | solution.py:483
  276.3 7.4 %convert_reduce_fusion = (f32[512]{0:T(512)S(1)}, bf16[2048,512]{1,0:T(8,128)(2,1)S(1)}) fusion(f32[2048,512]{1,0:T(8,128)} %get-tuple-element.48, f32[2048,512]{1,0:T(8,128)} %get-tuple-element.63, f32[512]{0:T(512)S(1)} %dynamic_slice.11, bf16[2048,1024]{1,0:T(8,128)(2,1)} %all-gather.10.cloned.1.call-done, bf16[512,1024]{1,0:T(8,128)(2,1)S(1)} %copy-done), kind=kOutput, calls=%fused_computation.15 | convolution fusion | flops 2165308928 | bytes 15732736 | tf_op jit(solution)/shard_map/td,fd->tf/dot_general | solution.py:458
  285.1 4.3 convolution_convert_fusion
  289.4 51.5 %reduce-scatter.7.cloned.1.call-done = bf16[256,1024]{1,0:T(8,128)(2,1)} async-done(((bf16[2048,1024]{1,0:T(8,128)(2,1)}), bf16[256,1024]{1,0:T(8,128)(2,1)}) %reduce-scatter.7.cloned.1.call-update) | async-done | bytes 524304 | tf_op jit(solution)/shard_map/reduce_scatter | solution.py:487
  350.7 3.5 all-to-all-start.5
  354.9 6.2 convolution_convert_fusion.4
  363.9 4.2 all-to-all-start.9
  370.5 27.6 %attn_bwd.1 = (bf16[2048,128]{1,0:T(8,128)(2,1)S(1)}, bf16[2048,128]{1,0:T(8,128)(2,1)S(1)}, bf16[2048,128]{1,0:T(8,128)(2,1)S(1)}) custom-call(s32[1,2048]{1,0:T(1,128)S(1)} %copy-done.2, s32[1,2048]{1,0:T(1,128)S(1)} %copy-done.2, bf16[2048,128]{1,0:T(8,128)(2,1)S(1)} %copy-done.4, bf16[2048,128]{1,0:T(8,128)(2,1)S(1)} %fusion.30.k_ref, ...), custom_call_target="tpu_custom_call" | custom-call | flops 5368709120 | bytes 3670016 | tf_op jit(solution)/shard_map/attn_bwd/pallas_call | solution.py:164
  399.6 4.1 all-to-all-start.6
  410.6 3.7 all-to-all-start.7
  421.1 3.4 all-to-all-start.8
  424.6 6.1 convolution_convert_fusion.3
  442.5 52.4 %all-reduce = (f32[4,1024]{1,0:T(4,128)S(1)}, f32[4096]{0:T(1024)S(1)}, f32[2,1024]{1,0:T(2,128)S(1)}, f32[2,1024]{1,0:T(2,128)S(1)}) all-reduce(f32[4,1024]{1,0:T(4,128)S(1)} %pad_maximum_fusion.1, f32[4096]{0:T(1024)S(1)} %dynamic_update_slice.13, ...), channel_id=1, replica_groups=mesh['rep'=4,'fsdp'=8] {'rep','fsdp'}, use_global_device_ids=true, to_apply=%region_20.0 | all-reduce | flops 12288 | bytes 98304 | tf_op jit(solution)/shard_map/psum | solution.py:513
  497.3 69.3 %all-reduce.4.cloned.1.call-done = (bf16[128,3072]{1,0:T(8,128)(2,1)}, bf16[128,1024]{1,0:T(8,128)(2,1)}, bf16[128,4096]{1,0:T(8,128)(2,1)}, bf16[512,1024]{1,0:T(8,128)(2,1)}) async-done(((bf16[128,3072]{1,0:T(8,128)(2,1)}, bf16[128,1024]{1,0:T(8,128)(2,1)}, bf16[128,4096]{1,0:T(8,128)(2,1)}, bf16[512,1024]{1,0:T(8,128)(2,1)}), (bf16[128,3072]{1,0:T(8,128)(2,1)}, bf16[128,1024]{1,0:T(8,128)(2,1)}, ...) | async-done | bytes 3145744 | tf_op jit(solution)/shard_map/psum | solution.py:501
  574.4 46.2 %reduce-scatter.9.cloned.1.call-done = bf16[256,1024]{1,0:T(8,128)(2,1)} async-done(((bf16[2048,1024]{1,0:T(8,128)(2,1)}), bf16[256,1024]{1,0:T(8,128)(2,1)}) %reduce-scatter.9.cloned.1.call-update) | async-done | bytes 524304 | tf_op jit(solution)/shard_map/reduce_scatter | solution.py:499
  (157 shorter events, 85.0 us)
Async XLA Ops:
  7.2 169.9 %copy-start = (bf16[512,1024]{1,0:T(8,128)(2,1)S(1)}, bf16[512,1024]{1,0:T(8,128)(2,1)}, u32[]{:S(2)}) copy-start(bf16[512,1024]{1,0:T(8,128)(2,1)} %param.16) | copy-start | bytes 3145732
  7.2 29.3 %copy-start.24 = (f32[4,1024]{1,0:T(4,128)S(1)}, f32[4,1024]{1,0:T(4,128)}, u32[]{:S(2)}) copy-start(f32[4,1024]{1,0:T(4,128)} %param.17) | copy-start | bytes 49156
  7.2 45.0 %all-gather.12.cloned.1.call-start = ((), (), s32[]{:S(2)}) async-start(), calls=%async_computation.21 | async-start | bytes 4718592 | tf_op jit(solution)/shard_map/all_gather | solution.py:463
  7.9 84.1 %all-gather.6.cloned.1.call-start = ((), (), s32[]{:S(2)}) async-start(), calls=%async_computation.14 | async-start | bytes 2359296 | tf_op jit(solution)/shard_map/all_gather | solution.py:470
  10.7 12.1 %all-to-all-start.2 = ((bf16[8,128,128]{1,2,0:T(8,128)(2,1)}), bf16[8,128,128]{1,2,0:T(8,128)(2,1)S(1)}, u32[]{:S(2)}, u32[]{:S(2)}) async-start(bf16[8,128,128]{1,2,0:T(8,128)(2,1)} %bitcast.10), calls=%async_computation.2 | async-start | bytes 524288 | tf_op jit(solution)/shard_map/all_to_all | solution.py:437
  22.8 10.3 %all-to-all-start = ((bf16[8,128,128]{1,2,0:T(8,128)(2,1)}), bf16[8,128,128]{1,2,0:T(8,128)(2,1)S(1)}, u32[]{:S(2)}, u32[]{:S(2)}) async-start(bf16[8,128,128]{1,2,0:T(8,128)(2,1)} %bitcast.3), calls=%async_computation | async-start | bytes 524288 | tf_op jit(solution)/shard_map/all_to_all | solution.py:437
  33.1 13.4 %all-to-all-start.1 = ((bf16[8,128,128]{1,2,0:T(8,128)(2,1)}), bf16[8,128,128]{1,2,0:T(8,128)(2,1)S(1)}, u32[]{:S(2)}, u32[]{:S(2)}) async-start(bf16[8,128,128]{1,2,0:T(8,128)(2,1)} %bitcast.7), calls=%async_computation.1 | async-start | bytes 524288 | tf_op jit(solution)/shard_map/all_to_all | solution.py:437
  36.9 20.1 %copy-start.17 = (bf16[8,128,128]{2,1,0:T(8,128)(2,1)}, bf16[8,128,128]{2,1,0:T(8,128)(2,1)S(1)}, u32[]{:S(2)}) copy-start(bf16[8,128,128]{2,1,0:T(8,128)(2,1)S(1)} %copy.47) | copy-start | bytes 786436
  46.7 9.1 %copy-start.19 = (bf16[8,128,128]{2,1,0:T(8,128)(2,1)}, bf16[8,128,128]{2,1,0:T(8,128)(2,1)S(1)}, u32[]{:S(2)}) copy-start(bf16[8,128,128]{2,1,0:T(8,128)(2,1)S(1)} %copy.49) | copy-start | bytes 786436
  58.4 28.0 %copy-start.3 = (bf16[2048,128]{1,0:T(8,128)(2,1)}, bf16[2048,128]{1,0:T(8,128)(2,1)S(1)}, u32[]{:S(2)}) copy-start(bf16[2048,128]{1,0:T(8,128)(2,1)S(1)} %fusion.27.q_ref) | copy-start | bytes 1572868
  58.4 33.6 %copy-start.25 = (f32[2,1024]{1,0:T(2,128)S(1)}, f32[2,1024]{1,0:T(2,128)}, u32[]{:S(2)}) copy-start(f32[2,1024]{1,0:T(2,128)} %param.19) | copy-start | bytes 24580
  58.4 33.7 %copy-start.26 = (f32[2,1024]{1,0:T(2,128)S(1)}, f32[2,1024]{1,0:T(2,128)}, u32[]{:S(2)}) copy-start(f32[2,1024]{1,0:T(2,128)} %param.20) | copy-start | bytes 24580
  88.5 13.2 %all-to-all-start.3 = ((bf16[8,256,128]{1,2,0:T(8,128)(2,1)}), bf16[8,256,128]{1,2,0:T(8,128)(2,1)S(1)}, u32[]{:S(2)}, u32[]{:S(2)}) async-start(bf16[8,256,128]{1,2,0:T(8,128)(2,1)} %copy.52), calls=%async_computation.3 | async-start | bytes 1048576 | tf_op jit(solution)/shard_map/all_to_all | solution.py:442
  92.0 69.2 %all-gather.8.cloned.1.call-start = ((), (), s32[]{:S(2)}) async-start(), calls=%async_computation.15 | async-start | bytes 4718592 | tf_op jit(solution)/shard_map/all_gather | solution.py:475
  108.7 23.8 %all-to-all-start.4 = ((bf16[8,128,512]{1,2,0:T(8,128)(2,1)}), bf16[8,128,512]{1,2,0:T(8,128)(2,1)}, u32[]{:S(2)}, u32[]{:S(2)}) async-start(bf16[8,128,512]{1,2,0:T(8,128)(2,1)} %bitcast.174), calls=%async_computation.4 | async-start | bytes 2097152 | tf_op jit(solution)/shard_map/all_to_all | solution.py:437
  112.9 120.0 %reduce-scatter.5.cloned.1.call-start = ((), (), s32[]{:S(2)}) async-start(), calls=%async_computation.16 | async-start | bytes 4718592 | tf_op jit(solution)/shard_map/reduce_scatter | solution.py:479
  181.4 94.9 %all-gather.10.cloned.1.call-start = ((), (), s32[]{:S(2)}) async-start(), calls=%async_computation.17 | async-start | bytes 4718592 | tf_op jit(solution)/shard_map/all_gather | solution.py:483
  239.5 101.4 %reduce-scatter.7.cloned.1.call-start = ((), (), s32[]{:S(2)}) async-start(), calls=%async_computation.18 | async-start | bytes 4718592 | tf_op jit(solution)/shard_map/reduce_scatter | solution.py:487
  276.3 8.7 %copy-start.22 = (bf16[8,128,512]{2,1,0:T(8,128)(2,1)S(1)}, bf16[8,128,512]{2,1,0:T(8,128)(2,1)}, u32[]{:S(2)}) copy-start(bf16[8,128,512]{2,1,0:T(8,128)(2,1)} %copy.54) | copy-start | bytes 3145732
  289.4 51.5 %copy-start.10 = (f32[256,1024]{1,0:T(8,128)S(1)}, f32[256,1024]{1,0:T(8,128)}, u32[]{:S(2)}) copy-start(f32[256,1024]{1,0:T(8,128)} %copy-done.9) | copy-start | bytes 3145732
  350.7 13.2 %all-to-all-start.5 = ((bf16[8,256,128]{2,1,0:T(8,128)(2,1)}), bf16[8,256,128]{2,1,0:T(8,128)(2,1)S(1)}, u32[]{:S(2)}, u32[]{:S(2)}) async-start(bf16[8,256,128]{2,1,0:T(8,128)(2,1)} %bitcast.165), calls=%async_computation.7 | async-start | bytes 1048576 | tf_op jit(solution)/shard_map/all_to_all | solution.py:437
  354.2 80.3 %reduce-scatter.11.cloned.1.call-start = ((), (), s32[]{:S(2)}) async-start(), calls=%async_computation.20 | async-start | bytes 2359296 | tf_op jit(solution)/shard_map/reduce_scatter | solution.py:495
  363.9 35.7 %all-to-all-start.9 = ((bf16[8,128,512]{2,1,0:T(8,128)(2,1)}), bf16[8,128,512]{2,1,0:T(8,128)(2,1)}, u32[]{:S(2)}, u32[]{:S(2)}) async-start(bf16[8,128,512]{2,1,0:T(8,128)(2,1)} %bitcast.40), calls=%async_computation.13 | async-start | bytes 2097152 | tf_op jit(solution)/shard_map/all_to_all | solution.py:442
  370.5 27.6 %copy-start.8 = (bf16[1,2048,1024]{2,1,0:T(8,128)(2,1)S(1)}, bf16[1,2048,1024]{2,1,0:T(8,128)(2,1)}, u32[]{:S(2)}) copy-start(bf16[1,2048,1024]{2,1,0:T(8,128)(2,1)} %all-gather.12.cloned.1.call-done) | copy-start | bytes 12582916
  399.6 11.0 %all-to-all-start.6 = ((bf16[8,128,128]{1,2,0:T(8,128)(2,1)}), bf16[8,128,128]{1,2,0:T(8,128)(2,1)S(1)}, u32[]{:S(2)}, u32[]{:S(2)}) async-start(bf16[8,128,128]{1,2,0:T(8,128)(2,1)} %bitcast.168), calls=%async_computation.9 | async-start | bytes 524288 | tf_op jit(solution)/shard_map/all_to_all | solution.py:442
  410.6 10.5 %all-to-all-start.7 = ((bf16[8,128,128]{1,2,0:T(8,128)(2,1)}), bf16[8,128,128]{1,2,0:T(8,128)(2,1)S(1)}, u32[]{:S(2)}, u32[]{:S(2)}) async-start(bf16[8,128,128]{1,2,0:T(8,128)(2,1)} %bitcast.167), calls=%async_computation.10 | async-start | bytes 524288 | tf_op jit(solution)/shard_map/all_to_all | solution.py:442
  421.1 12.3 %all-to-all-start.8 = ((bf16[8,128,128]{1,2,0:T(8,128)(2,1)}), bf16[8,128,128]{1,2,0:T(8,128)(2,1)S(1)}, u32[]{:S(2)}, u32[]{:S(2)}) async-start(bf16[8,128,128]{1,2,0:T(8,128)(2,1)} %bitcast.166), calls=%async_computation.11 | async-start | bytes 524288 | tf_op jit(solution)/shard_map/all_to_all | solution.py:442
  424.6 142.0 %all-reduce.4.cloned.1.call-start = ((), (), s32[]{:S(2)}) async-start(), calls=%async_computation.22 | async-start | bytes 6291456 | tf_op jit(solution)/shard_map/psum | solution.py:501
  434.5 186.1 %reduce-scatter.9.cloned.1.call-start = ((), (), s32[]{:S(2)}) async-start(), calls=%async_computation.19 | async-start | bytes 4718592 | tf_op jit(solution)/shard_map/reduce_scatter | solution.py:499
  566.6 6.2 copy-start.21
  568.5 52.1 %copy-start.12 = (f32[256,1024]{1,0:T(8,128)S(1)}, f32[256,1024]{1,0:T(8,128)}, u32[]{:S(2)}) copy-start(f32[256,1024]{1,0:T(8,128)} %copy-done.11) | copy-start | bytes 3145732
  568.5 54.1 %copy-start.1 = (bf16[512,1024]{1,0:T(8,128)(2,1)S(1)}, bf16[512,1024]{1,0:T(8,128)(2,1)}, u32[]{:S(2)}) copy-start(bf16[512,1024]{1,0:T(8,128)(2,1)} %param.16) | copy-start | bytes 3145732
  (16 other events, 32.8 us)
Sparse Core Ops, SparseCore 0:
  9.9 42.2 all-gather.11
  54.1 27.8 all-gather.5
  106.6 54.5 all-gather.7
  181.5 51.3 reduce-scatter.4
  239.6 36.6 all-gather.9
  289.5 51.3 reduce-scatter.6
  358.9 42.5 reduce-scatter.10
  434.7 131.8 all-reduce.3
  570.3 50.2 reduce-scatter.8

commit v2 on v1

--- a/solution.py
+++ b/solution.py
@@ -150,13 +150,13 @@
             return 0
 
         lax.fori_loop(lo, hi, step, 0)
-        dk_ref[rows, :] = dk_acc[...].astype(jnp.bfloat16)
-        dv_ref[rows, :] = dv_acc[...].astype(jnp.bfloat16)
+        dk_ref[lax.rem(j, 2), j // 2] = dk_acc[...].astype(jnp.bfloat16)
+        dv_ref[lax.rem(j, 2), j // 2] = dv_acc[...].astype(jnp.bfloat16)
 
     @pl.loop(0, n)
     def _(i):
         rows = pl.ds(pl.multiple_of(i * BQ, BQ), BQ)
-        dq_ref[rows, :] = (jnp.transpose(dqt[:, rows]) * scale).astype(jnp.bfloat16)
+        dq_ref[lax.rem(i, 2), i // 2] = (jnp.transpose(dqt[:, rows]) * scale).astype(jnp.bfloat16)
 
 
 def attn_bwd(scale, seg, q, k, v, g, o, lse):
@@ -164,7 +164,7 @@
     return pl.pallas_call(
         functools.partial(attn_bwd_body, scale),
         name="attn_bwd",
-        out_shape=tuple(jax.ShapeDtypeStruct((length, width), jnp.bfloat16) for _ in range(3)),
+        out_shape=tuple(jax.ShapeDtypeStruct((2, length // BQ // 2, BQ, width), jnp.bfloat16) for _ in range(3)),
         in_specs=[SM, VM, VM, VM, VM, VM, VM, VM],
         out_specs=(VM, VM, VM),
         scratch_shapes=[
@@ -176,6 +176,746 @@
         compiler_params=pltpu.CompilerParams(vmem_limit_bytes=32 << 20),
         cost_estimate=pl.CostEstimate(flops=10 * length * length * width, bytes_accessed=14 * length * width, transcendentals=2 * length * length),
     )(seg, seg, q, k, v, g, o, lse)
+
+
+MESH = pl.DeviceIdType.MESH
+ANY = pl.BlockSpec(memory_space=pl.ANY)
+F32 = jnp.float32
+BF16 = jnp.bfloat16
+
+
+def tn(a, b):
+    return lax.dot_general(a, b, (((0,), (0,)), ((), ())), preferred_element_type=F32)
+
+
+def fold_rows(v):
+    return jnp.sum(v.reshape(v.shape[0] // 8, 8, v.shape[1]), axis=0)
+
+
+class Wires:
+    def __init__(self, send_sems, recv_sems, local_sems):
+        self.send_sems, self.recv_sems, self.local_sems = send_sems, recv_sems, local_sems
+        self.count = 0
+        self.local_count = 0
+        self.sent = []
+        self.rep = lax.axis_index("rep")
+        self.own = lax.axis_index("fsdp")
+
+    def remote(self, src, dst, peer, rep=None):
+        i = self.count
+        self.count = i + 1
+        return pltpu.make_async_remote_copy(
+            src_ref=src, dst_ref=dst, send_sem=self.send_sems.at[i], recv_sem=self.recv_sems.at[i],
+            device_id=(self.rep if rep is None else rep, peer), device_id_type=MESH,
+        )
+
+    def send(self, src, dst, peer):
+        copy = self.remote(src, dst, peer)
+        copy.start()
+        self.sent.append(copy)
+        return copy
+
+    def local(self, src, dst):
+        copy = pltpu.make_async_copy(src, dst, self.local_sems.at[self.local_count])
+        self.local_count += 1
+        copy.start()
+        return copy
+
+    def greet(self, peers):
+        barrier = pltpu.get_barrier_semaphore()
+        for rep, peer in peers:
+            pl.semaphore_signal(barrier, inc=1, device_id=(rep, peer), device_id_type=MESH)
+        pl.semaphore_wait(barrier, len(peers))
+
+    def finish(self):
+        for copy in self.sent:
+            copy.wait_send()
+
+
+def rows_of(index, size):
+    return pl.ds(pl.multiple_of(index * size, size), size)
+
+
+class Spread:
+    def __init__(self, wires, slots, half):
+        self.wires, self.slots, self.half = wires, slots, half
+        self.chip = wires.own // 2
+        self.x, self.y = lax.bitwise_xor(wires.own, 2), lax.bitwise_xor(wires.own, 4)
+        self.cx, self.cy, self.cd = (lax.bitwise_xor(self.chip, m) for m in (1, 2, 3))
+        self.a, self.b = pl.ds(0, half), pl.ds(half, half)
+
+    def piece(self, chip, part):
+        return self.slots.at[chip, part]
+
+    def put(self, chip, part, peer):
+        return self.wires.send(self.piece(chip, part), self.piece(chip, part), peer)
+
+    def first_half(self):
+        self.xa = self.put(self.chip, self.a, self.x)
+        self.ya = self.put(self.chip, self.a, self.y)
+
+    def second_half(self):
+        self.yb = self.put(self.chip, self.b, self.y)
+        self.xb = self.put(self.chip, self.b, self.x)
+
+    def relay(self):
+        self.xa.wait_recv()
+        self.da = self.put(self.cx, self.a, self.y)
+        self.yb.wait_recv()
+        self.db = self.put(self.cy, self.b, self.x)
+
+    def wait_sides(self):
+        self.xb.wait_recv()
+        self.ya.wait_recv()
+
+    def wait_diagonal(self):
+        self.da.wait_recv()
+        self.db.wait_recv()
+
+
+class Gather:
+    def __init__(self, wires, part, side, last, half):
+        self.wires, self.part, self.side, self.last, self.half = wires, part, side, last, half
+        self.chip = wires.own // 2
+        self.x, self.y = lax.bitwise_xor(wires.own, 2), lax.bitwise_xor(wires.own, 4)
+        self.cx, self.cy, self.cd = (lax.bitwise_xor(self.chip, m) for m in (1, 2, 3))
+        self.a, self.b = pl.ds(0, half), pl.ds(half, half)
+
+    def send_x(self):
+        self.x_own = self.wires.send(self.part.at[self.cx, self.a], self.side.at[0], self.x)
+
+    def send_y(self):
+        self.y_own = self.wires.send(self.part.at[self.cy, self.b], self.side.at[1], self.y)
+
+    def send_diagonal(self):
+        self.x_far = self.wires.send(self.part.at[self.cd, self.a], self.side.at[2], self.x)
+        self.y_far = self.wires.send(self.part.at[self.cd, self.b], self.side.at[3], self.y)
+
+    def relay(self):
+        step = 32
+
+        def add(chip, start, slot):
+            @pl.loop(0, self.half // step)
+            def _(t):
+                rows = pl.ds(pl.multiple_of(start + t * step, step), step)
+                near = self.part[chip, rows, :].astype(F32) + self.side[slot, rows_of(t, step), :].astype(F32)
+                self.part[chip, rows, :] = near.astype(BF16)
+
+        self.x_far.wait_recv()
+        add(self.cy, 0, 2)
+        self.y_last = self.wires.send(self.part.at[self.cy, self.a], self.last.at[0], self.y)
+        self.y_far.wait_recv()
+        add(self.cx, self.half, 3)
+        self.x_last = self.wires.send(self.part.at[self.cx, self.b], self.last.at[1], self.x)
+
+    def wait_first(self):
+        self.x_own.wait_recv()
+        self.y_last.wait_recv()
+
+    def wait_second(self):
+        self.y_own.wait_recv()
+        self.x_last.wait_recv()
+
+    def total(self, which, offset, size):
+        rows = pl.ds(pl.multiple_of(which * self.half + offset, size), size)
+        here = pl.ds(pl.multiple_of(offset, size), size)
+        return self.part[self.chip, rows, :].astype(F32) + self.side[which, here, :].astype(F32) + self.last[which, here, :].astype(F32)
+
+
+def middle_body(
+    heads, x, cot, up_w, out_w, down_w, got_x, got_y, got_d, proj_bias, hidden_bias, gain, shift,
+    output, branch_grad, grad_heads, vec, down_grad, upout_grad,
+    att, out_full, up_full, down_full, h1, z1, r1, gs, fl, act, slope, part, side, last, sl, pre, part2, side2, last2,
+    branch_low, agl, acc, d_send, d_recv, d_keep, u_send, u_recv, u_keep, o_send, o_recv, o_keep,
+    send_sems, recv_sems, local_sems,
+):
+    w = Wires(send_sems, recv_sems, local_sems)
+    own = w.own
+    core, chip = lax.rem(own, 2), own // 2
+    mate = lax.bitwise_xor(own, 1)
+    cx, cy, cd = (lax.bitwise_xor(chip, m) for m in (1, 2, 3))
+    toks, width = x.shape
+    ff = up_full.shape[1]
+    head_width = heads.shape[1]
+    half = toks // 2
+    piece = up_w.shape[0]
+    tile = 256
+    w.greet([(w.rep, lax.bitwise_xor(own, m)) for m in range(1, 8)])
+
+    swaps = []
+    for m in (6, 2, 4, 1, 3, 5, 7):
+        peer = lax.bitwise_xor(own, m)
+        swaps.append(w.send(heads.at[rows_of(peer, toks)], att.at[:, rows_of(own, head_width)], peer))
+    weights = []
+    for m, src in ((0, None), (2, got_x), (4, got_y), (6, got_d)):
+        dst = rows_of(lax.bitwise_xor(own, m), piece)
+        src_out = out_w if src is None else src.at[pl.ds(piece, piece)]
+        src_up = up_w.at[:, rows_of(chip, ff)] if src is None else src.at[pl.ds(0, piece)]
+        for s, full in ((src_out, out_full), (src_up, up_full)):
+            weights.append((w.local(s, full.at[dst]), w.send(s, full.at[dst], mate)))
+    dst = rows_of(core, ff // 2)
+    weights.append((w.local(down_w, down_full.at[dst]), w.send(down_w, down_full.at[dst], mate)))
+    att[:, rows_of(own, head_width)] = heads[rows_of(own, toks), :]
+    for copy in swaps:
+        copy.wait_recv()
+    for here, there in weights:
+        here.wait()
+        there.wait_recv()
+
+    @pl.loop(0, width // tile)
+    def _(n):
+        cols = rows_of(n, tile)
+        h1[:, cols] = nn(att[...], out_full[:, cols]) + proj_bias[2:3, cols] + x[:, cols].astype(F32)
+
+    step = 32
+    acc[...] = jnp.zeros_like(acc)
+
+    def first_rows(t):
+        rows = rows_of(t, step)
+        v = h1[rows, :]
+        center = v - jnp.mean(v, axis=1, keepdims=True)
+        inv = lax.rsqrt(jnp.mean(center * center, axis=1, keepdims=True) + 1e-05)
+        z = center * inv
+        z1[rows, :] = z
+        r1[rows, :] = jnp.broadcast_to(inv, (step, 128))
+        fl[chip, rows, :] = (z * gain[0:1, :] + shift[0:1, :]).astype(BF16)
+
+    spread = Spread(w, fl, half)
+    pl.loop(0, half // step)(first_rows)
+    spread.first_half()
+    pl.loop(half // step, toks // step)(first_rows)
+    spread.second_half()
+
+    def forward(k):
+        @pl.loop(0, ff // tile)
+        def _(n):
+            cols = rows_of(n, tile)
+            hidden = nn(fl[k], up_full[:, cols]) + hidden_bias[:, pl.ds(pl.multiple_of(chip * ff + n * tile, tile), tile)]
+            cdf = 0.5 * (1.0 + lax.erf(hidden * (2.0**-0.5)))
+            act[k, :, cols] = (hidden * cdf).astype(BF16)
+            slope[k, :, cols] = cdf + hidden * (jnp.exp(-0.5 * hidden * hidden) * ((2.0 * math.pi) ** -0.5))
+
+        @pl.loop(0, width // tile)
+        def _(n):
+            cols = rows_of(n, tile)
+            part[k, :, cols] = nn(act[k], down_full[:, cols]).astype(BF16)
+
+    forward(chip)
+    gather = Gather(w, part, side, last, half)
+    spread.relay()
+    spread.wait_sides()
+    forward(cx)
+    gather.send_x()
+    forward(cy)
+    gather.send_y()
+    spread.wait_diagonal()
+    forward(cd)
+    gather.send_diagonal()
+    gather.relay()
+
+    def second_rows(which, t):
+        rows = pl.ds(pl.multiple_of(which * half + t * step, step), step)
+        v = z1[rows, :] * gain[0:1, :] + shift[0:1, :] + gather.total(which, t * step, step) + proj_bias[3:4, :]
+        center = v - jnp.mean(v, axis=1, keepdims=True)
+        inv = lax.rsqrt(jnp.mean(center * center, axis=1, keepdims=True) + 1e-05)
+        z = center * inv
+        output[rows, :] = (z * gain[1:2, :] + shift[1:2, :]).astype(BF16)
+        c = cot[rows, :].astype(F32)
+        e = c * gain[1:2, :]
+        grad = inv * (e - jnp.mean(e, axis=1, keepdims=True) - z * jnp.mean(e * z, axis=1, keepdims=True))
+        gs[rows, :] = grad
+        low = grad.astype(BF16)
+        sl[chip, rows, :] = low
+        acc[0] += fold_rows(c * z)
+        acc[1] += fold_rows(c)
+        acc[2] += fold_rows(low.astype(F32))
+
+    spread2 = Spread(w, sl, half)
+    gather.wait_first()
+    pl.loop(0, half // step)(functools.partial(second_rows, 0))
+    spread2.first_half()
+    gather.wait_second()
+    pl.loop(0, half // step)(functools.partial(second_rows, 1))
+    spread2.second_half()
+
+    def backward(k):
+        @pl.loop(0, ff // tile)
+        def _(n):
+            cols = rows_of(n, tile)
+            grad = nt(sl[k], down_full[cols, :]) * slope[k, :, cols]
+            low = grad.astype(BF16)
+            pre[k, :, cols] = low
+            acc[3, :, cols] += fold_rows(low.astype(F32))
+
+        @pl.loop(0, width // tile)
+        def _(n):
+            cols = rows_of(n, tile)
+            part2[k, :, cols] = nt(pre[k], up_full[cols, :]).astype(BF16)
+
+    backward(chip)
+    gather2 = Gather(w, part2, side2, last2, half)
+    spread2.relay()
+    spread2.wait_sides()
+    backward(cx)
+    gather2.send_x()
+    backward(cy)
+    gather2.send_y()
+    spread2.wait_diagonal()
+    backward(cd)
+    gather2.send_diagonal()
+
+    def down_rows(which, n):
+        cols = pl.ds(pl.multiple_of(which * (ff // 2) + n * tile, tile), tile)
+        lhs = act[:, :, cols].reshape(4 * toks, tile)
+        return tn(lhs, sl[...].reshape(4 * toks, width))
+
+    @pl.loop(0, ff // 2 // tile)
+    def _(n):
+        d_send[rows_of(n, tile), :] = down_rows(1 - core, n).astype(BF16)
+
+    d_copy = w.send(d_send, d_recv, mate)
+    gather2.relay()
+
+    @pl.loop(0, ff // 2 // tile)
+    def _(n):
+        d_keep[rows_of(n, tile), :] = down_rows(core, n)
+
+    def up_rows(which, k):
+        cols = pl.ds(pl.multiple_of((2 * k + which) * piece, piece), piece)
+        lhs = fl[:, :, cols].reshape(4 * toks, piece)
+        return tn(lhs, pre[...].reshape(4 * toks, ff))
+
+    @pl.loop(0, 4)
+    def _(k):
+        u_send[k] = up_rows(1 - core, k).astype(BF16)
+
+    u_copy = w.send(u_send, u_recv, mate)
+
+    def branch_rows(which, t):
+        rows = pl.ds(pl.multiple_of(which * half + t * step, step), step)
+        grad = gs[rows, :] + gather2.total(which, t * step, step)
+        z = z1[rows, :]
+        e = grad * gain[0:1, :]
+        out = r1[rows, 0:1] * (e - jnp.mean(e, axis=1, keepdims=True) - z * jnp.mean(e * z, axis=1, keepdims=True))
+        branch_grad[rows, :] = out
+        low = out.astype(BF16)
+        branch_low[rows, :] = low
+        acc[4] += fold_rows(grad * z)
+        acc[5] += fold_rows(grad)
+        acc[6] += fold_rows(low.astype(F32))
+
+    gather2.wait_first()
+    pl.loop(0, half // step)(functools.partial(branch_rows, 0))
+    gather2.wait_second()
+    pl.loop(0, half // step)(functools.partial(branch_rows, 1))
+
+    @pl.loop(0, width // tile)
+    def _(n):
+        cols = rows_of(n, tile)
+        agl[:, cols] = nt(branch_low[...], out_full[cols, :]).astype(BF16)
+
+    backs = []
+    for m in (6, 2, 4, 1, 3, 5, 7):
+        peer = lax.bitwise_xor(own, m)
+        backs.append(w.send(agl.at[:, rows_of(peer, head_width)], grad_heads.at[rows_of(own, toks)], peer))
+    grad_heads[rows_of(own, toks), :] = agl[:, rows_of(own, head_width)]
+
+    def out_rows(which, k):
+        cols = pl.ds(pl.multiple_of((2 * k + which) * piece, piece), piece)
+        return tn(att[:, cols], branch_low[...])
+
+    @pl.loop(0, 4)
+    def _(k):
+        o_send[k] = out_rows(1 - core, k).astype(BF16)
+
+    o_copy = w.send(o_send, o_recv, mate)
+
+    @pl.loop(0, 4)
+    def _(k):
+        u_keep[k] = up_rows(core, k)
+        o_keep[k] = out_rows(core, k)
+
+    d_copy.wait_recv()
+
+    @pl.loop(0, ff // 2 // 64)
+    def _(t):
+        rows = rows_of(t, 64)
+        down_grad[rows, :] = (d_keep[rows, :] + d_recv[rows, :].astype(F32)).astype(BF16)
+
+    u_copy.wait_recv()
+    o_copy.wait_recv()
+
+    @pl.loop(0, 4)
+    def _(k):
+        upout_grad[k, 0] = (u_keep[k] + u_recv[k].astype(F32)).astype(BF16)
+        upout_grad[k, 1] = (o_keep[k] + o_recv[k].astype(F32)).astype(BF16)
+
+    vec[...] = jnp.zeros_like(vec)
+    for row, slot in ((2, 6), (3, 2), (4, 4), (5, 0), (6, 5), (7, 1)):
+        vec[row : row + 1, :] = jnp.sum(acc[slot], axis=0, keepdims=True)
+    hidden_sum = jnp.sum(acc[3], axis=0, keepdims=True)
+    for k in range(4):
+        vec[8 + k : 9 + k, :] = jnp.where(chip == k, hidden_sum, jnp.zeros_like(hidden_sum))
+    for copy in backs:
+        copy.wait_recv()
+    w.finish()
+
+
+def middle(heads, x, cot, up_w, out_w, down_w, got_x, got_y, got_d, proj_bias, hidden_bias, gain, shift):
+    toks, width = x.shape
+    ff = up_w.shape[1] // 4
+    piece = up_w.shape[0]
+    half = toks // 2
+    shape = jax.ShapeDtypeStruct
+    vm = pltpu.VMEM
+    return pl.pallas_call(
+        middle_body,
+        name="middle",
+        out_shape=(
+            shape((toks, width), BF16),
+            shape((toks, width), F32),
+            shape(heads.shape, BF16),
+            shape((16, width), F32),
+            shape((ff // 2, width), BF16),
+            shape((4, 2, piece, width), BF16),
+        ),
+        in_specs=[VM, VM, VM] + [ANY] * 6 + [VM] * 4,
+        out_specs=(VM,) * 6,
+        scratch_shapes=[
+            vm((toks, width), BF16), vm((width, width), BF16), vm((width, ff), BF16), vm((ff, width), BF16),
+            vm((toks, width), F32), vm((toks, width), F32), vm((toks, 128), F32), vm((toks, width), F32),
+            vm((4, toks, width), BF16), vm((4, toks, ff), BF16), vm((4, toks, ff), F32),
+            vm((4, toks, width), BF16), vm((4, half, width), BF16), vm((2, half, width), BF16),
+            vm((4, toks, width), BF16), vm((4, toks, ff), BF16),
+            vm((4, toks, width), BF16), vm((4, half, width), BF16), vm((2, half, width), BF16),
+            vm((toks, width), BF16), vm((toks, width), BF16), vm((8, 8, width), F32),
+            vm((ff // 2, width), BF16), vm((ff // 2, width), BF16), vm((ff // 2, width), F32),
+            vm((4, piece, ff), BF16), vm((4, piece, ff), BF16), vm((4, piece, ff), F32),
+            vm((4, piece, width), BF16), vm((4, piece, width), BF16), vm((4, piece, width), F32),
+            pltpu.SemaphoreType.DMA((64,)), pltpu.SemaphoreType.DMA((64,)), pltpu.SemaphoreType.DMA((16,)),
+        ],
+        compiler_params=pltpu.CompilerParams(collective_id=1, has_side_effects=True, vmem_limit_bytes=60 << 20),
+    )(heads, x, cot, up_w, out_w, down_w, got_x, got_y, got_d, proj_bias, hidden_bias, gain, shift)
+
+
+def project_body(x, qkv_w, proj_bias, q_out, k_out, v_out, xs, w_full, stage, send_sems, recv_sems, local_sems):
+    w = Wires(send_sems, recv_sems, local_sems)
+    own = w.own
+    core, chip = lax.rem(own, 2), own // 2
+    mate = lax.bitwise_xor(own, 1)
+    toks, width = x.shape
+    piece = qkv_w.shape[0]
+    share = width // 4
+    head_width = share // 2
+    w.greet([(w.rep, lax.bitwise_xor(own, m)) for m in (1, 2, 4, 6)])
+    mine = rows_of(own, piece)
+
+    def source(part, to_chip):
+        return qkv_w.at[:, pl.ds(pl.multiple_of(part * width + to_chip * share, share), share)]
+
+    arrivals = []
+    for m in (6, 2, 4):
+        peer = lax.bitwise_xor(own, m)
+        copies = [w.send(source(p, lax.bitwise_xor(chip, m // 2)), w_full.at[mine, pl.ds(p * share, share)], peer) for p in range(3)]
+        arrivals.append((peer, copies))
+    xs[chip] = x[...]
+    spread = Spread(w, xs, toks // 2)
+    spread.first_half()
+    spread.second_half()
+    here = [w.local(source(p, chip), w_full.at[mine, pl.ds(p * share, share)]) for p in range(3)]
+    theirs = [w.send(source(p, chip), w_full.at[mine, pl.ds(p * share, share)], mate) for p in range(3)]
+    for peer, copies in arrivals:
+        for copy in copies:
+            copy.wait_recv()
+        rows = rows_of(peer, piece)
+        theirs.append(w.send(w_full.at[rows], w_full.at[rows], mate))
+    for copy in here:
+        copy.wait()
+    for copy in theirs:
+        copy.wait_recv()
+    outs = (q_out, k_out, v_out)
+    swaps = []
+
+    def block(k):
+        rows = rows_of(2 * k + core, toks)
+        for p in range(3):
+            r = nn(xs[k], w_full[:, pl.ds(p * share, share)])
+            if p != 1:
+                r = r + proj_bias[p // 2 : p // 2 + 1, rows_of(chip, share)]
+            stage[k, :, pl.ds(p * share, share)] = r.astype(BF16)
+            swaps.append(w.send(stage.at[k, :, pl.ds(pl.multiple_of(p * share + (1 - core) * head_width, head_width), head_width)], outs[p].at[rows], mate))
+            outs[p][rows, :] = stage[k, :, pl.ds(pl.multiple_of(p * share + core * head_width, head_width), head_width)]
+
+    block(chip)
+    spread.relay()
+    spread.wait_sides()
+    block(spread.cx)
+    block(spread.cy)
+    spread.wait_diagonal()
+    block(spread.cd)
+    for copy in swaps:
+        copy.wait_recv()
+    w.finish()
+
+
+def project(x, qkv_w, proj_bias):
+    toks, width = x.shape
+    piece = qkv_w.shape[0]
+    shape = jax.ShapeDtypeStruct
+    vm = pltpu.VMEM
+    heads = shape((8 * toks, width // 8), BF16)
+    return pl.pallas_call(
+        project_body,
+        name="project",
+        out_shape=(heads, heads, heads, shape((4, toks, width), BF16), shape((8 * piece, 3 * width // 4), BF16)),
+        in_specs=[VM] * 3,
+        out_specs=(VM,) * 5,
+        scratch_shapes=[
+            vm((4, toks, 3 * width // 4), BF16),
+            pltpu.SemaphoreType.DMA((48,)), pltpu.SemaphoreType.DMA((48,)), pltpu.SemaphoreType.DMA((8,)),
+        ],
+        compiler_params=pltpu.CompilerParams(collective_id=0, has_side_effects=True, vmem_limit_bytes=40 << 20),
+    )(x, qkv_w, proj_bias)
+
+
+CHUNKS = 8
+
+
+def finish_body(
+    dq, dk, dv, xs, w_full, branch_grad, vec, input_grad, qkv_total, vec_total,
+    grads, part, side, last, q_send, q_recv, q_keep, q_piece, z_own, z_in, z_mid, z_far, z_out, v_sum, v_recv,
+    send_sems, recv_sems, local_sems,
+):
+    w = Wires(send_sems, recv_sems, local_sems)
+    own, rep = w.own, w.rep
+    core, chip = lax.rem(own, 2), own // 2
+    mate = lax.bitwise_xor(own, 1)
+    toks, width = branch_grad.shape
+    share = width // 4
+    head_width = share // 2
+    piece = q_keep.shape[1]
+    half = toks // 2
+    tile = 256
+    z1, z2, z3 = (lax.bitwise_xor(rep, m) for m in (1, 2, 3))
+    w.greet([(rep, lax.bitwise_xor(own, m)) for m in (1, 2, 4, 6)] + [(z1, own), (z2, own), (z3, own)])
+
+    swaps = []
+    for p, g in enumerate((dq, dk, dv)):
+        cols = pl.ds(pl.multiple_of(p * share + core * head_width, head_width), head_width)
+        swaps.append(w.send(g.at[1 - core], grads.at[:, :, cols], mate))
+        grads[:, :, cols] = g[core]
+    v_sum[...] = vec[...]
+    for row, g in ((0, dq), (1, dv)):
+        total = jnp.sum(g[...].reshape(8 * toks, head_width).astype(F32), axis=0, keepdims=True)
+        v_sum[row : row + 1, rows_of(own, head_width)] = total
+    rounds = [(None, mate), (None, lax.bitwise_xor(own, 2)), (None, lax.bitwise_xor(own, 4)), (z1, own), (z2, own)]
+    flying = []
+
+    def vec_start(i):
+        copy = w.remote(v_sum.at[...] if i == 0 else v_recv.at[4 + i], v_recv.at[i], rounds[i][1], rounds[i][0])
+        copy.start()
+        w.sent.append(copy)
+        flying.append(copy)
+
+    def vec_step(i):
+        flying[i].wait_recv()
+        base = v_sum[...] if i == 0 else v_recv[4 + i]
+        if i < 4:
+            v_recv[5 + i] = base + v_recv[i]
+            vec_start(i + 1)
+        else:
+            vec_total[...] = base + v_recv[i]
+
+    vec_start(0)
+    for copy in swaps:
+        copy.wait_recv()
+
+    def qkv_rows(which, k):
+        cols = pl.ds(pl.multiple_of((2 * k + which) * piece, piece), piece)
+        return tn(xs[:, :, cols].reshape(4 * toks, piece), grads[...].reshape(4 * toks, 3 * share))
+
+    @pl.loop(0, 4)
+    def _(k):
+        q_send[k] = qkv_rows(1 - core, k).astype(BF16)
+
+    q_copy = w.send(q_send, q_recv, mate)
+
+    @pl.loop(0, 4)
+    def _(k):
+        q_keep[k] = qkv_rows(core, k)
+
+    q_copy.wait_recv()
+
+    @pl.loop(0, 4)
+    def _(k):
+        q_piece[k] = (q_keep[k] + q_recv[k].astype(F32)).astype(BF16)
+
+    moved = []
+    for m in (6, 2, 4):
+        peer = lax.bitwise_xor(own, m)
+        for p in range(3):
+            dst = z_own.at[:, pl.ds(pl.multiple_of(p * width + chip * share, share), share)]
+            moved.append(w.send(q_piece.at[lax.bitwise_xor(chip, m // 2), :, pl.ds(p * share, share)], dst, peer))
+    for p in range(3):
+        z_own[:, pl.ds(pl.multiple_of(p * width + chip * share, share), share)] = q_piece[chip, :, pl.ds(p * share, share)]
+    vec_step(0)
+
+    def partial(k):
+        @pl.loop(0, width // tile)
+        def _(n):
+            cols = rows_of(n, tile)
+            part[k, :, cols] = nt(grads[k], w_full[cols, :]).astype(BF16)
+
+    gather = Gather(w, part, side, last, half)
+    partial(gather.cd)
+    gather.send_diagonal()
+    partial(gather.cx)
+    gather.send_x()
+    partial(gather.cy)
+    gather.send_y()
+    partial(chip)
+    vec_step(1)
+    for copy in moved:
+        copy.wait_recv()
+
+    size = piece // CHUNKS
+    inner = jnp.logical_or(rep == 1, rep == 2)
+    first, middle_hop, back = [], [], []
+    for i in range(CHUNKS):
+        rows = pl.ds(i * size, size)
+        first.append(w.remote(z_own.at[rows], z_in.at[rows], own, z1))
+    for i in range(CHUNKS):
+        rows = pl.ds(i * size, size)
+        middle_hop.append(w.remote(z_mid.at[rows], z_far.at[rows], own, z3))
+    for i in range(CHUNKS):
+        rows = pl.ds(i * size, size)
+        back.append(w.remote(z_out.at[rows], z_out.at[rows], own, z1))
+
+    @pl.when(jnp.logical_not(inner))
+    def _():
+        for i in range(CHUNKS):
+            first[i].start()
+
+    @pl.when(inner)
+    def _():
+        for i in range(CHUNKS):
+            rows = pl.ds(i * size, size)
+            first[i].wait_recv()
+            z_mid[rows, :] = (z_own[rows, :].astype(F32) + z_in[rows, :].astype(F32)).astype(BF16)
+            middle_hop[i].start()
+
+    gather.relay()
+    vec_step(2)
+
+    @pl.when(inner)
+    def _():
+        for i in range(CHUNKS):
+            rows = pl.ds(i * size, size)
+            middle_hop[i].wait_recv()
+            z_out[rows, :] = (z_mid[rows, :].astype(F32) + z_far[rows, :].astype(F32)).astype(BF16)
+            back[i].start()
+
+    vec_step(3)
+    step = 32
+
+    def final_rows(which, t):
+        rows = pl.ds(pl.multiple_of(which * half + t * step, step), step)
+        input_grad[rows, :] = (branch_grad[rows, :] + gather.total(which, t * step, step)).astype(BF16)
+
+    gather.wait_first()
+    pl.loop(0, half // step)(functools.partial(final_rows, 0))
+    gather.wait_second()
+    pl.loop(0, half // step)(functools.partial(final_rows, 1))
+    vec_step(4)
+
+    @pl.when(jnp.logical_not(inner))
+    def _():
+        for i in range(CHUNKS):
+            first[i].wait_send()
+            back[i].wait_recv()
+
+    @pl.when(inner)
+    def _():
+        for i in range(CHUNKS):
+            middle_hop[i].wait_send()
+            back[i].wait_send()
+
+    qkv_total[...] = z_out[...]
+    w.finish()
+
+
+def finish(dq, dk, dv, xs, w_full, branch_grad, vec):
+    toks, width = branch_grad.shape
+    piece = w_full.shape[0] // 8
+    half = toks // 2
+    shape = jax.ShapeDtypeStruct
+    vm = pltpu.VMEM
+    line = vm((piece, 3 * width), BF16)
+    return pl.pallas_call(
+        finish_body,
+        name="finish",
+        out_shape=(shape((toks, width), BF16), shape((piece, 3 * width), BF16), shape(vec.shape, F32)),
+        in_specs=[VM] * 7,
+        out_specs=(VM,) * 3,
+        scratch_shapes=[
+            vm((4, toks, 3 * width // 4), BF16),
+            vm((4, toks, width), BF16), vm((4, half, width), BF16), vm((2, half, width), BF16),
+            vm((4, piece, 3 * width // 4), BF16), vm((4, piece, 3 * width // 4), BF16), vm((4, piece, 3 * width // 4), F32),
+            vm((4, piece, 3 * width // 4), BF16),
+            line, line, line, line, line,
+            vm(vec.shape, F32), vm((9,) + vec.shape, F32),
+            pltpu.SemaphoreType.DMA((64,)), pltpu.SemaphoreType.DMA((64,)), pltpu.SemaphoreType.DMA((8,)),
+        ],
+        compiler_params=pltpu.CompilerParams(collective_id=2, has_side_effects=True, vmem_limit_bytes=48 << 20),
+    )(dq, dk, dv, xs, w_full, branch_grad, vec)
+
+
+def local_tensor(tokens, segment_ids, qkv_weight, out_weight, up_weight, down_weight, proj_bias, hidden_bias, norm_gain, norm_shift, cotangent):
+    inputs = tokens[0]
+    toks, width = inputs.shape
+    scale = (width // HEADS) ** (-0.5)
+    own = lax.axis_index("fsdp")
+    chip = own // 2
+    ff = up_weight.shape[1] // 4
+    piece = up_weight.shape[0]
+
+    def for_chip(mask):
+        cols = lax.dynamic_slice_in_dim(up_weight, lax.bitwise_xor(chip, mask // 2) * ff, ff, axis=1)
+        return jnp.concatenate([cols, out_weight], axis=0)
+
+    got_x, got_y, got_d = (lax.ppermute(for_chip(m), "fsdp", [(i, i ^ m) for i in range(8)]) for m in (2, 4, 6))
+    queries, key_rows, value_rows, xs, w_full = project(inputs, qkv_weight, proj_bias)
+    attended, attended_low, lse = attn_fwd(scale, segment_ids, queries, key_rows, value_rows)
+    output, branch_grad, grad_heads, vec, down_part, upout_part = middle(
+        attended_low, inputs, cotangent[0], up_weight, out_weight, down_weight, got_x, got_y, got_d,
+        proj_bias, hidden_bias[None], norm_gain, norm_shift,
+    )
+    back_x, back_y, back_d = (
+        lax.ppermute(lax.dynamic_index_in_dim(upout_part, lax.bitwise_xor(chip, m // 2), keepdims=False), "fsdp", [(i, i ^ m) for i in range(8)])
+        for m in (2, 4, 6)
+    )
+    kept = lax.dynamic_index_in_dim(upout_part, chip, keepdims=False)
+    up_sum = jnp.zeros((piece, 4 * ff), BF16)
+    for m, block in ((0, kept), (2, back_x), (4, back_y), (6, back_d)):
+        up_sum = lax.dynamic_update_slice_in_dim(up_sum, block[0], lax.bitwise_xor(chip, m // 2) * ff, axis=1)
+    out_sum = sum(b[1].astype(F32) for b in (kept, back_x, back_y, back_d)).astype(BF16)
+    down_total, up_total, out_total = lax.psum((down_part, up_sum, out_sum), "rep")
+    query_grad, key_grad, value_grad = attn_bwd(scale, segment_ids, queries, key_rows, value_rows, grad_heads, attended, lse)
+    input_grad, qkv_total, vec_total = finish(query_grad, key_grad, value_grad, xs, w_full, branch_grad, vec)
+    grad_scale = (toks * lax.axis_size("fsdp") * lax.axis_size("rep")) ** (-0.5)
+    scaled = vec_total * grad_scale
+    return (
+        output[None],
+        input_grad[None],
+        qkv_total.astype(F32) * grad_scale,
+        out_total.astype(F32) * grad_scale,
+        up_total.astype(F32) * grad_scale,
+        down_total.astype(F32) * grad_scale,
+        scaled[0:4],
+        scaled[8:12].reshape(4 * width),
+        scaled[4:6],
+        scaled[6:8],
+    )
 
 
 def normalize(hidden, gain, shift):
@@ -431,105 +1171,9 @@
     )
 
 
-def exchange(rows, parts):
-    count, width = rows.shape
-    split = jnp.transpose(rows.reshape(count, parts, width // parts), (1, 0, 2))
-    return lax.all_to_all(split, "fsdp", 0, 0).reshape(parts * count, width // parts)
-
-
-def exchange_back(rows, parts):
-    count, width = rows.shape
-    got = lax.all_to_all(rows.reshape(parts, count // parts, width), "fsdp", 0, 0)
-    return jnp.transpose(got, (1, 0, 2)).reshape(count // parts, parts * width)
-
-
-def local_tensor(tokens, segment_ids, qkv_weight, out_weight, up_weight, down_weight, proj_bias, hidden_bias, norm_gain, norm_shift, cotangent):
-    f32, bf16 = jnp.float32, jnp.bfloat16
-    inputs = tokens[0]
-    tok_count, model_width = inputs.shape
-    parts = lax.axis_size("fsdp")
-    own = lax.axis_index("fsdp")
-    head_dim = model_width // HEADS
-    scale = head_dim ** (-0.5)
-    width = model_width // parts
-    ff = hidden_bias.shape[0] // parts
-
-    def dot(spec, a, b):
-        return jnp.einsum(spec, a, b, preferred_element_type=f32)
-
-    def mine(vector, size):
-        return lax.dynamic_slice_in_dim(vector, own * size, size)
-
-    tokens_all = lax.all_gather(inputs, "fsdp", axis=0, tiled=True)
-    weight_pieces = [exchange(qkv_weight[:, i * model_width : (i + 1) * model_width], parts) for i in range(3)]
-    queries = (dot("td,de->te", tokens_all, weight_pieces[0]) + mine(proj_bias[0], width)).astype(bf16)
-    key_rows = dot("td,de->te", tokens_all, weight_pieces[1]).astype(bf16)
-    value_rows = (dot("td,de->te", tokens_all, weight_pieces[2]) + mine(proj_bias[1], width)).astype(bf16)
-    attended, attended_low_heads, lse = attn_fwd(scale, segment_ids, queries, key_rows, value_rows)
-    attended_low = exchange_back(attended_low_heads, parts)
-    out_full = lax.all_gather(out_weight, "fsdp", axis=0, tiled=True)
-    branch = dot("te,ed->td", attended_low, out_full) + proj_bias[2]
-    first_norm, norm_one_back = jax.vjp(normalize, inputs.astype(f32) + branch, norm_gain[0], norm_shift[0])
-    first_low = first_norm.astype(bf16)
-    up_mine = exchange(up_weight, parts)
-    first_all = lax.all_gather(first_low, "fsdp", axis=0, tiled=True)
-    hidden_pre = dot("td,df->tf", first_all, up_mine) + mine(hidden_bias, ff)
-    activated, gelu_back = jax.vjp(exact_gelu, hidden_pre)
-    activated_low = activated.astype(bf16)
-    second = lax.psum_scatter(dot("tf,fd->td", activated_low, down_weight).astype(bf16), "fsdp", scatter_dimension=0, tiled=True).astype(f32) + proj_bias[3]
-    output, norm_two_back = jax.vjp(normalize, first_norm + second, norm_gain[1], norm_shift[1])
-    grad_second, gain_two, shift_two = norm_two_back(cotangent[0].astype(f32))
-    second_low = grad_second.astype(bf16)
-    second_all = lax.all_gather(second_low, "fsdp", axis=0, tiled=True)
-    (pre_grad,) = gelu_back(dot("td,fd->tf", second_all, down_weight))
-    pre_low = pre_grad.astype(bf16)
-    down_sum = dot("tf,td->fd", activated_low, second_all)
-    first_grad = grad_second + lax.psum_scatter(dot("tf,df->td", pre_low, up_mine).astype(bf16), "fsdp", scatter_dimension=0, tiled=True).astype(f32)
-    up_cols = dot("td,tf->df", first_all, pre_low)
-    up_sum = exchange_back(up_cols.astype(bf16), parts)
-    branch_grad, gain_one, shift_one = norm_one_back(first_grad)
-    branch_low = branch_grad.astype(bf16)
-    attended_grad = dot("td,ed->te", branch_low, out_full).astype(bf16)
-    grad_heads = exchange(attended_grad, parts)
-    out_term = dot("te,td->ed", attended_low, branch_low)
-    out_sum = lax.psum_scatter(out_term.astype(bf16), "fsdp", scatter_dimension=0, tiled=True)
-    up_total, down_total, out_total = lax.psum((up_sum, down_sum.astype(bf16), out_sum), "rep")
-    query_grad, key_grad, value_grad = attn_bwd(scale, segment_ids, queries, key_rows, value_rows, grad_heads, attended, lse)
-    partial_input = dot("te,de->td", query_grad, weight_pieces[0]) + dot("te,de->td", key_grad, weight_pieces[1]) + dot("te,de->td", value_grad, weight_pieces[2])
-    input_grad = branch_grad + lax.psum_scatter(partial_input.astype(bf16), "fsdp", scatter_dimension=0, tiled=True).astype(f32)
-    qkv_sum = jnp.concatenate([exchange_back(dot("td,te->de", tokens_all, g).astype(bf16), parts) for g in (query_grad, key_grad, value_grad)], axis=1)
-    qkv_total = lax.psum(qkv_sum, "rep")
-
-    def placed(vector):
-        return lax.dynamic_update_slice_in_dim(jnp.zeros((vector.shape[0] * parts,), f32), vector, own * vector.shape[0], 0)
-
-    bias_term = jnp.stack([
-        placed(jnp.sum(query_grad.astype(f32), axis=0)),
-        placed(jnp.sum(value_grad.astype(f32), axis=0)),
-        jnp.sum(branch_low.astype(f32), axis=0),
-        jnp.sum(second_low.astype(f32), axis=0),
-    ])
-    hidden_term = placed(jnp.sum(pre_low.astype(f32), axis=0))
-    bias_total, hidden_total, gain_total, shift_total = lax.psum(
-        (bias_term, hidden_term, jnp.stack([gain_one, gain_two]), jnp.stack([shift_one, shift_two])), ("rep", "fsdp")
-    )
-    grad_scale = (tok_count * parts * lax.axis_size("rep")) ** (-0.5)
-    return (
-        output.astype(bf16)[None],
-        input_grad.astype(bf16)[None],
-        qkv_total.astype(f32) * grad_scale,
-        out_total.astype(f32) * grad_scale,
-        up_total.astype(f32) * grad_scale,
-        down_total.astype(f32) * grad_scale,
-        bias_total * grad_scale,
-        hidden_total * grad_scale,
-        gain_total * grad_scale,
-        shift_total * grad_scale,
-    )
-
-
 def solution(mesh):
-    local = local_tensor if HEADS == 2 * mesh.shape["fsdp"] else local_gather
+    small = mesh.shape["fsdp"] == 8 and mesh.shape["rep"] == 4
+    local = local_tensor if small else local_gather
     return jax.shard_map(
         local,
         mesh=mesh,

time: 637 us -> 383 us (0.60); the launches traced: 630 us -> 383 us
  waiting for transfers between devices: 348 us -> 18.7 us
  Pallas kernels: 55.5 us -> 312 us
  matrix products: 68.4 us -> 0 us
  blocking collectives: 52.4 us -> 0 us
  starting transfers between devices: 39.4 us -> 7.99 us
  other arithmetic: 24.2 us -> 11.9 us
  local copies, waits for them, and re-layouts: 26.8 us -> 17.8 us
    pallas_call x0 -> x3, Pallas kernels: none -> 242 us  [the longest x1 104 us: middle(): pl.pallas_call(middle_body, name='middle', out_shape=(shape((toks, width)...]
    reduce_scatter x4 -> x0, waiting for transfers between devices: 149 us -> none  [the longest x1 51.5 us: local_tensor(): lax.psum_scatter(dot('tf,df->td', pre_low, up_mine).astype(bf16), 'fsdp',...]
    psum x1, waiting for transfers between devices: 69.3 us -> 0.01 us  [local_tensor(): lax.psum((down_part, up_sum, out_sum), 'rep')]
    all_gather x4 -> x0, waiting for transfers between devices: 68.5 us -> none  [the longest x1 36.6 us: local_tensor(): second_all = lax.all_gather(second_low, 'fsdp', axis=0, tiled=True)]
    dot_general x18 -> x0, matrix products: 68.4 us -> none  [dot(): return jnp.einsum(spec, a, b, preferred_element_type=f32)]
    all_to_all x10 -> x0, waiting for transfers between devices: 58.9 us -> none  [the longest x5 43 us: exchange(): lax.all_to_all(split, 'fsdp', 0, 0).reshape(parts * count, width // parts)]
    psum x1 -> x0, blocking collectives: 52.4 us -> none  [local_tensor(): lax.psum((bias_term, hidden_term, jnp.stack([gain_one, gain_two]), jnp.st...]
    all_to_all x10 -> x0, starting transfers between devices: 38.7 us -> none  [the longest x5 19.7 us: exchange(): lax.all_to_all(split, 'fsdp', 0, 0).reshape(parts * count, width // parts)]
  transfers between devices with their start and end apart: 19 -> 7, of which waited for: 15 -> 2; matrix products, arithmetic and copies ran while one was open for 9% -> 2% of each run, Pallas kernels for 9% -> 54%
where the time goes in v2:
time: 383 us
  Pallas kernels  312 us (81%)
  waiting for transfers between devices  18.7 us (5%)
  local copies, waits for them, and re-layouts  17.8 us (5%)
  between operations  14.3 us (4%)
  other arithmetic  11.9 us (3%)
  starting transfers between devices  7.99 us (2%)
    pallas_call x1, Pallas kernels, middle(): pl.pallas_call(middle_body, name='middle', out_shape=(shape((toks, width)...  104 us
    pallas_call x1, Pallas kernels, finish(): pl.pallas_call(finish_body, name='finish', out_shape=(shape((toks, width)...  86 us
    pallas_call x1, Pallas kernels, project(): pl.pallas_call(project_body, name='project', out_shape=(heads, heads, hea...  51.9 us
    pallas_call x1, Pallas kernels, attn_fwd(): pl.pallas_call(functools.partial(attn_fwd_body, scale), name='attn_fwd',...  35.6 us
    pallas_call x1, Pallas kernels, attn_bwd(): pl.pallas_call(functools.partial(attn_bwd_body, scale), name='attn_bwd',...  35 us
    ppermute x3, waiting for transfers between devices, local_tensor(): lax.ppermute(lax.dynamic_index_in_dim(upout_part, lax.bitwise_xor(chip, m...  18.7 us
  transfers between devices with their start and end apart: 7, of which 2 were waited for; matrix products, arithmetic and copies ran while one was open for 2% of the time, Pallas kernels for 54%

profile of v2, /device:TPU:0, one launch (start us, length us, event | category | flops | bytes accessed | tf_op | source)
XLA Modules:
  0.0 382.8 jit_solution(1201918706633577845)
XLA Ops:
  7.3 1.3 constant_dynamic-slice_fusion
  8.6 2.2 pad_maximum_fusion
  10.8 2.9 collective-permute-start
  13.7 1.5 collective-permute-start.1
  15.3 51.9 %project.1 = (bf16[2048,128]{1,0:T(8,128)(2,1)S(1)}, bf16[2048,128]{1,0:T(8,128)(2,1)S(1)}, bf16[2048,128]{1,0:T(8,128)(2,1)S(1)}, bf16[4,256,1024]{2,1,0:T(8,128)(2,1)S(1)}, bf16[1024,768]{1,0:T(8,128)(2,1)S(1)}) custom-call(bf16[256,1024]{1,0:T(8,128)(2,1)S(1)} %bitcast.53, bf16[128,3072]{1,0:T(8,128)(2,1)S(1)} %copy-done.3, f32[4,1024]{1,0:T(4,128)S(1)} %copy-done.6), custom_call_target="tpu_custom_call" | custom-call | tf_op jit(solution)/shard_map/project/pallas_call | solution.py:667
  67.2 35.6 %attn_fwd.1 = (f32[2048,128]{1,0:T(8,128)S(1)}, bf16[2048,128]{1,0:T(8,128)(2,1)S(1)}, f32[8,2048]{1,0:T(8,128)S(1)}) custom-call(s32[1,2048]{1,0:T(1,128)S(1)} %copy-done.12, s32[1,2048]{1,0:T(1,128)S(1)} %copy-done.12, bf16[2048,128]{1,0:T(8,128)(2,1)S(1)} %get-tuple-element.30.q_ref, bf16[2048,128]{1,0:T(8,128)(2,1)S(1)} %get-tuple-element.31.k_ref, ...), custom_call_target="tpu_custom_call" | custom-call | flops 2147483648 | bytes 1572864 | tf_op jit(solution)/shard_map/attn_fwd/pallas_call | solution.py:87
  102.8 0.8 copy-done.4
  103.6 1.0 copy-done.13
  104.6 103.6 %middle.1 = (bf16[256,1024]{1,0:T(8,128)(2,1)}, f32[256,1024]{1,0:T(8,128)}, bf16[2048,128]{1,0:T(8,128)(2,1)}, f32[16,1024]{1,0:T(8,128)}, bf16[512,1024]{1,0:T...) custom-call(bf16[2048,128]{1,0:T(8,128)(2,1)} %copy-done.4, bf16[256,1024]{1,0:T(8,128)(2,1)} %bitcast.52, ...), custom_call_target="tpu_custom_call" | custom-call | tf_op jit(solution)/shard_map/middle/pallas_call | solution.py:571
  208.2 2.3 dynamic-slice_bitcast_fusion.2
  210.5 0.8 collective-permute-start.3
  211.3 0.8 collective-permute-start.4
  212.0 1.9 collective-permute-start.5
  214.0 1.1 broadcast_in_dim.15
  215.0 1.7 fusion.4
  216.7 8.6 %collective-permute-done.3 = bf16[2,128,1024]{2,1,0:T(8,128)(2,1)} collective-permute-done((bf16[2,128,1024]{2,1,0:T(8,128)(2,1)S(1)}, bf16[2,128,1024]{2,1,0:T(8,128)(2,1)}, u32[]{:S(2)}, u32[]{:S(2)}) %collective-permute-start.3) | collective-permute-done | bytes 524320 | tf_op jit(solution)/shard_map/ppermute | solution.py:894
  225.3 1.7 fusion.3
  227.0 10.1 %collective-permute-done.4 = bf16[2,128,1024]{2,1,0:T(8,128)(2,1)} collective-permute-done((bf16[2,128,1024]{2,1,0:T(8,128)(2,1)S(1)}, bf16[2,128,1024]{2,1,0:T(8,128)(2,1)}, u32[]{:S(2)}, u32[]{:S(2)}) %collective-permute-start.4) | collective-permute-done | bytes 524320 | tf_op jit(solution)/shard_map/ppermute | solution.py:894
  237.1 1.7 fusion.2
  238.8 2.1 fusion
  240.8 0.7 fusion.1
  241.6 1.0 copy-done.11
  242.6 1.2 copy-done.14
  243.9 35.0 %attn_bwd.1 = (bf16[2,4,256,128]{3,2,1,0:T(8,128)(2,1)S(1)}, bf16[2,4,256,128]{3,2,1,0:T(8,128)(2,1)S(1)}, bf16[2,4,256,128]{3,2,1,0:T(8,128)(2,1)S(1)}) custom-call(s32[1,2048]{1,0:T(1,128)S(1)} %copy-done.12, s32[1,2048]{1,0:T(1,128)S(1)} %copy-done.12, bf16[2048,128]{1,0:T(8,128)(2,1)S(1)} %get-tuple-element.30.q_ref, bf16[2048,128]{1,0:T(8,128)(2,1)S(1)} %copy-done.8, ...), custom_call_target="tpu_custom_call" | custom-call | flops 5368709120 | bytes 3670016 | tf_op jit(solution)/shard_map/attn_bwd/pallas_call | solution.py:164
  278.9 86.0 %finish.1 = (bf16[256,1024]{1,0:T(8,128)(2,1)S(1)}, bf16[128,3072]{1,0:T(8,128)(2,1)S(1)}, f32[16,1024]{1,0:T(8,128)S(1)}) custom-call(bf16[2,4,256,128]{3,2,1,0:T(8,128)(2,1)S(1)} %get-tuple-element.38.dq, bf16[2,4,256,128]{3,2,1,0:T(8,128)(2,1)S(1)} %get-tuple-element.39.dk, bf16[2,4,256,128]{3,2,1,0:T(8,128)(2,1)S(1)} %get-tuple-element.40.dv, ...), custom_call_target="tpu_custom_call" | custom-call | tf_op jit(solution)/shard_map/finish/pallas_call | solution.py:854
  365.0 0.6 slice_bitcast_fusion.6
  366.8 1.3 convert_multiply_fusion.2
  368.1 1.9 convert_multiply_fusion.3
  370.0 2.8 convert_multiply_fusion.1
  372.8 1.6 convert_multiply_fusion
  374.4 0.8 copy.33
  375.2 0.8 copy.34
  (41 shorter events, 1.4 us)
Async XLA Ops:
  7.2 360.9 %all-reduce.3.cloned.1.call-start = ((), (), s32[]{:S(2)}) async-start(), calls=%async_computation | async-start | bytes 4718592 | tf_op jit(solution)/shard_map/psum | solution.py:902
  7.3 8.0 %copy-start.1 = (bf16[1,256,1024]{2,1,0:T(8,128)(2,1)S(1)}, bf16[1,256,1024]{2,1,0:T(8,128)(2,1)}, u32[]{:S(2)}) copy-start(bf16[1,256,1024]{2,1,0:T(8,128)(2,1)} %param.11) | copy-start | bytes 1572868
  7.3 8.0 %copy-start.3 = (bf16[128,3072]{1,0:T(8,128)(2,1)S(1)}, bf16[128,3072]{1,0:T(8,128)(2,1)}, u32[]{:S(2)}) copy-start(bf16[128,3072]{1,0:T(8,128)(2,1)} %qkv_w.1) | copy-start | bytes 2359300
  7.3 8.0 %copy-start.6 = (f32[4,1024]{1,0:T(4,128)S(1)}, f32[4,1024]{1,0:T(4,128)}, u32[]{:S(2)}) copy-start(f32[4,1024]{1,0:T(4,128)} %proj_bias.3) | copy-start | bytes 49156
  8.6 58.6 %copy-start.12 = (s32[1,2048]{1,0:T(1,128)S(1)}, s32[1,2048]{1,0:T(1,128)}, u32[]{:S(2)}) copy-start(s32[1,2048]{1,0:T(1,128)} %seg_v.3) | copy-start | bytes 24580
  10.8 93.8 %collective-permute-start = (bf16[256,1024]{1,0:T(8,128)(2,1)}, bf16[256,1024]{1,0:T(8,128)(2,1)}, u32[]{:S(2)}, u32[]{:S(2)}) collective-permute-start(bf16[256,1024]{1,0:T(8,128)(2,1)} %get-tuple-element.61), channel_id=1, source_target_pairs={{0,2},{1,3},{2,0},{3,1},{4,6},{5,7},{6,4},{7,5},{8,10},{9,11},{10,... | collective-permute-start | bytes 1572872 | tf_op jit(solution)/shard_map/ppermute | solution.py:886
  13.7 90.8 %collective-permute-start.1 = (bf16[256,1024]{1,0:T(8,128)(2,1)}, bf16[256,1024]{1,0:T(8,128)(2,1)}, u32[]{:S(2)}, u32[]{:S(2)}) collective-permute-start(bf16[256,1024]{1,0:T(8,128)(2,1)} %get-tuple-element.60), channel_id=1, source_target_pairs={{0,4},{1,5},{2,6},{3,7},{4,0},{5,1},{6,2},{7,3},{8,12},{9,13},{10,... | collective-permute-start | bytes 1572872 | tf_op jit(solution)/shard_map/ppermute | solution.py:886
  15.3 89.3 %collective-permute-start.2 = (bf16[256,1024]{1,0:T(8,128)(2,1)}, bf16[256,1024]{1,0:T(8,128)(2,1)}, u32[]{:S(2)}, u32[]{:S(2)}) collective-permute-start(bf16[256,1024]{1,0:T(8,128)(2,1)} %get-tuple-element.59), channel_id=1, source_target_pairs={{0,6},{1,7},{2,4},{3,5},{4,2},{5,3},{6,0},{7,1},{8,14},{9,15},{10,... | collective-permute-start | bytes 1572872 | tf_op jit(solution)/shard_map/ppermute | solution.py:886
  67.2 35.6 %copy-start = (bf16[4,256,1024]{2,1,0:T(8,128)(2,1)}, bf16[4,256,1024]{2,1,0:T(8,128)(2,1)S(1)}, u32[]{:S(2)}) copy-start(bf16[4,256,1024]{2,1,0:T(8,128)(2,1)S(1)} %get-tuple-element.41.xs) | copy-start | bytes 6291460
  67.2 35.6 %copy-start.7 = (bf16[2048,128]{1,0:T(8,128)(2,1)}, bf16[2048,128]{1,0:T(8,128)(2,1)S(1)}, u32[]{:S(2)}) copy-start(bf16[2048,128]{1,0:T(8,128)(2,1)S(1)} %get-tuple-element.31.k_ref) | copy-start | bytes 1572868
  67.2 35.6 %copy-start.9 = (bf16[2048,128]{1,0:T(8,128)(2,1)}, bf16[2048,128]{1,0:T(8,128)(2,1)S(1)}, u32[]{:S(2)}) copy-start(bf16[2048,128]{1,0:T(8,128)(2,1)S(1)} %get-tuple-element.32.v_ref) | copy-start | bytes 1572868
  102.8 0.8 copy-start.4
  103.6 1.0 copy-start.13
  210.5 14.9 %collective-permute-start.3 = (bf16[2,128,1024]{2,1,0:T(8,128)(2,1)S(1)}, bf16[2,128,1024]{2,1,0:T(8,128)(2,1)}, u32[]{:S(2)}, u32[]{:S(2)}) collective-permute-start(bf16[2,128,1024]{2,1,0:T(8,128)(2,1)S(1)} %get-tuple-element.53), channel_id=1, source_target_pairs={{0,2},{1,3},{2,0},{3,1},{4,6},{5,7},{6,4},{7,5},{8,10},{9,11},{10,... | collective-permute-start | bytes 1572872 | tf_op jit(solution)/shard_map/ppermute | solution.py:894
  211.3 25.8 %collective-permute-start.4 = (bf16[2,128,1024]{2,1,0:T(8,128)(2,1)S(1)}, bf16[2,128,1024]{2,1,0:T(8,128)(2,1)}, u32[]{:S(2)}, u32[]{:S(2)}) collective-permute-start(bf16[2,128,1024]{2,1,0:T(8,128)(2,1)S(1)} %get-tuple-element.55), channel_id=1, source_target_pairs={{0,4},{1,5},{2,6},{3,7},{4,0},{5,1},{6,2},{7,3},{8,12},{9,13},{10,... | collective-permute-start | bytes 1572872 | tf_op jit(solution)/shard_map/ppermute | solution.py:894
  212.0 26.7 %collective-permute-start.5 = (bf16[2,128,1024]{2,1,0:T(8,128)(2,1)}, bf16[2,128,1024]{2,1,0:T(8,128)(2,1)S(1)}, u32[]{:S(2)}, u32[]{:S(2)}) collective-permute-start(bf16[2,128,1024]{2,1,0:T(8,128)(2,1)} %get-tuple-element.54), channel_id=1, source_target_pairs={{0,6},{1,7},{2,4},{3,5},{4,2},{5,3},{6,0},{7,1},{8,14},{9,15},{10,... | collective-permute-start | bytes 1572872 | tf_op jit(solution)/shard_map/ppermute | solution.py:894
  238.7 2.8 copy-start.8
  238.8 2.8 copy-start.10
  241.6 1.0 copy-start.11
  242.6 1.2 copy-start.14
  243.9 35.0 %copy-start.2 = (f32[256,1024]{1,0:T(8,128)S(1)}, f32[256,1024]{1,0:T(8,128)}, u32[]{:S(2)}) copy-start(f32[256,1024]{1,0:T(8,128)} %get-tuple-element.43.branch_grad) | copy-start | bytes 3145732
  243.9 35.0 %copy-start.5 = (f32[16,1024]{1,0:T(8,128)S(1)}, f32[16,1024]{1,0:T(8,128)}, u32[]{:S(2)}) copy-start(f32[16,1024]{1,0:T(8,128)} %get-tuple-element.44.vec) | copy-start | bytes 196612
  368.1 4.7 %copy-start.15 = (bf16[512,1024]{1,0:T(8,128)(2,1)S(1)}, bf16[512,1024]{1,0:T(8,128)(2,1)}, u32[]{:S(2)}) copy-start(bf16[512,1024]{1,0:T(8,128)(2,1)} %get-tuple-element.52) | copy-start | bytes 3145732
  372.8 1.6 copy-start.16
Sparse Core Ops, SparseCore 0:
  241.7 111.6 all-reduce.2

commit v3 on v2

--- a/solution.py
+++ b/solution.py
@@ -12,6 +12,7 @@
 
 NEGATIVE = -1e30
 BQ = 256
+BK = 512
 VM = pl.BlockSpec(memory_space=pltpu.VMEM)
 SM = pl.BlockSpec(memory_space=pltpu.SMEM)
 
@@ -24,9 +25,9 @@
     return jnp.dot(a, b, preferred_element_type=jnp.float32)
 
 
-def block_range(seg_s, blk, i, n):
-    first = seg_s[0, i * blk]
-    last = seg_s[0, i * blk + blk - 1]
+def block_range(seg_s, start, size, blk, n):
+    first = seg_s[0, start]
+    last = seg_s[0, start + size - 1]
     lo = jnp.int32(0)
     hi = jnp.int32(0)
     for j in range(n):
@@ -39,47 +40,99 @@
     return lax.broadcasted_iota(jnp.int32, shape, 1) < half
 
 
-def attn_fwd_body(scale, seg_s, seg_v, q_ref, k_ref, v_ref, o_ref, a_ref, lse_ref):
+def rows_of(index, size):
+    return pl.ds(pl.multiple_of(index * size, size), size)
+
+
+def seg_columns(seg_v, seg_c):
+    length = seg_c.shape[0]
+
+    @pl.loop(0, length // BQ)
+    def _(i):
+        rows = rows_of(i, BQ)
+        seg_c[rows, :] = jnp.transpose(jnp.broadcast_to(seg_v[:, rows].astype(jnp.float32), (128, BQ)))
+
+
+def wide(column, lanes):
+    return jnp.concatenate([column] * (lanes // 128), axis=1)
+
+
+def attn_fwd_body(scale, seg_s, seg_v, q_ref, k_ref, v_ref, o_ref, a_ref, lse_ref, vt, seg_c):
     length, width = q_ref.shape
     half = width // 2
     n = length // BQ
     first = head_lanes((BQ, width), half)
+    seg_columns(seg_v, seg_c)
 
     @pl.loop(0, n)
     def _(i):
-        lo, hi = block_range(seg_s, BQ, i, n)
-        rows = pl.ds(pl.multiple_of(i * BQ, BQ), BQ)
+        rows = rows_of(i, BQ)
+        t = jnp.transpose(v_ref[rows, :])
+        for h in range(2):
+            vt[h, 0:half, rows] = t[h * half : (h + 1) * half]
+            vt[h, half : half + 16, rows] = jnp.ones((16, BQ), jnp.bfloat16)
+
+    sides = []
+    heads = (lax.broadcasted_iota(jnp.int32, (16, width), 1) < half) == (lax.broadcasted_iota(jnp.int32, (16, width), 0) < 8)
+    heads = heads.astype(jnp.float32).astype(jnp.bfloat16)
+    for ref in (q_ref, k_ref):
+        squares = nt(heads, ref[...] * ref[...])
+        sides.append((jnp.max(squares[0:8]), jnp.max(squares[8:16])))
+    bound = (40.0 / scale) ** 2
+    small = jnp.logical_and(sides[0][0] * sides[1][0] <= bound, sides[0][1] * sides[1][1] <= bound)
+
+    @pl.loop(0, n)
+    def _(i):
+        lo, hi = block_range(seg_s, i * BQ, BQ, BK, length // BK)
+        rows = rows_of(i, BQ)
         q = q_ref[rows, :] * jnp.bfloat16(scale)
         zero = jnp.zeros_like(q)
         qs = (jnp.where(first, q, zero), jnp.where(first, zero, q))
-        seg_row = seg_v[:, rows].astype(jnp.float32)
-        seg_col = jnp.transpose(jnp.broadcast_to(seg_row, (128, BQ)))
-        seg_col = jnp.concatenate([seg_col] * (BQ // 128), axis=1)
-
-        def step(j, state):
-            cols = pl.ds(pl.multiple_of(j * BQ, BQ), BQ)
-            kb = k_ref[cols, :]
-            vb = v_ref[cols, :]
-            same = seg_col == seg_v[:, cols].astype(jnp.float32)
-            out = []
+        seg_q = seg_v[:, rows].astype(jnp.float32)
+
+
+        def masked(cols, h):
+            same = wide(seg_c[cols, :], BQ) == seg_q
+            return jnp.where(same, nt(k_ref[cols, :], qs[h]), NEGATIVE)
+
+        def store(tops, accs):
+            o = []
             for h in range(2):
-                m, l, acc = state[h]
-                s = jnp.where(same, nt(qs[h], kb), NEGATIVE)
-                top = jnp.maximum(m, jnp.max(s, axis=1, keepdims=True))
-                p = jnp.exp(s - top)
-                factor = jnp.exp(m - top)
-                l = l * factor + jnp.sum(p, axis=1, keepdims=True)
-                acc = acc * factor + nn(p.astype(jnp.bfloat16), vb)
-                out.append((top, l, acc))
-            return tuple(out)
-
-        one = (jnp.full((BQ, 1), NEGATIVE, jnp.float32), jnp.zeros((BQ, 1), jnp.float32), jnp.zeros((BQ, width), jnp.float32))
-        (m0, l0, acc0), (m1, l1, acc1) = lax.fori_loop(lo, hi, step, (one, one))
-        o = jnp.where(first, acc0 / l0, acc1 / l1)
-        o_ref[rows, :] = o
-        a_ref[rows, :] = o.astype(jnp.bfloat16)
-        lse_ref[0:1, rows] = jnp.transpose(jnp.broadcast_to(m0 + jnp.log(l0), (BQ, 128)))[0:1, :]
-        lse_ref[1:2, rows] = jnp.transpose(jnp.broadcast_to(m1 + jnp.log(l1), (BQ, 128)))[0:1, :]
+                total = accs[h][half : half + 1]
+                o.append(accs[h][0:half] / total)
+                lse_ref[h : h + 1, rows] = tops[h] + jnp.log(total)
+            o = jnp.transpose(jnp.concatenate(o, axis=0))
+            o_ref[rows, :] = o
+            a_ref[rows, :] = o.astype(jnp.bfloat16)
+
+        def direct(count):
+            base = jnp.minimum(lo, length // BK - count)
+            accs = [jnp.zeros((half + 16, BQ), jnp.float32)] * 2
+            for j in range(count):
+                cols = rows_of(base + j, BK)
+                for h in range(2):
+                    accs[h] = accs[h] + nn(vt[h, :, cols], jnp.exp(masked(cols, h)).astype(jnp.bfloat16))
+            store([jnp.zeros((1, BQ), jnp.float32)] * 2, accs)
+
+        def running():
+            def step(j, state):
+                cols = rows_of(j, BK)
+                out = []
+                for h in range(2):
+                    m, acc = state[h]
+                    s = masked(cols, h)
+                    top = jnp.maximum(m, jnp.max(s, axis=0, keepdims=True))
+                    p = jnp.exp(s - top).astype(jnp.bfloat16)
+                    out.append((top, acc * jnp.exp(m - top) + nn(vt[h, :, cols], p)))
+                return tuple(out)
+
+            one = (jnp.full((1, BQ), NEGATIVE, jnp.float32), jnp.zeros((half + 16, BQ), jnp.float32))
+            state = lax.fori_loop(lo, hi, step, (one, one))
+            store([state[h][0] for h in range(2)], [state[h][1] for h in range(2)])
+
+        for count in range(1, length // BK + 1):
+            pl.when(jnp.logical_and(small, hi - lo == count))(functools.partial(direct, count))
+        pl.when(jnp.logical_not(small))(running)
 
 
 def attn_fwd(scale, seg, q, k, v):
@@ -94,69 +147,76 @@
         ),
         in_specs=[SM, VM, VM, VM, VM],
         out_specs=(VM, VM, VM),
+        scratch_shapes=[pltpu.VMEM((2, width // 2 + 16, length), jnp.bfloat16), pltpu.VMEM((length, 128), jnp.float32)],
         compiler_params=pltpu.CompilerParams(vmem_limit_bytes=32 << 20),
         cost_estimate=pl.CostEstimate(flops=4 * length * length * width, bytes_accessed=6 * length * width, transcendentals=2 * length * length),
     )(seg, seg, q, k, v)
 
 
-def attn_bwd_body(scale, seg_s, seg_v, q_ref, k_ref, v_ref, g_ref, o_ref, lse_ref, dq_ref, dk_ref, dv_ref, corr, dqt, dk_acc, dv_acc):
+def attn_bwd_body(scale, seg_s, seg_v, q_ref, k_ref, v_ref, g_ref, o_ref, lse_ref, dq_ref, dk_ref, dv_ref, corr, kt, dk_acc, dv_acc, dqt, seg_c):
     length, width = q_ref.shape
     half = width // 2
     n = length // BQ
     first = head_lanes((BQ, width), half)
+    seg_columns(seg_v, seg_c)
 
     @pl.loop(0, n)
     def _(i):
-        rows = pl.ds(pl.multiple_of(i * BQ, BQ), BQ)
+        rows = rows_of(i, BQ)
         prod = jnp.transpose(g_ref[rows, :].astype(jnp.float32) * o_ref[rows, :])
         corr[0:1, rows] = jnp.sum(prod[:half], axis=0, keepdims=True)
         corr[1:2, rows] = jnp.sum(prod[half:], axis=0, keepdims=True)
-        dqt[:, rows] = jnp.zeros((width, BQ), jnp.float32)
+        kt[:, rows] = jnp.transpose(k_ref[rows, :])
+        dk_acc[rows, :] = jnp.zeros((BQ, width), jnp.float32)
+        dv_acc[rows, :] = jnp.zeros((BQ, width), jnp.float32)
 
     @pl.loop(0, n)
-    def _(j):
-        lo, hi = block_range(seg_s, BQ, j, n)
-        rows = pl.ds(pl.multiple_of(j * BQ, BQ), BQ)
-        kb = k_ref[rows, :]
-        vb = v_ref[rows, :]
-        zero = jnp.zeros_like(kb)
-        ks = (jnp.where(first, kb, zero), jnp.where(first, zero, kb))
-        vs = (jnp.where(first, vb, zero), jnp.where(first, zero, vb))
-        kt = jnp.transpose(kb)
-        seg_row = seg_v[:, rows].astype(jnp.float32)
-        seg_col = jnp.transpose(jnp.broadcast_to(seg_row, (128, BQ)))
-        seg_col = jnp.concatenate([seg_col] * (BQ // 128), axis=1)
-        dk_acc[...] = jnp.zeros_like(dk_acc)
-        dv_acc[...] = jnp.zeros_like(dv_acc)
-
-        def step(i, _):
-            cols = pl.ds(pl.multiple_of(i * BQ, BQ), BQ)
-            qb = q_ref[cols, :] * jnp.bfloat16(scale)
-            gb = g_ref[cols, :]
-            same = seg_col == seg_v[:, cols].astype(jnp.float32)
+    def _(i):
+        lo, hi = block_range(seg_s, i * BQ, BQ, BK, length // BK)
+        rows = rows_of(i, BQ)
+        qb = q_ref[rows, :] * jnp.bfloat16(scale)
+        gb = g_ref[rows, :]
+        zero = jnp.zeros_like(qb)
+        qs = (jnp.where(first, qb, zero), jnp.where(first, zero, qb))
+        gs = (jnp.where(first, gb, zero), jnp.where(first, zero, gb))
+        qz = jnp.concatenate(qs, axis=0)
+        gz = jnp.concatenate(gs, axis=0)
+        seg_q = seg_v[:, rows].astype(jnp.float32)
+
+        def term(cols, dq):
+            kb = k_ref[cols, :]
+            vb = v_ref[cols, :]
+            same = wide(seg_c[cols, :], BQ) == seg_q
             ps, ds = [], []
             for h in range(2):
-                s = jnp.where(same, nt(ks[h], qb), NEGATIVE)
-                p = jnp.exp(s - lse_ref[h : h + 1, cols])
-                dp = nt(vs[h], gb)
-                d = (p * (dp - corr[h : h + 1, cols])).astype(jnp.bfloat16)
+                s = jnp.where(same, nt(kb, qs[h]), NEGATIVE)
+                p = jnp.exp(s - lse_ref[h : h + 1, rows])
+                dp = nt(vb, gs[h])
+                d = (p * (dp - corr[h : h + 1, rows])).astype(jnp.bfloat16)
                 ps.append(p.astype(jnp.bfloat16))
                 ds.append(d)
-                dqt[h * half : (h + 1) * half, cols] += nn(kt[h * half : (h + 1) * half, :], d)
-            gz = jnp.concatenate([jnp.where(first, gb, zero), jnp.where(first, zero, gb)], axis=0)
-            qz = jnp.concatenate([jnp.where(first, qb, zero), jnp.where(first, zero, qb)], axis=0)
-            dv_acc[...] += nn(jnp.concatenate(ps, axis=1), gz)
-            dk_acc[...] += nn(jnp.concatenate(ds, axis=1), qz)
-            return 0
-
-        lax.fori_loop(lo, hi, step, 0)
-        dk_ref[lax.rem(j, 2), j // 2] = dk_acc[...].astype(jnp.bfloat16)
-        dv_ref[lax.rem(j, 2), j // 2] = dv_acc[...].astype(jnp.bfloat16)
+                dq[h] = dq[h] + nn(kt[h * half : (h + 1) * half, cols], d)
+            dv_acc[cols, :] += nn(jnp.concatenate(ps, axis=1), gz)
+            dk_acc[cols, :] += nn(jnp.concatenate(ds, axis=1), qz)
+            return dq
+
+        def run(count):
+            base = jnp.minimum(lo, length // BK - count)
+            dq = [jnp.zeros((half, BQ), jnp.float32)] * 2
+            for j in range(count):
+                dq = term(rows_of(base + j, BK), dq)
+            dqt[0:half, :] = dq[0]
+            dqt[half:, :] = dq[1]
+
+        for count in range(1, length // BK + 1):
+            pl.when(hi - lo == count)(functools.partial(run, count))
+        dq_ref[lax.rem(i, 2), i // 2] = (jnp.transpose(dqt[...]) * scale).astype(jnp.bfloat16)
 
     @pl.loop(0, n)
     def _(i):
-        rows = pl.ds(pl.multiple_of(i * BQ, BQ), BQ)
-        dq_ref[lax.rem(i, 2), i // 2] = (jnp.transpose(dqt[:, rows]) * scale).astype(jnp.bfloat16)
+        rows = rows_of(i, BQ)
+        dk_ref[lax.rem(i, 2), i // 2] = dk_acc[rows, :].astype(jnp.bfloat16)
+        dv_ref[lax.rem(i, 2), i // 2] = dv_acc[rows, :].astype(jnp.bfloat16)
 
 
 def attn_bwd(scale, seg, q, k, v, g, o, lse):
@@ -169,9 +229,11 @@
         out_specs=(VM, VM, VM),
         scratch_shapes=[
             pltpu.VMEM((8, length), jnp.float32),
-            pltpu.VMEM((width, length), jnp.float32),
-            pltpu.VMEM((BQ, width), jnp.float32),
-            pltpu.VMEM((BQ, width), jnp.float32),
+            pltpu.VMEM((width, length), jnp.bfloat16),
+            pltpu.VMEM((length, width), jnp.float32),
+            pltpu.VMEM((length, width), jnp.float32),
+            pltpu.VMEM((width, BQ), jnp.float32),
+            pltpu.VMEM((length, 128), jnp.float32),
         ],
         compiler_params=pltpu.CompilerParams(vmem_limit_bytes=32 << 20),
         cost_estimate=pl.CostEstimate(flops=10 * length * length * width, bytes_accessed=14 * length * width, transcendentals=2 * length * length),
@@ -179,7 +241,7 @@
 
 
 MESH = pl.DeviceIdType.MESH
-ANY = pl.BlockSpec(memory_space=pl.ANY)
+HBM = pl.BlockSpec(memory_space=pltpu.HBM)
 F32 = jnp.float32
 BF16 = jnp.bfloat16
 
@@ -232,8 +294,60 @@
             copy.wait_send()
 
 
-def rows_of(index, size):
-    return pl.ds(pl.multiple_of(index * size, size), size)
+class Line:
+    def __init__(self, wires, own, land, far, count):
+        self.own, self.land, self.far = own, land, far
+        rep, dev = wires.rep, wires.own
+        size = own.shape[0] // count
+        self.rows = [pl.ds(i * size, size) for i in range(count)]
+        self.inner = jnp.logical_or(rep == 1, rep == 2)
+        self.outer = jnp.logical_not(self.inner)
+        near, across = lax.bitwise_xor(rep, 1), lax.bitwise_xor(rep, 3)
+        self.first = [wires.remote(own.at[r], land.at[r], dev, near) for r in self.rows]
+        self.middle = [wires.remote(own.at[r], far.at[r], dev, across) for r in self.rows]
+        self.back = [wires.remote(land.at[r], land.at[r], dev, near) for r in self.rows]
+
+    def start(self):
+        @pl.when(self.outer)
+        def _():
+            for copy in self.first:
+                copy.start()
+
+    def collect(self, which):
+        @pl.when(self.inner)
+        def _():
+            for i in which:
+                r = self.rows[i]
+                self.first[i].wait_recv()
+                self.own[r, :] = (self.own[r, :].astype(F32) + self.land[r, :].astype(F32)).astype(BF16)
+                self.middle[i].start()
+
+    def total(self, which):
+        @pl.when(self.inner)
+        def _():
+            for i in which:
+                r = self.rows[i]
+                self.middle[i].wait_recv()
+                self.land[r, :] = (self.own[r, :].astype(F32) + self.far[r, :].astype(F32)).astype(BF16)
+                self.back[i].start()
+
+    def arrive(self, which):
+        @pl.when(self.outer)
+        def _():
+            for i in which:
+                self.back[i].wait_recv()
+
+    def finish(self):
+        @pl.when(self.outer)
+        def _():
+            for copy in self.first:
+                copy.wait_send()
+
+        @pl.when(self.inner)
+        def _():
+            for i in range(len(self.rows)):
+                self.middle[i].wait_send()
+                self.back[i].wait_send()
 
 
 class Spread:
@@ -323,10 +437,10 @@
 
 
 def middle_body(
-    heads, x, cot, up_w, out_w, down_w, got_x, got_y, got_d, proj_bias, hidden_bias, gain, shift,
-    output, branch_grad, grad_heads, vec, down_grad, upout_grad,
+    grad_scale, heads, x, cot, upout, down_w, proj_bias, hidden_bias, gain, shift,
+    output, branch_grad, grad_heads, vec, down_grad, keep, to_x, to_y, to_d,
     att, out_full, up_full, down_full, h1, z1, r1, gs, fl, act, slope, part, side, last, sl, pre, part2, side2, last2,
-    branch_low, agl, acc, d_send, d_recv, d_keep, u_send, u_recv, u_keep, o_send, o_recv, o_keep,
+    branch_low, agl, acc, d_send, d_recv, d_keep, d_own, d_land, d_far, u_send, u_recv, u_keep, o_send, o_recv, o_keep,
     send_sems, recv_sems, local_sems,
 ):
     w = Wires(send_sems, recv_sems, local_sems)
@@ -338,20 +452,18 @@
     ff = up_full.shape[1]
     head_width = heads.shape[1]
     half = toks // 2
-    piece = up_w.shape[0]
+    piece = upout.shape[2]
     tile = 256
-    w.greet([(w.rep, lax.bitwise_xor(own, m)) for m in range(1, 8)])
+    w.greet([(w.rep, lax.bitwise_xor(own, m)) for m in range(1, 8)] + [(lax.bitwise_xor(w.rep, m), own) for m in (1, 3)])
 
     swaps = []
     for m in (6, 2, 4, 1, 3, 5, 7):
         peer = lax.bitwise_xor(own, m)
         swaps.append(w.send(heads.at[rows_of(peer, toks)], att.at[:, rows_of(own, head_width)], peer))
     weights = []
-    for m, src in ((0, None), (2, got_x), (4, got_y), (6, got_d)):
-        dst = rows_of(lax.bitwise_xor(own, m), piece)
-        src_out = out_w if src is None else src.at[pl.ds(piece, piece)]
-        src_up = up_w.at[:, rows_of(chip, ff)] if src is None else src.at[pl.ds(0, piece)]
-        for s, full in ((src_out, out_full), (src_up, up_full)):
+    for k in range(4):
+        dst = rows_of(2 * k + core, piece)
+        for s, full in ((upout.at[k, 1], out_full), (upout.at[k, 0], up_full)):
             weights.append((w.local(s, full.at[dst]), w.send(s, full.at[dst], mate)))
     dst = rows_of(core, ff // 2)
     weights.append((w.local(down_w, down_full.at[dst]), w.send(down_w, down_full.at[dst], mate)))
@@ -391,9 +503,8 @@
         def _(n):
             cols = rows_of(n, tile)
             hidden = nn(fl[k], up_full[:, cols]) + hidden_bias[:, pl.ds(pl.multiple_of(chip * ff + n * tile, tile), tile)]
-            cdf = 0.5 * (1.0 + lax.erf(hidden * (2.0**-0.5)))
-            act[k, :, cols] = (hidden * cdf).astype(BF16)
-            slope[k, :, cols] = cdf + hidden * (jnp.exp(-0.5 * hidden * hidden) * ((2.0 * math.pi) ** -0.5))
+            slope[k, :, cols] = hidden
+            act[k, :, cols] = (hidden * (0.5 * (1.0 + lax.erf(hidden * (2.0**-0.5))))).astype(BF16)
 
         @pl.loop(0, width // tile)
         def _(n):
@@ -411,7 +522,20 @@
     spread.wait_diagonal()
     forward(cd)
     gather.send_diagonal()
+
+    def slopes(k):
+        @pl.loop(0, toks // 32)
+        def _(t):
+            rows = rows_of(t, 32)
+            hidden = slope[k, rows, :]
+            cdf = 0.5 * (1.0 + lax.erf(hidden * (2.0**-0.5)))
+            slope[k, rows, :] = cdf + hidden * (jnp.exp(-0.5 * hidden * hidden) * ((2.0 * math.pi) ** -0.5))
+
+    slopes(0)
+    slopes(1)
     gather.relay()
+    slopes(2)
+    slopes(3)
 
     def second_rows(which, t):
         rows = pl.ds(pl.multiple_of(which * half + t * step, step), step)
@@ -474,11 +598,21 @@
         d_send[rows_of(n, tile), :] = down_rows(1 - core, n).astype(BF16)
 
     d_copy = w.send(d_send, d_recv, mate)
-    gather2.relay()
 
     @pl.loop(0, ff // 2 // tile)
     def _(n):
         d_keep[rows_of(n, tile), :] = down_rows(core, n)
+
+    gather2.relay()
+    d_copy.wait_recv()
+
+    @pl.loop(0, ff // 2 // 64)
+    def _(t):
+        rows = rows_of(t, 64)
+        d_own[rows, :] = (d_keep[rows, :] + d_recv[rows, :].astype(F32)).astype(BF16)
+
+    line = Line(w, d_own, d_land, d_far, 8)
+    line.start()
 
     def up_rows(which, k):
         cols = pl.ds(pl.multiple_of((2 * k + which) * piece, piece), piece)
@@ -506,6 +640,7 @@
 
     gather2.wait_first()
     pl.loop(0, half // step)(functools.partial(branch_rows, 0))
+    line.collect((0, 1))
     gather2.wait_second()
     pl.loop(0, half // step)(functools.partial(branch_rows, 1))
 
@@ -519,6 +654,8 @@
         peer = lax.bitwise_xor(own, m)
         backs.append(w.send(agl.at[:, rows_of(peer, head_width)], grad_heads.at[rows_of(own, toks)], peer))
     grad_heads[rows_of(own, toks), :] = agl[:, rows_of(own, head_width)]
+    line.collect((2, 3))
+    line.total((0, 1))
 
     def out_rows(which, k):
         cols = pl.ds(pl.multiple_of((2 * k + which) * piece, piece), piece)
@@ -529,27 +666,24 @@
         o_send[k] = out_rows(1 - core, k).astype(BF16)
 
     o_copy = w.send(o_send, o_recv, mate)
+    line.collect((4,))
+    line.total((2,))
 
     @pl.loop(0, 4)
     def _(k):
         u_keep[k] = up_rows(core, k)
         o_keep[k] = out_rows(core, k)
 
-    d_copy.wait_recv()
-
-    @pl.loop(0, ff // 2 // 64)
-    def _(t):
-        rows = rows_of(t, 64)
-        down_grad[rows, :] = (d_keep[rows, :] + d_recv[rows, :].astype(F32)).astype(BF16)
-
+    line.collect((5,))
+    line.total((3,))
     u_copy.wait_recv()
     o_copy.wait_recv()
-
-    @pl.loop(0, 4)
-    def _(k):
-        upout_grad[k, 0] = (u_keep[k] + u_recv[k].astype(F32)).astype(BF16)
-        upout_grad[k, 1] = (o_keep[k] + o_recv[k].astype(F32)).astype(BF16)
-
+    for m, ref in enumerate((keep, to_x, to_y, to_d)):
+        k = lax.bitwise_xor(chip, m)
+        ref[0] = (u_keep[k] + u_recv[k].astype(F32)).astype(BF16)
+        ref[1] = (o_keep[k] + o_recv[k].astype(F32)).astype(BF16)
+    line.collect((6, 7))
+    line.total((4, 5, 6, 7))
     vec[...] = jnp.zeros_like(vec)
     for row, slot in ((2, 6), (3, 2), (4, 4), (5, 0), (6, 5), (7, 1)):
         vec[row : row + 1, :] = jnp.sum(acc[slot], axis=0, keepdims=True)
@@ -558,29 +692,34 @@
         vec[8 + k : 9 + k, :] = jnp.where(chip == k, hidden_sum, jnp.zeros_like(hidden_sum))
     for copy in backs:
         copy.wait_recv()
+    for i in range(8):
+        line.arrive((i,))
+        rows = line.rows[i]
+        down_grad[rows, :] = d_land[rows, :].astype(F32) * grad_scale
+    line.finish()
     w.finish()
 
 
-def middle(heads, x, cot, up_w, out_w, down_w, got_x, got_y, got_d, proj_bias, hidden_bias, gain, shift):
+def middle(grad_scale, heads, x, cot, upout, down_w, proj_bias, hidden_bias, gain, shift):
     toks, width = x.shape
-    ff = up_w.shape[1] // 4
-    piece = up_w.shape[0]
+    piece = upout.shape[2]
+    ff = 2 * down_w.shape[0]
     half = toks // 2
     shape = jax.ShapeDtypeStruct
     vm = pltpu.VMEM
     return pl.pallas_call(
-        middle_body,
+        functools.partial(middle_body, grad_scale),
         name="middle",
         out_shape=(
             shape((toks, width), BF16),
             shape((toks, width), F32),
             shape(heads.shape, BF16),
             shape((16, width), F32),
-            shape((ff // 2, width), BF16),
-            shape((4, 2, piece, width), BF16),
-        ),
-        in_specs=[VM, VM, VM] + [ANY] * 6 + [VM] * 4,
-        out_specs=(VM,) * 6,
+            shape((ff // 2, width), F32),
+        )
+        + (shape((2, piece, width), BF16),) * 4,
+        in_specs=[VM, VM, VM, HBM, HBM] + [VM] * 4,
+        out_specs=(VM,) * 9,
         scratch_shapes=[
             vm((toks, width), BF16), vm((width, width), BF16), vm((width, ff), BF16), vm((ff, width), BF16),
             vm((toks, width), F32), vm((toks, width), F32), vm((toks, 128), F32), vm((toks, width), F32),
@@ -590,15 +729,16 @@
             vm((4, toks, width), BF16), vm((4, half, width), BF16), vm((2, half, width), BF16),
             vm((toks, width), BF16), vm((toks, width), BF16), vm((8, 8, width), F32),
             vm((ff // 2, width), BF16), vm((ff // 2, width), BF16), vm((ff // 2, width), F32),
+            vm((ff // 2, width), BF16), vm((ff // 2, width), BF16), vm((ff // 2, width), BF16),
             vm((4, piece, ff), BF16), vm((4, piece, ff), BF16), vm((4, piece, ff), F32),
             vm((4, piece, width), BF16), vm((4, piece, width), BF16), vm((4, piece, width), F32),
-            pltpu.SemaphoreType.DMA((64,)), pltpu.SemaphoreType.DMA((64,)), pltpu.SemaphoreType.DMA((16,)),
+            pltpu.SemaphoreType.DMA((96,)), pltpu.SemaphoreType.DMA((96,)), pltpu.SemaphoreType.DMA((16,)),
         ],
         compiler_params=pltpu.CompilerParams(collective_id=1, has_side_effects=True, vmem_limit_bytes=60 << 20),
-    )(heads, x, cot, up_w, out_w, down_w, got_x, got_y, got_d, proj_bias, hidden_bias, gain, shift)
-
-
-def project_body(x, qkv_w, proj_bias, q_out, k_out, v_out, xs, w_full, stage, send_sems, recv_sems, local_sems):
+    )(heads, x, cot, upout, down_w, proj_bias, hidden_bias, gain, shift)
+
+
+def project_body(x, qkv_w, up_w, out_w, proj_bias, q_out, k_out, v_out, xs, w_full, upout, stage, send_sems, recv_sems, local_sems):
     w = Wires(send_sems, recv_sems, local_sems)
     own = w.own
     core, chip = lax.rem(own, 2), own // 2
@@ -607,8 +747,11 @@
     piece = qkv_w.shape[0]
     share = width // 4
     head_width = share // 2
-    w.greet([(w.rep, lax.bitwise_xor(own, m)) for m in (1, 2, 4, 6)])
+    rep = w.rep
+    reps = 4
+    w.greet([(rep, lax.bitwise_xor(own, m)) for m in (1, 2, 4, 6)] + [(lax.rem(rep + 1, reps), own), (lax.rem(rep + reps - 1, reps), own)])
     mine = rows_of(own, piece)
+    quarter = piece // reps
 
     def source(part, to_chip):
         return qkv_w.at[:, pl.ds(pl.multiple_of(part * width + to_chip * share, share), share)]
@@ -618,6 +761,44 @@
         peer = lax.bitwise_xor(own, m)
         copies = [w.send(source(p, lax.bitwise_xor(chip, m // 2)), w_full.at[mine, pl.ds(p * share, share)], peer) for p in range(3)]
         arrivals.append((peer, copies))
+    fetched = []
+    for m in (6, 2, 4):
+        peer, to_chip = lax.bitwise_xor(own, m), lax.bitwise_xor(chip, m // 2)
+        some = rows_of(rep, quarter)
+        fetched.append(w.send(up_w.at[some, rows_of(to_chip, width)], upout.at[chip, 0, some], peer))
+        fetched.append(w.send(out_w.at[some], upout.at[chip, 1, some], peer))
+    kept = [w.local(up_w.at[:, rows_of(chip, width)], upout.at[chip, 0]), w.local(out_w, upout.at[chip, 1])]
+    others = [lax.bitwise_xor(chip, m) for m in (3, 1, 2)]
+    hops = []
+    for hop in range(1, reps):
+        for step in (1, -1):
+            index = rep - step * (hop - 1)
+            to = rep + step
+            going = jnp.logical_and(jnp.logical_and(index >= 0, index < reps), jnp.logical_and(to >= 0, to < reps))
+            come = rep - step * hop
+            coming = jnp.logical_and(come >= 0, come < reps)
+            some = rows_of(jnp.clip(index, 0, reps - 1), quarter)
+            copies = [w.remote(upout.at[c, :, some], upout.at[c, :, some], own, jnp.clip(to, 0, reps - 1)) for c in others]
+            hops.append((hop, going, coming, copies))
+
+    def hop_start(which):
+        for hop, going, coming, copies in hops:
+            if hop == which:
+
+                @pl.when(going)
+                def _():
+                    for copy in copies:
+                        copy.start()
+
+    def hop_wait(which):
+        for hop, going, coming, copies in hops:
+            if hop == which:
+
+                @pl.when(coming)
+                def _():
+                    for copy in copies:
+                        copy.wait_recv()
+
     xs[chip] = x[...]
     spread = Spread(w, xs, toks // 2)
     spread.first_half()
@@ -646,19 +827,36 @@
             swaps.append(w.send(stage.at[k, :, pl.ds(pl.multiple_of(p * share + (1 - core) * head_width, head_width), head_width)], outs[p].at[rows], mate))
             outs[p][rows, :] = stage[k, :, pl.ds(pl.multiple_of(p * share + core * head_width, head_width), head_width)]
 
+    for copy in fetched:
+        copy.wait_recv()
+    hop_start(1)
     block(chip)
     spread.relay()
+    hop_wait(1)
+    hop_start(2)
     spread.wait_sides()
     block(spread.cx)
     block(spread.cy)
+    hop_wait(2)
+    hop_start(3)
     spread.wait_diagonal()
     block(spread.cd)
     for copy in swaps:
         copy.wait_recv()
+    hop_wait(3)
+    for copy in kept:
+        copy.wait()
+    for hop, going, coming, copies in hops:
+
+        @pl.when(going)
+        def _():
+            for copy in copies:
+                copy.wait_send()
+
     w.finish()
 
 
-def project(x, qkv_w, proj_bias):
+def project(x, qkv_w, up_w, out_w, proj_bias):
     toks, width = x.shape
     piece = qkv_w.shape[0]
     shape = jax.ShapeDtypeStruct
@@ -667,23 +865,24 @@
     return pl.pallas_call(
         project_body,
         name="project",
-        out_shape=(heads, heads, heads, shape((4, toks, width), BF16), shape((8 * piece, 3 * width // 4), BF16)),
-        in_specs=[VM] * 3,
-        out_specs=(VM,) * 5,
+        out_shape=(heads, heads, heads, shape((4, toks, width), BF16), shape((8 * piece, 3 * width // 4), BF16), shape((4, 2, piece, width), BF16)),
+        in_specs=[VM, VM, HBM, HBM, VM],
+        out_specs=(VM,) * 5 + (HBM,),
         scratch_shapes=[
             vm((4, toks, 3 * width // 4), BF16),
-            pltpu.SemaphoreType.DMA((48,)), pltpu.SemaphoreType.DMA((48,)), pltpu.SemaphoreType.DMA((8,)),
+            pltpu.SemaphoreType.DMA((72,)), pltpu.SemaphoreType.DMA((72,)), pltpu.SemaphoreType.DMA((8,)),
         ],
         compiler_params=pltpu.CompilerParams(collective_id=0, has_side_effects=True, vmem_limit_bytes=40 << 20),
-    )(x, qkv_w, proj_bias)
+    )(x, qkv_w, up_w, out_w, proj_bias)
 
 
 CHUNKS = 8
 
 
 def finish_body(
-    dq, dk, dv, xs, w_full, branch_grad, vec, input_grad, qkv_total, vec_total,
-    grads, part, side, last, q_send, q_recv, q_keep, q_piece, z_own, z_in, z_mid, z_far, z_out, v_sum, v_recv,
+    grad_scale, dq, dk, dv, xs, w_full, branch_grad, vec, keep, got_x, got_y, got_d,
+    input_grad, qkv_total, out_total, up_total, bias_total, hidden_total, gain_total, shift_total,
+    grads, part, side, last, q_send, q_recv, q_keep, q_piece, z_own, z_in, z_far, y_own, y_in, y_far, v_sum, v_recv,
     send_sems, recv_sems, local_sems,
 ):
     w = Wires(send_sems, recv_sems, local_sems)
@@ -699,6 +898,11 @@
     z1, z2, z3 = (lax.bitwise_xor(rep, m) for m in (1, 2, 3))
     w.greet([(rep, lax.bitwise_xor(own, m)) for m in (1, 2, 4, 6)] + [(z1, own), (z2, own), (z3, own)])
 
+    for m, ref in enumerate((keep, got_x, got_y, got_d)):
+        y_own[m * piece : (m + 1) * piece, :] = ref[0]
+    y_own[4 * piece :, :] = (keep[1].astype(F32) + got_x[1].astype(F32) + got_y[1].astype(F32) + got_d[1].astype(F32)).astype(BF16)
+    early = Line(w, y_own, y_in, y_far, 10)
+    early.start()
     swaps = []
     for p, g in enumerate((dq, dk, dv)):
         cols = pl.ds(pl.multiple_of(p * share + core * head_width, head_width), head_width)
@@ -724,7 +928,12 @@
             v_recv[5 + i] = base + v_recv[i]
             vec_start(i + 1)
         else:
-            vec_total[...] = base + v_recv[i]
+            final = (base + v_recv[i]) * grad_scale
+            bias_total[...] = final[0:4]
+            gain_total[...] = final[4:6]
+            shift_total[...] = final[6:8]
+            for k in range(4):
+                hidden_total[:, k * width : (k + 1) * width] = final[8 + k : 9 + k]
 
     vec_start(0)
     for copy in swaps:
@@ -739,11 +948,13 @@
         q_send[k] = qkv_rows(1 - core, k).astype(BF16)
 
     q_copy = w.send(q_send, q_recv, mate)
+    early.collect((0,))
 
     @pl.loop(0, 4)
     def _(k):
         q_keep[k] = qkv_rows(core, k)
 
+    early.collect((1,))
     q_copy.wait_recv()
 
     @pl.loop(0, 4)
@@ -769,53 +980,26 @@
     gather = Gather(w, part, side, last, half)
     partial(gather.cd)
     gather.send_diagonal()
+    early.collect((2,))
+    early.total((0,))
     partial(gather.cx)
     gather.send_x()
     partial(gather.cy)
     gather.send_y()
+    early.collect((3,))
+    early.total((1,))
     partial(chip)
     vec_step(1)
     for copy in moved:
         copy.wait_recv()
-
-    size = piece // CHUNKS
-    inner = jnp.logical_or(rep == 1, rep == 2)
-    first, middle_hop, back = [], [], []
-    for i in range(CHUNKS):
-        rows = pl.ds(i * size, size)
-        first.append(w.remote(z_own.at[rows], z_in.at[rows], own, z1))
-    for i in range(CHUNKS):
-        rows = pl.ds(i * size, size)
-        middle_hop.append(w.remote(z_mid.at[rows], z_far.at[rows], own, z3))
-    for i in range(CHUNKS):
-        rows = pl.ds(i * size, size)
-        back.append(w.remote(z_out.at[rows], z_out.at[rows], own, z1))
-
-    @pl.when(jnp.logical_not(inner))
-    def _():
-        for i in range(CHUNKS):
-            first[i].start()
-
-    @pl.when(inner)
-    def _():
-        for i in range(CHUNKS):
-            rows = pl.ds(i * size, size)
-            first[i].wait_recv()
-            z_mid[rows, :] = (z_own[rows, :].astype(F32) + z_in[rows, :].astype(F32)).astype(BF16)
-            middle_hop[i].start()
-
+    late = Line(w, z_own, z_in, z_far, CHUNKS)
+    late.start()
+    early.collect((4,))
+    early.total((2,))
     gather.relay()
     vec_step(2)
-
-    @pl.when(inner)
-    def _():
-        for i in range(CHUNKS):
-            rows = pl.ds(i * size, size)
-            middle_hop[i].wait_recv()
-            z_out[rows, :] = (z_mid[rows, :].astype(F32) + z_far[rows, :].astype(F32)).astype(BF16)
-            back[i].start()
-
-    vec_step(3)
+    early.collect((5, 6))
+    early.total((3, 4))
     step = 32
 
     def final_rows(which, t):
@@ -824,97 +1008,93 @@
 
     gather.wait_first()
     pl.loop(0, half // step)(functools.partial(final_rows, 0))
+    vec_step(3)
+    early.collect((7,))
+    early.total((5,))
     gather.wait_second()
     pl.loop(0, half // step)(functools.partial(final_rows, 1))
     vec_step(4)
-
-    @pl.when(jnp.logical_not(inner))
-    def _():
-        for i in range(CHUNKS):
-            first[i].wait_send()
-            back[i].wait_recv()
-
-    @pl.when(inner)
-    def _():
-        for i in range(CHUNKS):
-            middle_hop[i].wait_send()
-            back[i].wait_send()
-
-    qkv_total[...] = z_out[...]
+    early.collect((8, 9))
+    early.total((6, 7))
+    late.collect((0,))
+    early.total((8,))
+    late.collect((1,))
+    early.total((9,))
+    for i in range(2, CHUNKS):
+        late.collect((i,))
+        late.total((i - 2,))
+    late.total((CHUNKS - 2, CHUNKS - 1))
+    for m in range(4):
+        for i in (2 * m, 2 * m + 1):
+            early.arrive((i,))
+        up_total[:, rows_of(lax.bitwise_xor(chip, m), width)] = y_in[m * piece : (m + 1) * piece, :].astype(F32) * grad_scale
+    early.arrive((8, 9))
+    out_total[...] = y_in[4 * piece :, :].astype(F32) * grad_scale
+    for i in range(CHUNKS):
+        late.arrive((i,))
+        rows = late.rows[i]
+        qkv_total[rows, :] = z_in[rows, :].astype(F32) * grad_scale
+    early.finish()
+    late.finish()
     w.finish()
 
 
-def finish(dq, dk, dv, xs, w_full, branch_grad, vec):
+def finish(grad_scale, dq, dk, dv, xs, w_full, branch_grad, vec, keep, got_x, got_y, got_d):
     toks, width = branch_grad.shape
     piece = w_full.shape[0] // 8
     half = toks // 2
     shape = jax.ShapeDtypeStruct
     vm = pltpu.VMEM
     line = vm((piece, 3 * width), BF16)
+    five = vm((5 * piece, width), BF16)
     return pl.pallas_call(
-        finish_body,
+        functools.partial(finish_body, grad_scale),
         name="finish",
-        out_shape=(shape((toks, width), BF16), shape((piece, 3 * width), BF16), shape(vec.shape, F32)),
-        in_specs=[VM] * 7,
-        out_specs=(VM,) * 3,
+        out_shape=(
+            shape((toks, width), BF16), shape((piece, 3 * width), F32), shape((piece, width), F32), shape((piece, 4 * width), F32),
+            shape((4, width), F32), shape((1, 4 * width), F32), shape((2, width), F32), shape((2, width), F32),
+        ),
+        in_specs=[VM] * 11,
+        out_specs=(VM,) * 8,
         scratch_shapes=[
             vm((4, toks, 3 * width // 4), BF16),
             vm((4, toks, width), BF16), vm((4, half, width), BF16), vm((2, half, width), BF16),
             vm((4, piece, 3 * width // 4), BF16), vm((4, piece, 3 * width // 4), BF16), vm((4, piece, 3 * width // 4), F32),
             vm((4, piece, 3 * width // 4), BF16),
-            line, line, line, line, line,
+            line, line, line, five, five, five,
             vm(vec.shape, F32), vm((9,) + vec.shape, F32),
-            pltpu.SemaphoreType.DMA((64,)), pltpu.SemaphoreType.DMA((64,)), pltpu.SemaphoreType.DMA((8,)),
+            pltpu.SemaphoreType.DMA((96,)), pltpu.SemaphoreType.DMA((96,)), pltpu.SemaphoreType.DMA((8,)),
         ],
         compiler_params=pltpu.CompilerParams(collective_id=2, has_side_effects=True, vmem_limit_bytes=48 << 20),
-    )(dq, dk, dv, xs, w_full, branch_grad, vec)
+    )(dq, dk, dv, xs, w_full, branch_grad, vec, keep, got_x, got_y, got_d)
 
 
 def local_tensor(tokens, segment_ids, qkv_weight, out_weight, up_weight, down_weight, proj_bias, hidden_bias, norm_gain, norm_shift, cotangent):
     inputs = tokens[0]
     toks, width = inputs.shape
     scale = (width // HEADS) ** (-0.5)
-    own = lax.axis_index("fsdp")
-    chip = own // 2
-    ff = up_weight.shape[1] // 4
-    piece = up_weight.shape[0]
-
-    def for_chip(mask):
-        cols = lax.dynamic_slice_in_dim(up_weight, lax.bitwise_xor(chip, mask // 2) * ff, ff, axis=1)
-        return jnp.concatenate([cols, out_weight], axis=0)
-
-    got_x, got_y, got_d = (lax.ppermute(for_chip(m), "fsdp", [(i, i ^ m) for i in range(8)]) for m in (2, 4, 6))
-    queries, key_rows, value_rows, xs, w_full = project(inputs, qkv_weight, proj_bias)
+    grad_scale = (toks * lax.axis_size("fsdp") * lax.axis_size("rep")) ** (-0.5)
+    queries, key_rows, value_rows, xs, w_full, upout = project(inputs, qkv_weight, up_weight, out_weight, proj_bias)
     attended, attended_low, lse = attn_fwd(scale, segment_ids, queries, key_rows, value_rows)
-    output, branch_grad, grad_heads, vec, down_part, upout_part = middle(
-        attended_low, inputs, cotangent[0], up_weight, out_weight, down_weight, got_x, got_y, got_d,
-        proj_bias, hidden_bias[None], norm_gain, norm_shift,
-    )
-    back_x, back_y, back_d = (
-        lax.ppermute(lax.dynamic_index_in_dim(upout_part, lax.bitwise_xor(chip, m // 2), keepdims=False), "fsdp", [(i, i ^ m) for i in range(8)])
-        for m in (2, 4, 6)
-    )
-    kept = lax.dynamic_index_in_dim(upout_part, chip, keepdims=False)
-    up_sum = jnp.zeros((piece, 4 * ff), BF16)
-    for m, block in ((0, kept), (2, back_x), (4, back_y), (6, back_d)):
-        up_sum = lax.dynamic_update_slice_in_dim(up_sum, block[0], lax.bitwise_xor(chip, m // 2) * ff, axis=1)
-    out_sum = sum(b[1].astype(F32) for b in (kept, back_x, back_y, back_d)).astype(BF16)
-    down_total, up_total, out_total = lax.psum((down_part, up_sum, out_sum), "rep")
+    output, branch_grad, grad_heads, vec, down_total, keep, to_x, to_y, to_d = middle(
+        grad_scale, attended_low, inputs, cotangent[0], upout, down_weight, proj_bias, hidden_bias[None], norm_gain, norm_shift
+    )
+    got_x, got_y, got_d = (lax.ppermute(block, "fsdp", [(i, i ^ m) for i in range(8)]) for block, m in ((to_x, 2), (to_y, 4), (to_d, 6)))
     query_grad, key_grad, value_grad = attn_bwd(scale, segment_ids, queries, key_rows, value_rows, grad_heads, attended, lse)
-    input_grad, qkv_total, vec_total = finish(query_grad, key_grad, value_grad, xs, w_full, branch_grad, vec)
-    grad_scale = (toks * lax.axis_size("fsdp") * lax.axis_size("rep")) ** (-0.5)
-    scaled = vec_total * grad_scale
+    input_grad, qkv_total, out_total, up_total, bias_total, hidden_total, gain_total, shift_total = finish(
+        grad_scale, query_grad, key_grad, value_grad, xs, w_full, branch_grad, vec, keep, got_x, got_y, got_d
+    )
     return (
         output[None],
         input_grad[None],
-        qkv_total.astype(F32) * grad_scale,
-        out_total.astype(F32) * grad_scale,
-        up_total.astype(F32) * grad_scale,
-        down_total.astype(F32) * grad_scale,
-        scaled[0:4],
-        scaled[8:12].reshape(4 * width),
-        scaled[4:6],
-        scaled[6:8],
+        qkv_total,
+        out_total,
+        up_total,
+        down_total,
+        bias_total,
+        hidden_total.reshape(4 * width),
+        gain_total,
+        shift_total,
     )
 
 

time: 383 us -> 333 us (0.87)
  waiting for transfers between devices: 18.7 us -> 0.01 us
  between operations: 14.3 us -> 0.84 us
  other arithmetic: 11.9 us -> 0 us
  starting transfers between devices: 7.99 us -> 3.55 us
    pallas_call x2, Pallas kernels: 190 us -> 212 us  [the longest x1 125 us: middle(): pl.pallas_call(functools.partial(middle_body, grad_scale), name='middle',...]
    ppermute x6 -> x3, waiting for transfers between devices: 18.7 us -> 0.01 us  [local_tensor(): lax.ppermute(block, 'fsdp', [(i, i ^ m) for i in range(8)])]
    pallas_call x1, Pallas kernels: 35 us -> 23.9 us  [attn_bwd(): pl.pallas_call(functools.partial(attn_bwd_body, scale), name='attn_bwd',...]
    pallas_call x1, Pallas kernels: 35.6 us -> 24.7 us  [attn_fwd(): pl.pallas_call(functools.partial(attn_fwd_body, scale), name='attn_fwd',...]
    unnamed x38 -> x46, local copies, waits for them, and re-layouts: 6.88 us -> 16.8 us
    mul x5 -> x0, other arithmetic: 7.59 us -> none  [the longest x1 2.77 us: local_tensor(): up_total.astype(F32) * grad_scale]
    dynamic_update_slice x4 -> x0, local copies, waits for them, and re-layouts: 5.73 us -> none  [local_tensor(): lax.dynamic_update_slice_in_dim(up_sum, block[0], lax.bitwise_xor(chip, m...]
    ppermute x6 -> x3, starting transfers between devices: 7.95 us -> 3.55 us  [local_tensor(): lax.ppermute(block, 'fsdp', [(i, i ^ m) for i in range(8)])]
  transfers between devices with their start and end apart: 7 -> 3, of which waited for: 2 -> 0; matrix products, arithmetic and copies ran while one was open for 2% -> 0% of each run, Pallas kernels for 54% -> 7%
where the time goes in v3:
time: 333 us; the launch traced here: 332 us
  Pallas kernels  310 us (93%)
  local copies, waits for them, and re-layouts  16.8 us (5%)
  starting transfers between devices  3.55 us (1%)
    pallas_call x1, Pallas kernels, middle(): pl.pallas_call(functools.partial(middle_body, grad_scale), name='middle',...  125 us
    pallas_call x1, Pallas kernels, finish(): pl.pallas_call(functools.partial(finish_body, grad_scale), name='finish',...  86.7 us
    pallas_call x1, Pallas kernels, project(): pl.pallas_call(project_body, name='project', out_shape=(heads, heads, hea...  50 us
    pallas_call x1, Pallas kernels, attn_fwd(): pl.pallas_call(functools.partial(attn_fwd_body, scale), name='attn_fwd',...  24.7 us
    pallas_call x1, Pallas kernels, attn_bwd(): pl.pallas_call(functools.partial(attn_bwd_body, scale), name='attn_bwd',...  23.9 us
    unnamed x46, local copies, waits for them, and re-layouts  16.8 us
  transfers between devices with their start and end apart: 3, of which 0 were waited for; matrix products, arithmetic and copies ran while one was open for 0% of the time, Pallas kernels for 7%

profile of v3, /device:TPU:0, one launch (start us, length us, event | category | flops | bytes accessed | tf_op | source)
XLA Modules:
  0.0 331.5 jit_solution(5985727338380224222)
XLA Ops:
  0.6 0.0 copy-start
  0.7 1.0 copy-done
  1.7 1.2 copy-done.4
  2.9 1.1 copy-done.6
  4.0 0.9 copy-done.9
  5.0 0.7 copy-done.11
  5.7 50.0 %project.1 = (bf16[2048,128]{1,0:T(8,128)(2,1)S(1)}, bf16[2048,128]{1,0:T(8,128)(2,1)S(1)}, bf16[2048,128]{1,0:T(8,128)(2,1)S(1)}, bf16[4,256,1024]{2,1,0:T(8,12...) custom-call(bf16[256,1024]{1,0:T(8,128)(2,1)S(1)} %bitcast.7, ...), custom_call_target="tpu_custom_call" | custom-call | tf_op jit(solution)/shard_map/project/pallas_call | solution.py:865
  55.7 0.0 copy-start.1
  55.8 0.0 copy-start.2
  55.8 0.0 copy-start.3
  55.8 24.7 %attn_fwd.1 = (f32[2048,128]{1,0:T(8,128)S(1)}, bf16[2048,128]{1,0:T(8,128)(2,1)S(1)}, f32[8,2048]{1,0:T(8,128)S(1)}) custom-call(s32[1,2048]{1,0:T(1,128)S(1)} %copy-done.13, s32[1,2048]{1,0:T(1,128)S(1)} %copy-done.13, bf16[2048,128]{1,0:T(8,128)(2,1)S(1)} %get-tuple-element.39.q_ref, bf16[2048,128]{1,0:T(8,128)(2,1)S(1)} %get-tuple-element.40.k_ref, ...), custom_call_target="tpu_custom_call" | custom-call | flops 2147483648 | bytes 1572864 | tf_op jit(solution)/shard_map/attn_fwd/pallas_call | solution.py:140
  80.6 0.0 copy-start.8
  80.6 0.8 copy-done.8
  81.4 125.0 %middle.1 = (bf16[256,1024]{1,0:T(8,128)(2,1)}, f32[256,1024]{1,0:T(8,128)}, bf16[2048,128]{1,0:T(8,128)(2,1)}, f32[16,1024]{1,0:T(8,128)}, f32[512,1024]{1,0:T(...) custom-call(bf16[2048,128]{1,0:T(8,128)(2,1)} %copy-done.8, ...), custom_call_target="tpu_custom_call" | custom-call | tf_op jit(solution)/shard_map/middle/pallas_call | solution.py:710
  206.3 0.7 collective-permute-start
  207.0 1.4 collective-permute-start.1
  208.4 1.5 collective-permute-start.2
  209.9 1.0 copy-done.12
  210.9 23.9 %attn_bwd.1 = (bf16[2,4,256,128]{3,2,1,0:T(8,128)(2,1)S(1)}, bf16[2,4,256,128]{3,2,1,0:T(8,128)(2,1)S(1)}, bf16[2,4,256,128]{3,2,1,0:T(8,128)(2,1)S(1)}) custom-call(s32[1,2048]{1,0:T(1,128)S(1)} %copy-done.13, s32[1,2048]{1,0:T(1,128)S(1)} %copy-done.13, bf16[2048,128]{1,0:T(8,128)(2,1)S(1)} %get-tuple-element.39.q_ref, ...), custom_call_target="tpu_custom_call" | custom-call | flops 5368709120 | bytes 3670016 | tf_op jit(solution)/shard_map/attn_bwd/pallas_call | solution.py:224
  234.9 86.7 %finish.1 = (bf16[256,1024]{1,0:T(8,128)(2,1)S(1)}, f32[128,3072]{1,0:T(8,128)}, f32[128,1024]{1,0:T(8,128)S(1)}, f32[128,4096]{1,0:T(8,128)}, f32[4,1024]{1,0:T...) custom-call(bf16[2,4,256,128]{3,2,1,0:T(8,128)(2,1)S(1)} %get-tuple-element.48.dq, ...), custom_call_target="tpu_custom_call" | custom-call | tf_op jit(solution)/shard_map/finish/pallas_call | solution.py:1050
  321.6 0.8 copy.31
  322.4 0.8 copy.32
  323.2 1.1 copy.33
  324.3 0.8 copy.34
  325.1 0.3 copy-done.15
  325.4 1.3 copy.35
  326.8 1.0 copy-done.14
  327.8 1.3 copy.36
  329.1 0.6 copy.37
  329.7 0.6 copy.38
  330.3 0.6 copy.39
  330.9 0.6 copy.40
  (25 shorter events, 0.0 us)
Async XLA Ops:
  0.6 1.0 copy-start
  1.7 1.2 copy-start.4
  2.9 1.1 copy-start.6
  4.0 0.9 copy-start.9
  5.0 0.7 copy-start.11
  5.7 50.1 %copy-start.13 = (s32[1,2048]{1,0:T(1,128)S(1)}, s32[1,2048]{1,0:T(1,128)}, u32[]{:S(2)}) copy-start(s32[1,2048]{1,0:T(1,128)} %seg_v.3) | copy-start | bytes 24580
  55.7 24.8 %copy-start.1 = (bf16[4,2,128,1024]{3,2,1,0:T(8,128)(2,1)}, bf16[4,2,128,1024]{3,2,1,0:T(8,128)(2,1)S(1)}, u32[]{:S(2)}) copy-start(bf16[4,2,128,1024]{3,2,1,0:T(8,128)(2,1)S(1)} %get-tuple-element.43.upout) | copy-start | bytes 6291460
  55.8 24.8 %copy-start.2 = (bf16[4,256,1024]{2,1,0:T(8,128)(2,1)}, bf16[4,256,1024]{2,1,0:T(8,128)(2,1)S(1)}, u32[]{:S(2)}) copy-start(bf16[4,256,1024]{2,1,0:T(8,128)(2,1)S(1)} %get-tuple-element.51.xs) | copy-start | bytes 6291460
  55.8 24.8 %copy-start.3 = (bf16[1024,768]{1,0:T(8,128)(2,1)}, bf16[1024,768]{1,0:T(8,128)(2,1)S(1)}, u32[]{:S(2)}) copy-start(bf16[1024,768]{1,0:T(8,128)(2,1)S(1)} %get-tuple-element.52.w_full) | copy-start | bytes 4718596
  80.6 0.8 copy-start.8
  206.3 28.5 %collective-permute-start = (bf16[2,128,1024]{2,1,0:T(8,128)(2,1)}, bf16[2,128,1024]{2,1,0:T(8,128)(2,1)S(1)}, u32[]{:S(2)}, u32[]{:S(2)}) collective-permute-start(bf16[2,128,1024]{2,1,0:T(8,128)(2,1)} %get-tuple-element.56), channel_id=1, source_target_pairs={{0,2},{1,3},{2,0},{3,1},{4,6},{5,7},{6,4},{7,5},{8,10},{9,11},{10,... | collective-permute-start | bytes 1572872 | tf_op jit(solution)/shard_map/ppermute | solution.py:1082
  207.0 27.8 %collective-permute-start.1 = (bf16[2,128,1024]{2,1,0:T(8,128)(2,1)}, bf16[2,128,1024]{2,1,0:T(8,128)(2,1)S(1)}, u32[]{:S(2)}, u32[]{:S(2)}) collective-permute-start(bf16[2,128,1024]{2,1,0:T(8,128)(2,1)} %get-tuple-element.57), channel_id=1, source_target_pairs={{0,4},{1,5},{2,6},{3,7},{4,0},{5,1},{6,2},{7,3},{8,12},{9,13},{10,... | collective-permute-start | bytes 1572872 | tf_op jit(solution)/shard_map/ppermute | solution.py:1082
  208.4 26.4 %collective-permute-start.2 = (bf16[2,128,1024]{2,1,0:T(8,128)(2,1)}, bf16[2,128,1024]{2,1,0:T(8,128)(2,1)S(1)}, u32[]{:S(2)}, u32[]{:S(2)}) collective-permute-start(bf16[2,128,1024]{2,1,0:T(8,128)(2,1)} %get-tuple-element.58), channel_id=1, source_target_pairs={{0,6},{1,7},{2,4},{3,5},{4,2},{5,3},{6,0},{7,1},{8,14},{9,15},{10,... | collective-permute-start | bytes 1572872 | tf_op jit(solution)/shard_map/ppermute | solution.py:1082
  209.9 1.0 copy-start.12
  210.9 23.9 %copy-start.5 = (f32[256,1024]{1,0:T(8,128)S(1)}, f32[256,1024]{1,0:T(8,128)}, u32[]{:S(2)}) copy-start(f32[256,1024]{1,0:T(8,128)} %get-tuple-element.53.branch_grad) | copy-start | bytes 3145732
  210.9 23.9 %copy-start.7 = (bf16[2,128,1024]{2,1,0:T(8,128)(2,1)S(1)}, bf16[2,128,1024]{2,1,0:T(8,128)(2,1)}, u32[]{:S(2)}) copy-start(bf16[2,128,1024]{2,1,0:T(8,128)(2,1)} %get-tuple-element.55.keep) | copy-start | bytes 1572868
  210.9 23.9 %copy-start.10 = (f32[16,1024]{1,0:T(8,128)S(1)}, f32[16,1024]{1,0:T(8,128)}, u32[]{:S(2)}) copy-start(f32[16,1024]{1,0:T(8,128)} %get-tuple-element.54.vec) | copy-start | bytes 196612
  234.9 86.7 %copy-start.17 = (bf16[256,1024]{1,0:T(8,128)(2,1)S(1)}, bf16[256,1024]{1,0:T(8,128)(2,1)}, u32[]{:S(2)}) copy-start(bf16[256,1024]{1,0:T(8,128)(2,1)} %get-tuple-element.44) | copy-start | bytes 1572868
  321.6 1.6 copy-start.16
  323.2 2.3 copy-start.15
  325.4 2.3 copy-start.14

commit v4 on v3

--- a/solution.py
+++ b/solution.py
@@ -153,93 +153,6 @@
     )(seg, seg, q, k, v)
 
 
-def attn_bwd_body(scale, seg_s, seg_v, q_ref, k_ref, v_ref, g_ref, o_ref, lse_ref, dq_ref, dk_ref, dv_ref, corr, kt, dk_acc, dv_acc, dqt, seg_c):
-    length, width = q_ref.shape
-    half = width // 2
-    n = length // BQ
-    first = head_lanes((BQ, width), half)
-    seg_columns(seg_v, seg_c)
-
-    @pl.loop(0, n)
-    def _(i):
-        rows = rows_of(i, BQ)
-        prod = jnp.transpose(g_ref[rows, :].astype(jnp.float32) * o_ref[rows, :])
-        corr[0:1, rows] = jnp.sum(prod[:half], axis=0, keepdims=True)
-        corr[1:2, rows] = jnp.sum(prod[half:], axis=0, keepdims=True)
-        kt[:, rows] = jnp.transpose(k_ref[rows, :])
-        dk_acc[rows, :] = jnp.zeros((BQ, width), jnp.float32)
-        dv_acc[rows, :] = jnp.zeros((BQ, width), jnp.float32)
-
-    @pl.loop(0, n)
-    def _(i):
-        lo, hi = block_range(seg_s, i * BQ, BQ, BK, length // BK)
-        rows = rows_of(i, BQ)
-        qb = q_ref[rows, :] * jnp.bfloat16(scale)
-        gb = g_ref[rows, :]
-        zero = jnp.zeros_like(qb)
-        qs = (jnp.where(first, qb, zero), jnp.where(first, zero, qb))
-        gs = (jnp.where(first, gb, zero), jnp.where(first, zero, gb))
-        qz = jnp.concatenate(qs, axis=0)
-        gz = jnp.concatenate(gs, axis=0)
-        seg_q = seg_v[:, rows].astype(jnp.float32)
-
-        def term(cols, dq):
-            kb = k_ref[cols, :]
-            vb = v_ref[cols, :]
-            same = wide(seg_c[cols, :], BQ) == seg_q
-            ps, ds = [], []
-            for h in range(2):
-                s = jnp.where(same, nt(kb, qs[h]), NEGATIVE)
-                p = jnp.exp(s - lse_ref[h : h + 1, rows])
-                dp = nt(vb, gs[h])
-                d = (p * (dp - corr[h : h + 1, rows])).astype(jnp.bfloat16)
-                ps.append(p.astype(jnp.bfloat16))
-                ds.append(d)
-                dq[h] = dq[h] + nn(kt[h * half : (h + 1) * half, cols], d)
-            dv_acc[cols, :] += nn(jnp.concatenate(ps, axis=1), gz)
-            dk_acc[cols, :] += nn(jnp.concatenate(ds, axis=1), qz)
-            return dq
-
-        def run(count):
-            base = jnp.minimum(lo, length // BK - count)
-            dq = [jnp.zeros((half, BQ), jnp.float32)] * 2
-            for j in range(count):
-                dq = term(rows_of(base + j, BK), dq)
-            dqt[0:half, :] = dq[0]
-            dqt[half:, :] = dq[1]
-
-        for count in range(1, length // BK + 1):
-            pl.when(hi - lo == count)(functools.partial(run, count))
-        dq_ref[lax.rem(i, 2), i // 2] = (jnp.transpose(dqt[...]) * scale).astype(jnp.bfloat16)
-
-    @pl.loop(0, n)
-    def _(i):
-        rows = rows_of(i, BQ)
-        dk_ref[lax.rem(i, 2), i // 2] = dk_acc[rows, :].astype(jnp.bfloat16)
-        dv_ref[lax.rem(i, 2), i // 2] = dv_acc[rows, :].astype(jnp.bfloat16)
-
-
-def attn_bwd(scale, seg, q, k, v, g, o, lse):
-    length, width = q.shape
-    return pl.pallas_call(
-        functools.partial(attn_bwd_body, scale),
-        name="attn_bwd",
-        out_shape=tuple(jax.ShapeDtypeStruct((2, length // BQ // 2, BQ, width), jnp.bfloat16) for _ in range(3)),
-        in_specs=[SM, VM, VM, VM, VM, VM, VM, VM],
-        out_specs=(VM, VM, VM),
-        scratch_shapes=[
-            pltpu.VMEM((8, length), jnp.float32),
-            pltpu.VMEM((width, length), jnp.bfloat16),
-            pltpu.VMEM((length, width), jnp.float32),
-            pltpu.VMEM((length, width), jnp.float32),
-            pltpu.VMEM((width, BQ), jnp.float32),
-            pltpu.VMEM((length, 128), jnp.float32),
-        ],
-        compiler_params=pltpu.CompilerParams(vmem_limit_bytes=32 << 20),
-        cost_estimate=pl.CostEstimate(flops=10 * length * length * width, bytes_accessed=14 * length * width, transcendentals=2 * length * length),
-    )(seg, seg, q, k, v, g, o, lse)
-
-
 MESH = pl.DeviceIdType.MESH
 HBM = pl.BlockSpec(memory_space=pltpu.HBM)
 F32 = jnp.float32
@@ -350,6 +263,38 @@
                 self.back[i].wait_send()
 
 
+class Hops:
+    def __init__(self, wires, view):
+        rep, reps = wires.rep, 4
+        self.all = []
+        for hop in range(1, reps):
+            for step in (1, -1):
+                index, to, come = rep - step * (hop - 1), rep + step, rep - step * hop
+                going = (index >= 0) & (index < reps) & (to >= 0) & (to < reps)
+                coming = (come >= 0) & (come < reps)
+                refs = view(jnp.clip(index, 0, reps - 1))
+                copies = [wires.remote(ref, ref, wires.own, jnp.clip(to, 0, reps - 1)) for ref in refs]
+                self.all.append((hop, going, coming, copies))
+
+    def each(self, hop, kind):
+        for at, going, coming, copies in self.all:
+            if hop in (0, at):
+
+                @pl.when(coming if kind == "wait_recv" else going)
+                def _():
+                    for copy in copies:
+                        getattr(copy, kind)()
+
+    def start(self, hop):
+        self.each(hop, "start")
+
+    def wait(self, hop):
+        self.each(hop, "wait_recv")
+
+    def finish(self):
+        self.each(0, "wait_send")
+
+
 class Spread:
     def __init__(self, wires, slots, half):
         self.wires, self.slots, self.half = wires, slots, half
@@ -437,10 +382,10 @@
 
 
 def middle_body(
-    grad_scale, heads, x, cot, upout, down_w, proj_bias, hidden_bias, gain, shift,
+    heads, x, cot, upout, down_w, proj_bias, hidden_bias, gain, shift,
     output, branch_grad, grad_heads, vec, down_grad, keep, to_x, to_y, to_d,
     att, out_full, up_full, down_full, h1, z1, r1, gs, fl, act, slope, part, side, last, sl, pre, part2, side2, last2,
-    branch_low, agl, acc, d_send, d_recv, d_keep, d_own, d_land, d_far, u_send, u_recv, u_keep, o_send, o_recv, o_keep,
+    branch_low, agl, acc, d_send, d_recv, d_keep, u_send, u_recv, u_keep, o_send, o_recv, o_keep,
     send_sems, recv_sems, local_sems,
 ):
     w = Wires(send_sems, recv_sems, local_sems)
@@ -454,20 +399,37 @@
     half = toks // 2
     piece = upout.shape[2]
     tile = 256
-    w.greet([(w.rep, lax.bitwise_xor(own, m)) for m in range(1, 8)] + [(lax.bitwise_xor(w.rep, m), own) for m in (1, 3)])
+    w.greet(
+        [(w.rep, lax.bitwise_xor(own, m)) for m in range(1, 8)] + [(lax.rem(w.rep + 1, 4), own), (lax.rem(w.rep + 3, 4), own)]
+    )
 
     swaps = []
     for m in (6, 2, 4, 1, 3, 5, 7):
         peer = lax.bitwise_xor(own, m)
         swaps.append(w.send(heads.at[rows_of(peer, toks)], att.at[:, rows_of(own, head_width)], peer))
+    quarter = piece // 4
+    some = rows_of(w.rep, quarter)
+
+    def up_piece(k, r):
+        return up_full.at[pl.ds(pl.multiple_of((2 * k + core) * piece + r * quarter, quarter), quarter)]
+
+    others = (cd, cx, cy)
+    seeds = [w.local(upout.at[k, 0, some], up_piece(k, w.rep)) for k in others]
+    hops = Hops(w, lambda r: [up_piece(k, r) for k in others])
     weights = []
     for k in range(4):
         dst = rows_of(2 * k + core, piece)
-        for s, full in ((upout.at[k, 1], out_full), (upout.at[k, 0], up_full)):
-            weights.append((w.local(s, full.at[dst]), w.send(s, full.at[dst], mate)))
+        weights.append((w.local(upout.at[k, 1], out_full.at[dst]), w.send(upout.at[k, 1], out_full.at[dst], mate)))
+    dst = rows_of(own, piece)
+    weights.append((w.local(upout.at[chip, 0], up_full.at[dst]), w.send(upout.at[chip, 0], up_full.at[dst], mate)))
     dst = rows_of(core, ff // 2)
     weights.append((w.local(down_w, down_full.at[dst]), w.send(down_w, down_full.at[dst], mate)))
+    for copy in seeds:
+        copy.wait()
+    hops.start(1)
     att[:, rows_of(own, head_width)] = heads[rows_of(own, toks), :]
+    hops.wait(1)
+    hops.start(2)
     for copy in swaps:
         copy.wait_recv()
     for here, there in weights:
@@ -481,6 +443,8 @@
 
     step = 32
     acc[...] = jnp.zeros_like(acc)
+    hops.wait(2)
+    hops.start(3)
 
     def first_rows(t):
         rows = rows_of(t, step)
@@ -511,6 +475,13 @@
             cols = rows_of(n, tile)
             part[k, :, cols] = nn(act[k], down_full[:, cols]).astype(BF16)
 
+    hops.wait(3)
+    passed = []
+    for k in others:
+        dst = rows_of(2 * k + core, piece)
+        passed.append(w.send(up_full.at[dst], up_full.at[dst], mate))
+    for copy in passed:
+        copy.wait_recv()
     forward(chip)
     gather = Gather(w, part, side, last, half)
     spread.relay()
@@ -609,10 +580,7 @@
     @pl.loop(0, ff // 2 // 64)
     def _(t):
         rows = rows_of(t, 64)
-        d_own[rows, :] = (d_keep[rows, :] + d_recv[rows, :].astype(F32)).astype(BF16)
-
-    line = Line(w, d_own, d_land, d_far, 8)
-    line.start()
+        down_grad[rows, :] = (d_keep[rows, :] + d_recv[rows, :].astype(F32)).astype(BF16)
 
     def up_rows(which, k):
         cols = pl.ds(pl.multiple_of((2 * k + which) * piece, piece), piece)
@@ -640,7 +608,6 @@
 
     gather2.wait_first()
     pl.loop(0, half // step)(functools.partial(branch_rows, 0))
-    line.collect((0, 1))
     gather2.wait_second()
     pl.loop(0, half // step)(functools.partial(branch_rows, 1))
 
@@ -654,8 +621,6 @@
         peer = lax.bitwise_xor(own, m)
         backs.append(w.send(agl.at[:, rows_of(peer, head_width)], grad_heads.at[rows_of(own, toks)], peer))
     grad_heads[rows_of(own, toks), :] = agl[:, rows_of(own, head_width)]
-    line.collect((2, 3))
-    line.total((0, 1))
 
     def out_rows(which, k):
         cols = pl.ds(pl.multiple_of((2 * k + which) * piece, piece), piece)
@@ -666,24 +631,18 @@
         o_send[k] = out_rows(1 - core, k).astype(BF16)
 
     o_copy = w.send(o_send, o_recv, mate)
-    line.collect((4,))
-    line.total((2,))
 
     @pl.loop(0, 4)
     def _(k):
         u_keep[k] = up_rows(core, k)
         o_keep[k] = out_rows(core, k)
 
-    line.collect((5,))
-    line.total((3,))
     u_copy.wait_recv()
     o_copy.wait_recv()
     for m, ref in enumerate((keep, to_x, to_y, to_d)):
         k = lax.bitwise_xor(chip, m)
         ref[0] = (u_keep[k] + u_recv[k].astype(F32)).astype(BF16)
         ref[1] = (o_keep[k] + o_recv[k].astype(F32)).astype(BF16)
-    line.collect((6, 7))
-    line.total((4, 5, 6, 7))
     vec[...] = jnp.zeros_like(vec)
     for row, slot in ((2, 6), (3, 2), (4, 4), (5, 0), (6, 5), (7, 1)):
         vec[row : row + 1, :] = jnp.sum(acc[slot], axis=0, keepdims=True)
@@ -692,15 +651,11 @@
         vec[8 + k : 9 + k, :] = jnp.where(chip == k, hidden_sum, jnp.zeros_like(hidden_sum))
     for copy in backs:
         copy.wait_recv()
-    for i in range(8):
-        line.arrive((i,))
-        rows = line.rows[i]
-        down_grad[rows, :] = d_land[rows, :].astype(F32) * grad_scale
-    line.finish()
+    hops.finish()
     w.finish()
 
 
-def middle(grad_scale, heads, x, cot, upout, down_w, proj_bias, hidden_bias, gain, shift):
+def middle(heads, x, cot, upout, down_w, proj_bias, hidden_bias, gain, shift):
     toks, width = x.shape
     piece = upout.shape[2]
     ff = 2 * down_w.shape[0]
@@ -708,14 +663,14 @@
     shape = jax.ShapeDtypeStruct
     vm = pltpu.VMEM
     return pl.pallas_call(
-        functools.partial(middle_body, grad_scale),
+        middle_body,
         name="middle",
         out_shape=(
             shape((toks, width), BF16),
             shape((toks, width), F32),
             shape(heads.shape, BF16),
             shape((16, width), F32),
-            shape((ff // 2, width), F32),
+            shape((ff // 2, width), BF16),
         )
         + (shape((2, piece, width), BF16),) * 4,
         in_specs=[VM, VM, VM, HBM, HBM] + [VM] * 4,
@@ -729,12 +684,11 @@
             vm((4, toks, width), BF16), vm((4, half, width), BF16), vm((2, half, width), BF16),
             vm((toks, width), BF16), vm((toks, width), BF16), vm((8, 8, width), F32),
             vm((ff // 2, width), BF16), vm((ff // 2, width), BF16), vm((ff // 2, width), F32),
-            vm((ff // 2, width), BF16), vm((ff // 2, width), BF16), vm((ff // 2, width), BF16),
             vm((4, piece, ff), BF16), vm((4, piece, ff), BF16), vm((4, piece, ff), F32),
             vm((4, piece, width), BF16), vm((4, piece, width), BF16), vm((4, piece, width), F32),
             pltpu.SemaphoreType.DMA((96,)), pltpu.SemaphoreType.DMA((96,)), pltpu.SemaphoreType.DMA((16,)),
         ],
-        compiler_params=pltpu.CompilerParams(collective_id=1, has_side_effects=True, vmem_limit_bytes=60 << 20),
+        compiler_params=pltpu.CompilerParams(collective_id=1, has_side_effects=True, vmem_limit_bytes=44 << 20),
     )(heads, x, cot, upout, down_w, proj_bias, hidden_bias, gain, shift)
 
 
@@ -769,36 +723,7 @@
         fetched.append(w.send(out_w.at[some], upout.at[chip, 1, some], peer))
     kept = [w.local(up_w.at[:, rows_of(chip, width)], upout.at[chip, 0]), w.local(out_w, upout.at[chip, 1])]
     others = [lax.bitwise_xor(chip, m) for m in (3, 1, 2)]
-    hops = []
-    for hop in range(1, reps):
-        for step in (1, -1):
-            index = rep - step * (hop - 1)
-            to = rep + step
-            going = jnp.logical_and(jnp.logical_and(index >= 0, index < reps), jnp.logical_and(to >= 0, to < reps))
-            come = rep - step * hop
-            coming = jnp.logical_and(come >= 0, come < reps)
-            some = rows_of(jnp.clip(index, 0, reps - 1), quarter)
-            copies = [w.remote(upout.at[c, :, some], upout.at[c, :, some], own, jnp.clip(to, 0, reps - 1)) for c in others]
-            hops.append((hop, going, coming, copies))
-
-    def hop_start(which):
-        for hop, going, coming, copies in hops:
-            if hop == which:
-
-                @pl.when(going)
-                def _():
-                    for copy in copies:
-                        copy.start()
-
-    def hop_wait(which):
-        for hop, going, coming, copies in hops:
-            if hop == which:
-
-                @pl.when(coming)
-                def _():
-                    for copy in copies:
-                        copy.wait_recv()
-
+    hops = Hops(w, lambda r: [upout.at[c, 1, rows_of(r, quarter)] for c in others])
     xs[chip] = x[...]
     spread = Spread(w, xs, toks // 2)
     spread.first_half()
@@ -810,6 +735,9 @@
             copy.wait_recv()
         rows = rows_of(peer, piece)
         theirs.append(w.send(w_full.at[rows], w_full.at[rows], mate))
+    for copy in fetched:
+        copy.wait_recv()
+    hops.start(1)
     for copy in here:
         copy.wait()
     for copy in theirs:
@@ -827,32 +755,23 @@
             swaps.append(w.send(stage.at[k, :, pl.ds(pl.multiple_of(p * share + (1 - core) * head_width, head_width), head_width)], outs[p].at[rows], mate))
             outs[p][rows, :] = stage[k, :, pl.ds(pl.multiple_of(p * share + core * head_width, head_width), head_width)]
 
-    for copy in fetched:
-        copy.wait_recv()
-    hop_start(1)
     block(chip)
     spread.relay()
-    hop_wait(1)
-    hop_start(2)
+    hops.wait(1)
+    hops.start(2)
     spread.wait_sides()
     block(spread.cx)
     block(spread.cy)
-    hop_wait(2)
-    hop_start(3)
+    hops.wait(2)
+    hops.start(3)
     spread.wait_diagonal()
     block(spread.cd)
     for copy in swaps:
         copy.wait_recv()
-    hop_wait(3)
+    hops.wait(3)
     for copy in kept:
         copy.wait()
-    for hop, going, coming, copies in hops:
-
-        @pl.when(going)
-        def _():
-            for copy in copies:
-                copy.wait_send()
-
+    hops.finish()
     w.finish()
 
 
@@ -876,13 +795,11 @@
     )(x, qkv_w, up_w, out_w, proj_bias)
 
 
-CHUNKS = 8
-
-
-def finish_body(
-    grad_scale, dq, dk, dv, xs, w_full, branch_grad, vec, keep, got_x, got_y, got_d,
-    input_grad, qkv_total, out_total, up_total, bias_total, hidden_total, gain_total, shift_total,
-    grads, part, side, last, q_send, q_recv, q_keep, q_piece, z_own, z_in, z_far, y_own, y_in, y_far, v_sum, v_recv,
+def backward_body(
+    scale, seg, q, k, v, g, o, lse, xs, w_full, branch_grad, vec, down, keep, to_x, to_y, to_d,
+    input_grad, qkv_sum, upout_sum, down_sum, vec_sum,
+    corr, kt, dk_acc, dv_acc, dqt, seg_c, heads, grads, part, side, last, q_send, q_recv, q_keep, q_piece, l_own, l_far,
+    d_own, d_far, got, y_own, y_far, v_sum, v_recv,
     send_sems, recv_sems, local_sems,
 ):
     w = Wires(send_sems, recv_sems, local_sems)
@@ -892,25 +809,106 @@
     toks, width = branch_grad.shape
     share = width // 4
     head_width = share // 2
-    piece = q_keep.shape[1]
+    piece = keep.shape[1]
     half = toks // 2
     tile = 256
     z1, z2, z3 = (lax.bitwise_xor(rep, m) for m in (1, 2, 3))
     w.greet([(rep, lax.bitwise_xor(own, m)) for m in (1, 2, 4, 6)] + [(z1, own), (z2, own), (z3, own)])
 
-    for m, ref in enumerate((keep, got_x, got_y, got_d)):
-        y_own[m * piece : (m + 1) * piece, :] = ref[0]
-    y_own[4 * piece :, :] = (keep[1].astype(F32) + got_x[1].astype(F32) + got_y[1].astype(F32) + got_d[1].astype(F32)).astype(BF16)
-    early = Line(w, y_own, y_in, y_far, 10)
-    early.start()
+    spread = [w.send(ref, got.at[i], lax.bitwise_xor(own, m)) for i, (m, ref) in enumerate(((6, to_d), (2, to_x), (4, to_y)))]
+    d_own[...] = down[...]
+    down_line = Line(w, d_own, down_sum, d_far, 8)
+    down_line.start()
+    upout_line = Line(w, y_own, upout_sum, y_far, 10)
+    lines = [Line(w, l_own.at[p], qkv_sum.at[p], l_far.at[p], 4) for p in range(3)]
+
+    def upout_start():
+        for copy in spread:
+            copy.wait_recv()
+        for i, ref in enumerate((keep, got.at[1], got.at[2], got.at[0])):
+            y_own[i * piece : (i + 1) * piece, :] = ref[0]
+        y_own[4 * piece :, :] = (keep[1].astype(F32) + got[0, 1].astype(F32) + got[1, 1].astype(F32) + got[2, 1].astype(F32)).astype(BF16)
+        upout_line.start()
+
+    hooks = {
+        0: lambda: down_line.collect((0,)),
+        1: lambda: (down_line.collect((1,)), down_line.total((0,))),
+        2: lambda: (down_line.collect((2, 3)), down_line.total((1,))),
+        3: lambda: (down_line.collect((4,)), down_line.total((2, 3))),
+        4: lambda: (down_line.collect((5, 6)), down_line.total((4,))),
+        5: lambda: (upout_start(), down_line.collect((7,)), down_line.total((5, 6))),
+        6: lambda: (down_line.total((7,)), upout_line.collect((0,))),
+        7: lambda: (upout_line.collect((1,)), upout_line.total((0,))),
+    }
+
+    length, head_cols = q.shape
+    headd = head_cols // 2
+    blocks = length // BQ
+    first = head_lanes((BQ, head_cols), headd)
+    seg_columns(seg, seg_c)
+
+    @pl.loop(0, blocks)
+    def _(i):
+        rows = rows_of(i, BQ)
+        prod = jnp.transpose(g[rows, :].astype(F32) * o[rows, :])
+        corr[0:1, rows] = jnp.sum(prod[:headd], axis=0, keepdims=True)
+        corr[1:2, rows] = jnp.sum(prod[headd:], axis=0, keepdims=True)
+        kt[:, rows] = jnp.transpose(k[rows, :])
+        dk_acc[rows, :] = jnp.zeros((BQ, head_cols), F32)
+        dv_acc[rows, :] = jnp.zeros((BQ, head_cols), F32)
+
+    @pl.loop(0, blocks)
+    def _(i):
+        rows = rows_of(i, BQ)
+        qb = q[rows, :] * jnp.bfloat16(scale)
+        gb = g[rows, :]
+        zero = jnp.zeros_like(qb)
+        qs = (jnp.where(first, qb, zero), jnp.where(first, zero, qb))
+        gs = (jnp.where(first, gb, zero), jnp.where(first, zero, gb))
+        qz = jnp.concatenate(qs, axis=0)
+        gz = jnp.concatenate(gs, axis=0)
+        seg_q = seg[:, rows].astype(F32)
+        dq = [jnp.zeros((headd, BQ), F32)] * 2
+        for j in range(length // BK):
+            cols = pl.ds(j * BK, BK)
+            kb = k[cols, :]
+            vb = v[cols, :]
+            same = wide(seg_c[cols, :], BQ) == seg_q
+            ps, ds = [], []
+            for h in range(2):
+                s = jnp.where(same, nt(kb, qs[h]), NEGATIVE)
+                p = jnp.exp(s - lse[h : h + 1, rows])
+                dp = nt(vb, gs[h])
+                dscore = (p * (dp - corr[h : h + 1, rows])).astype(BF16)
+                ps.append(p.astype(BF16))
+                ds.append(dscore)
+                dq[h] = dq[h] + nn(kt[h * headd : (h + 1) * headd, cols], dscore)
+            dv_acc[cols, :] += nn(jnp.concatenate(ps, axis=1), gz)
+            dk_acc[cols, :] += nn(jnp.concatenate(ds, axis=1), qz)
+        dqt[0:headd, :] = dq[0]
+        dqt[headd:, :] = dq[1]
+        heads[0, lax.rem(i, 2), i // 2] = (jnp.transpose(dqt[...]) * scale).astype(BF16)
+        for at, hook in hooks.items():
+
+            @pl.when(i == at)
+            def _(hook=hook):
+                hook()
+
+    @pl.loop(0, blocks)
+    def _(i):
+        rows = rows_of(i, BQ)
+        heads[1, lax.rem(i, 2), i // 2] = dk_acc[rows, :].astype(BF16)
+        heads[2, lax.rem(i, 2), i // 2] = dv_acc[rows, :].astype(BF16)
+
     swaps = []
-    for p, g in enumerate((dq, dk, dv)):
+    for p in range(3):
         cols = pl.ds(pl.multiple_of(p * share + core * head_width, head_width), head_width)
-        swaps.append(w.send(g.at[1 - core], grads.at[:, :, cols], mate))
-        grads[:, :, cols] = g[core]
+        swaps.append(w.send(heads.at[p, 1 - core], grads.at[:, :, cols], mate))
+        grads[:, :, cols] = heads[p, core]
+    upout_line.collect((2,))
     v_sum[...] = vec[...]
-    for row, g in ((0, dq), (1, dv)):
-        total = jnp.sum(g[...].reshape(8 * toks, head_width).astype(F32), axis=0, keepdims=True)
+    for row, p in ((0, 0), (1, 2)):
+        total = jnp.sum(heads[p].reshape(8 * toks, head_width).astype(F32), axis=0, keepdims=True)
         v_sum[row : row + 1, rows_of(own, head_width)] = total
     rounds = [(None, mate), (None, lax.bitwise_xor(own, 2)), (None, lax.bitwise_xor(own, 4)), (z1, own), (z2, own)]
     flying = []
@@ -928,145 +926,197 @@
             v_recv[5 + i] = base + v_recv[i]
             vec_start(i + 1)
         else:
-            final = (base + v_recv[i]) * grad_scale
-            bias_total[...] = final[0:4]
-            gain_total[...] = final[4:6]
-            shift_total[...] = final[6:8]
-            for k in range(4):
-                hidden_total[:, k * width : (k + 1) * width] = final[8 + k : 9 + k]
+            vec_sum[...] = base + v_recv[i]
 
     vec_start(0)
-    for copy in swaps:
+
+    def qkv_rows(which, kk, p):
+        cols = pl.ds(pl.multiple_of((2 * kk + which) * piece, piece), piece)
+        return tn(xs[:, :, cols].reshape(4 * toks, piece), grads[:, :, p * share : (p + 1) * share].reshape(4 * toks, share))
+
+    def theirs(p):
+        @pl.loop(0, 4)
+        def _(kk):
+            q_send[p, kk] = qkv_rows(1 - core, kk, p).astype(BF16)
+
+        return w.send(q_send.at[p], q_recv.at[p], mate)
+
+    def ours(p):
+        @pl.loop(0, 4)
+        def _(kk):
+            q_keep[p, kk] = qkv_rows(core, kk, p)
+
+    moved = []
+
+    def pieces(p, copy):
         copy.wait_recv()
 
-    def qkv_rows(which, k):
-        cols = pl.ds(pl.multiple_of((2 * k + which) * piece, piece), piece)
-        return tn(xs[:, :, cols].reshape(4 * toks, piece), grads[...].reshape(4 * toks, 3 * share))
-
-    @pl.loop(0, 4)
-    def _(k):
-        q_send[k] = qkv_rows(1 - core, k).astype(BF16)
-
-    q_copy = w.send(q_send, q_recv, mate)
-    early.collect((0,))
-
-    @pl.loop(0, 4)
-    def _(k):
-        q_keep[k] = qkv_rows(core, k)
-
-    early.collect((1,))
-    q_copy.wait_recv()
-
-    @pl.loop(0, 4)
-    def _(k):
-        q_piece[k] = (q_keep[k] + q_recv[k].astype(F32)).astype(BF16)
-
-    moved = []
-    for m in (6, 2, 4):
-        peer = lax.bitwise_xor(own, m)
-        for p in range(3):
-            dst = z_own.at[:, pl.ds(pl.multiple_of(p * width + chip * share, share), share)]
-            moved.append(w.send(q_piece.at[lax.bitwise_xor(chip, m // 2), :, pl.ds(p * share, share)], dst, peer))
-    for p in range(3):
-        z_own[:, pl.ds(pl.multiple_of(p * width + chip * share, share), share)] = q_piece[chip, :, pl.ds(p * share, share)]
+        @pl.loop(0, 4)
+        def _(kk):
+            q_piece[p, kk] = (q_keep[p, kk] + q_recv[p, kk].astype(F32)).astype(BF16)
+
+        cols = rows_of(chip, share)
+        moved.append([w.send(q_piece.at[p, lax.bitwise_xor(chip, m // 2)], l_own.at[p, :, cols], lax.bitwise_xor(own, m)) for m in (6, 2, 4)])
+        l_own[p, :, cols] = q_piece[p, chip]
+
+    def line_start(p):
+        for copy in moved[p]:
+            copy.wait_recv()
+        lines[p].start()
+
+    swaps[0].wait_recv()
+    copies = [theirs(0)]
+    ours(0)
+    upout_line.collect((3,))
+    upout_line.total((1,))
+    swaps[1].wait_recv()
+    copies.append(theirs(1))
+    pieces(0, copies[0])
+    upout_line.collect((4,))
+    upout_line.total((2,))
+    ours(1)
+    swaps[2].wait_recv()
+    copies.append(theirs(2))
+    upout_line.collect((5,))
+    upout_line.total((3,))
+    pieces(1, copies[1])
+    ours(2)
+    upout_line.collect((6,))
+    upout_line.total((4,))
+    pieces(2, copies[2])
     vec_step(0)
 
-    def partial(k):
+    def partial(kk):
         @pl.loop(0, width // tile)
         def _(n):
             cols = rows_of(n, tile)
-            part[k, :, cols] = nt(grads[k], w_full[cols, :]).astype(BF16)
+            part[kk, :, cols] = nt(grads[kk], w_full[cols, :]).astype(BF16)
 
     gather = Gather(w, part, side, last, half)
     partial(gather.cd)
     gather.send_diagonal()
-    early.collect((2,))
-    early.total((0,))
+    line_start(0)
     partial(gather.cx)
     gather.send_x()
+    line_start(1)
+    upout_line.collect((7,))
+    upout_line.total((5, 6))
     partial(gather.cy)
     gather.send_y()
-    early.collect((3,))
-    early.total((1,))
+    line_start(2)
     partial(chip)
+    upout_line.collect((8,))
+    upout_line.total((7,))
     vec_step(1)
-    for copy in moved:
-        copy.wait_recv()
-    late = Line(w, z_own, z_in, z_far, CHUNKS)
-    late.start()
-    early.collect((4,))
-    early.total((2,))
+    upout_line.collect((9,))
     gather.relay()
+    upout_line.total((8, 9))
     vec_step(2)
-    early.collect((5, 6))
-    early.total((3, 4))
     step = 32
 
     def final_rows(which, t):
         rows = pl.ds(pl.multiple_of(which * half + t * step, step), step)
         input_grad[rows, :] = (branch_grad[rows, :] + gather.total(which, t * step, step)).astype(BF16)
 
+    order = [(p, i) for p in range(3) for i in range(4)]
+
+    def hop(at):
+        if at < len(order):
+            lines[order[at][0]].collect((order[at][1],))
+        if at >= 2:
+            lines[order[at - 2][0]].total((order[at - 2][1],))
+
+    for at in range(5):
+        hop(at)
+    vec_step(3)
     gather.wait_first()
     pl.loop(0, half // step)(functools.partial(final_rows, 0))
-    vec_step(3)
-    early.collect((7,))
-    early.total((5,))
+    for at in range(5, 8):
+        hop(at)
+    vec_step(4)
     gather.wait_second()
     pl.loop(0, half // step)(functools.partial(final_rows, 1))
-    vec_step(4)
-    early.collect((8, 9))
-    early.total((6, 7))
-    late.collect((0,))
-    early.total((8,))
-    late.collect((1,))
-    early.total((9,))
-    for i in range(2, CHUNKS):
-        late.collect((i,))
-        late.total((i - 2,))
-    late.total((CHUNKS - 2, CHUNKS - 1))
-    for m in range(4):
-        for i in (2 * m, 2 * m + 1):
-            early.arrive((i,))
-        up_total[:, rows_of(lax.bitwise_xor(chip, m), width)] = y_in[m * piece : (m + 1) * piece, :].astype(F32) * grad_scale
-    early.arrive((8, 9))
-    out_total[...] = y_in[4 * piece :, :].astype(F32) * grad_scale
-    for i in range(CHUNKS):
-        late.arrive((i,))
-        rows = late.rows[i]
-        qkv_total[rows, :] = z_in[rows, :].astype(F32) * grad_scale
-    early.finish()
-    late.finish()
+    for at in range(8, len(order) + 2):
+        hop(at)
+    down_line.arrive(range(8))
+    upout_line.arrive(range(10))
+    for line in lines:
+        line.arrive(range(4))
+    for line in [down_line, upout_line] + lines:
+        line.finish()
     w.finish()
 
 
-def finish(grad_scale, dq, dk, dv, xs, w_full, branch_grad, vec, keep, got_x, got_y, got_d):
+def backward(scale, seg, q, k, v, g, o, lse, xs, w_full, branch_grad, vec, down, keep, to_x, to_y, to_d):
     toks, width = branch_grad.shape
-    piece = w_full.shape[0] // 8
+    length, head_cols = q.shape
+    piece = keep.shape[1]
+    share = width // 4
     half = toks // 2
     shape = jax.ShapeDtypeStruct
     vm = pltpu.VMEM
-    line = vm((piece, 3 * width), BF16)
+    small = vm((3, 4, piece, share), BF16)
     five = vm((5 * piece, width), BF16)
+    line = vm((3, piece, width), BF16)
     return pl.pallas_call(
-        functools.partial(finish_body, grad_scale),
-        name="finish",
+        functools.partial(backward_body, scale),
+        name="backward",
         out_shape=(
-            shape((toks, width), BF16), shape((piece, 3 * width), F32), shape((piece, width), F32), shape((piece, 4 * width), F32),
-            shape((4, width), F32), shape((1, 4 * width), F32), shape((2, width), F32), shape((2, width), F32),
+            shape((toks, width), BF16), shape((3, piece, width), BF16), shape((5 * piece, width), BF16), shape(down.shape, BF16), shape(vec.shape, F32),
         ),
-        in_specs=[VM] * 11,
-        out_specs=(VM,) * 8,
+        in_specs=[VM] * 16,
+        out_specs=(VM,) * 5,
         scratch_shapes=[
-            vm((4, toks, 3 * width // 4), BF16),
+            vm((8, length), F32), vm((head_cols, length), BF16), vm((length, head_cols), F32), vm((length, head_cols), F32),
+            vm((head_cols, BQ), F32), vm((length, 128), F32), vm((3, 2, 4, toks, head_cols), BF16),
+            vm((4, toks, 3 * share), BF16),
             vm((4, toks, width), BF16), vm((4, half, width), BF16), vm((2, half, width), BF16),
-            vm((4, piece, 3 * width // 4), BF16), vm((4, piece, 3 * width // 4), BF16), vm((4, piece, 3 * width // 4), F32),
-            vm((4, piece, 3 * width // 4), BF16),
-            line, line, line, five, five, five,
+            small, small, vm((3, 4, piece, share), F32), small, line, line,
+            vm(down.shape, BF16), vm(down.shape, BF16), vm((3, 2, piece, width), BF16), five, five,
             vm(vec.shape, F32), vm((9,) + vec.shape, F32),
-            pltpu.SemaphoreType.DMA((96,)), pltpu.SemaphoreType.DMA((96,)), pltpu.SemaphoreType.DMA((8,)),
+            pltpu.SemaphoreType.DMA((160,)), pltpu.SemaphoreType.DMA((160,)), pltpu.SemaphoreType.DMA((8,)),
         ],
-        compiler_params=pltpu.CompilerParams(collective_id=2, has_side_effects=True, vmem_limit_bytes=48 << 20),
-    )(dq, dk, dv, xs, w_full, branch_grad, vec, keep, got_x, got_y, got_d)
+        compiler_params=pltpu.CompilerParams(collective_id=2, has_side_effects=True, vmem_limit_bytes=34 << 20),
+    )(seg, q, k, v, g, o, lse, xs, w_full, branch_grad, vec, down, keep, to_x, to_y, to_d)
+
+
+def emit_body(
+    grad_scale, who, low, grad, qkv_sum, upout_sum, down_sum, vec_sum,
+    output, input_grad, qkv_total, out_total, up_total, down_total, bias_total, hidden_total, gain_total, shift_total,
+):
+    width = low.shape[1]
+    piece = qkv_sum.shape[1]
+    output[...] = low[...]
+    input_grad[...] = grad[...]
+    for p in range(3):
+        qkv_total[:, p * width : (p + 1) * width] = qkv_sum[p].astype(F32) * grad_scale
+    chip = who[0]
+    for m in range(4):
+        up_total[:, rows_of(lax.bitwise_xor(chip, m), width)] = upout_sum[m * piece : (m + 1) * piece, :].astype(F32) * grad_scale
+    out_total[...] = upout_sum[4 * piece :, :].astype(F32) * grad_scale
+    down_total[...] = down_sum[...].astype(F32) * grad_scale
+    bias_total[...] = vec_sum[0:4] * grad_scale
+    gain_total[...] = vec_sum[4:6] * grad_scale
+    shift_total[...] = vec_sum[6:8] * grad_scale
+    for kk in range(4):
+        hidden_total[:, kk * width : (kk + 1) * width] = vec_sum[8 + kk : 9 + kk] * grad_scale
+
+
+def emit(grad_scale, who, low, grad, qkv_sum, upout_sum, down_sum, vec_sum):
+    toks, width = low.shape
+    piece = qkv_sum.shape[1]
+    shape = jax.ShapeDtypeStruct
+    return pl.pallas_call(
+        functools.partial(emit_body, grad_scale),
+        name="emit",
+        out_shape=(
+            shape((toks, width), BF16), shape((toks, width), BF16), shape((piece, 3 * width), F32), shape((piece, width), F32), shape((piece, 4 * width), F32),
+            shape(down_sum.shape, F32), shape((4, width), F32), shape((1, 4 * width), F32), shape((2, width), F32), shape((2, width), F32),
+        ),
+        in_specs=[SM] + [VM] * 6,
+        out_specs=(VM,) * 10,
+        compiler_params=pltpu.CompilerParams(vmem_limit_bytes=32 << 20),
+    )(who, low, grad, qkv_sum, upout_sum, down_sum, vec_sum)
 
 
 def local_tensor(tokens, segment_ids, qkv_weight, out_weight, up_weight, down_weight, proj_bias, hidden_bias, norm_gain, norm_shift, cotangent):
@@ -1076,13 +1126,14 @@
     grad_scale = (toks * lax.axis_size("fsdp") * lax.axis_size("rep")) ** (-0.5)
     queries, key_rows, value_rows, xs, w_full, upout = project(inputs, qkv_weight, up_weight, out_weight, proj_bias)
     attended, attended_low, lse = attn_fwd(scale, segment_ids, queries, key_rows, value_rows)
-    output, branch_grad, grad_heads, vec, down_total, keep, to_x, to_y, to_d = middle(
-        grad_scale, attended_low, inputs, cotangent[0], upout, down_weight, proj_bias, hidden_bias[None], norm_gain, norm_shift
-    )
-    got_x, got_y, got_d = (lax.ppermute(block, "fsdp", [(i, i ^ m) for i in range(8)]) for block, m in ((to_x, 2), (to_y, 4), (to_d, 6)))
-    query_grad, key_grad, value_grad = attn_bwd(scale, segment_ids, queries, key_rows, value_rows, grad_heads, attended, lse)
-    input_grad, qkv_total, out_total, up_total, bias_total, hidden_total, gain_total, shift_total = finish(
-        grad_scale, query_grad, key_grad, value_grad, xs, w_full, branch_grad, vec, keep, got_x, got_y, got_d
+    low, branch_grad, grad_heads, vec, down, keep, to_x, to_y, to_d = middle(
+        attended_low, inputs, cotangent[0], upout, down_weight, proj_bias, hidden_bias[None], norm_gain, norm_shift
+    )
+    grad, qkv_sum, upout_sum, down_sum, vec_sum = backward(
+        scale, segment_ids, queries, key_rows, value_rows, grad_heads, attended, lse, xs, w_full, branch_grad, vec, down, keep, to_x, to_y, to_d
+    )
+    output, input_grad, qkv_total, out_total, up_total, down_total, bias_total, hidden_total, gain_total, shift_total = emit(
+        grad_scale, (lax.axis_index("fsdp") // 2).reshape(1), low, grad, qkv_sum, upout_sum, down_sum, vec_sum
     )
     return (
         output[None],

time: 333 us -> 287 us (0.86)
  Pallas kernels: 310 us -> 277 us
  local copies, waits for them, and re-layouts: 16.8 us -> 10 us
  starting transfers between devices: 3.55 us -> 0 us
    pallas_call x3, Pallas kernels: 236 us -> 209 us  [the longest x1 104 us: middle(): pl.pallas_call(middle_body, name='middle', out_shape=(shape((toks, width)...]
    unnamed x46 -> x38, local copies, waits for them, and re-layouts: 16.8 us -> 10 us
    pallas_call x1, Pallas kernels: 50 us -> 43.7 us  [project(): pl.pallas_call(project_body, name='project', out_shape=(heads, heads, hea...]
    ppermute x3 -> x0, starting transfers between devices: 3.55 us -> none  [local_tensor(): lax.ppermute(block, 'fsdp', [(i, i ^ m) for i in range(8)])]
  transfers between devices with their start and end apart: 3 -> 0, of which waited for: 0 -> 0; matrix products, arithmetic and copies ran while one was open for 0% -> 0% of each run, Pallas kernels for 7% -> 0%
where the time goes in v4:
time: 287 us; the launch traced here: 288 us
  Pallas kernels  277 us (97%)
  local copies, waits for them, and re-layouts  10 us (3%)
    pallas_call x1, Pallas kernels, middle(): pl.pallas_call(middle_body, name='middle', out_shape=(shape((toks, width)...  104 us
    pallas_call x1, Pallas kernels, backward(): pl.pallas_call(functools.partial(backward_body, scale), name='backward',...  101 us
    pallas_call x1, Pallas kernels, project(): pl.pallas_call(project_body, name='project', out_shape=(heads, heads, hea...  43.7 us
    pallas_call x1, Pallas kernels, attn_fwd(): pl.pallas_call(functools.partial(attn_fwd_body, scale), name='attn_fwd',...  24.8 us
    unnamed x38, local copies, waits for them, and re-layouts  10 us

profile of v4, /device:TPU:0, one launch (start us, length us, event | category | flops | bytes accessed | tf_op | source)
XLA Modules:
  0.0 288.0 jit_solution(12334531184081013475)
XLA Ops:
  0.6 0.0 copy-start
  0.7 1.0 copy-done
  1.7 1.2 copy-done.2
  2.9 1.1 copy-done.4
  4.0 0.9 copy-done.12
  5.0 0.7 copy-done.13
  5.7 43.7 %project.1 = (bf16[2048,128]{1,0:T(8,128)(2,1)S(1)}, bf16[2048,128]{1,0:T(8,128)(2,1)S(1)}, bf16[2048,128]{1,0:T(8,128)(2,1)S(1)}, bf16[4,256,1024]{2,1,0:T(8,12...) custom-call(bf16[256,1024]{1,0:T(8,128)(2,1)S(1)} %bitcast.7, ...), custom_call_target="tpu_custom_call" | custom-call | tf_op jit(solution)/shard_map/project/pallas_call | solution.py:784
  49.5 0.0 copy-start.1
  49.5 0.0 copy-start.3
  49.5 0.0 copy-start.5
  49.5 0.0 copy-start.14
  49.5 0.0 copy-start.15
  49.5 0.0 copy-start.16
  49.5 0.0 copy-start.17
  49.5 24.8 %attn_fwd.1 = (f32[2048,128]{1,0:T(8,128)S(1)}, bf16[2048,128]{1,0:T(8,128)(2,1)S(1)}, f32[8,2048]{1,0:T(8,128)S(1)}) custom-call(s32[1,2048]{1,0:T(1,128)S(1)} %copy-done.18, s32[1,2048]{1,0:T(1,128)S(1)} %copy-done.18, bf16[2048,128]{1,0:T(8,128)(2,1)S(1)} %get-tuple-element.43.q_ref.q, bf16[2048,128]{1,0:T(8,128)(2,1)S(1)} %get-tuple-element.44.k_ref.k, ...), custom_call_target="tpu_custom_call" | custom-call | flops 2147483648 | bytes 1572864 | tf_op jit(solution)/shard_map/attn_fwd/pallas_call | solution.py:140
  74.3 0.0 copy-done.1
  74.3 0.0 copy-done.3
  74.3 0.0 copy-done.5
  74.4 0.0 copy-done.14
  74.4 0.0 copy-done.15
  74.4 0.0 copy-done.16
  74.4 0.0 copy-done.17
  74.4 103.7 %middle.1 = (bf16[256,1024]{1,0:T(8,128)(2,1)S(1)}, f32[256,1024]{1,0:T(8,128)S(1)}, bf16[2048,128]{1,0:T(8,128)(2,1)S(1)}, f32[16,1024]{1,0:T(8,128)S(1)}, bf16...) custom-call(bf16[2048,128]{1,0:T(8,128)(2,1)S(1)} %get-tuple-element, ...), custom_call_target="tpu_custom_call" | custom-call | tf_op jit(solution)/shard_map/middle/pallas_call | solution.py:665
  178.1 0.0 copy-start.10
  178.1 0.8 copy-done.10
  178.9 1.2 copy-done.11
  180.1 101.4 %backward.1 = (bf16[256,1024]{1,0:T(8,128)(2,1)S(1)}, bf16[3,128,1024]{2,1,0:T(8,128)(2,1)S(1)}, bf16[640,1024]{1,0:T(8,128)(2,1)S(1)}, bf16[512,1024]{1,0:T(8,128)(2,1)S(1)}, f32[16,1024]{1,0:T(8,128)S(1)}) custom-call(s32[1,2048]{1,0:T(1,128)S(1)} %copy-done.18, bf16[2048,128]{1,0:T(8,128)(2,1)S(1)} %get-tuple-element.43.q_ref.q, ...), custom_call_target="tpu_custom_call" | custom-call | tf_op jit(solution)/shard_map/backward/pallas_call | solution.py:1061
  281.6 0.0 copy-start.8
  281.6 0.8 copy-done.8
  282.4 1.0 copy-done.7
  283.4 1.0 copy-done.9
  284.4 3.5 %emit.1 = (bf16[256,1024]{1,0:T(8,128)(2,1)}, bf16[256,1024]{1,0:T(8,128)(2,1)}, f32[128,3072]{1,0:T(8,128)}, f32[128,1024]{1,0:T(8,128)}, f32[128,4096]{1,0:T(8...) custom-call(s32[1]{0:T(128)} %bitcast.who, ...), custom_call_target="tpu_custom_call" | custom-call | tf_op jit(solution)/shard_map/emit/pallas_call | solution.py:1109
  (11 shorter events, 0.0 us)
Async XLA Ops:
  0.6 1.0 copy-start
  1.7 1.2 copy-start.2
  2.9 1.1 copy-start.4
  4.0 0.9 copy-start.12
  5.0 0.7 copy-start.13
  5.7 43.7 %copy-start.18 = (s32[1,2048]{1,0:T(1,128)S(1)}, s32[1,2048]{1,0:T(1,128)}, u32[]{:S(2)}) copy-start(s32[1,2048]{1,0:T(1,128)} %seg.1) | copy-start | bytes 24580
  49.5 24.9 %copy-start.1 = (bf16[1,256,1024]{2,1,0:T(8,128)(2,1)S(1)}, bf16[1,256,1024]{2,1,0:T(8,128)(2,1)}, u32[]{:S(2)}) copy-start(bf16[1,256,1024]{2,1,0:T(8,128)(2,1)} %param.11) | copy-start | bytes 1572868
  49.5 24.9 %copy-start.3 = (bf16[512,1024]{1,0:T(8,128)(2,1)S(1)}, bf16[512,1024]{1,0:T(8,128)(2,1)}, u32[]{:S(2)}) copy-start(bf16[512,1024]{1,0:T(8,128)(2,1)} %down_w.1) | copy-start | bytes 3145732
  49.5 24.9 %copy-start.5 = (bf16[1,256,1024]{2,1,0:T(8,128)(2,1)S(1)}, bf16[1,256,1024]{2,1,0:T(8,128)(2,1)}, u32[]{:S(2)}) copy-start(bf16[1,256,1024]{2,1,0:T(8,128)(2,1)} %param.21) | copy-start | bytes 1572868
  49.5 24.9 %copy-start.14 = (f32[4,1024]{1,0:T(4,128)S(1)}, f32[4,1024]{1,0:T(4,128)}, u32[]{:S(2)}) copy-start(f32[4,1024]{1,0:T(4,128)} %proj_bias.3) | copy-start | bytes 49156
  49.5 24.9 %copy-start.15 = (f32[4096]{0:T(1024)S(1)}, f32[4096]{0:T(1024)}, u32[]{:S(2)}) copy-start(f32[4096]{0:T(1024)} %param.18) | copy-start | bytes 49156
  49.5 24.9 %copy-start.16 = (f32[2,1024]{1,0:T(2,128)S(1)}, f32[2,1024]{1,0:T(2,128)}, u32[]{:S(2)}) copy-start(f32[2,1024]{1,0:T(2,128)} %gain.1) | copy-start | bytes 24580
  49.5 24.9 %copy-start.17 = (f32[2,1024]{1,0:T(2,128)S(1)}, f32[2,1024]{1,0:T(2,128)}, u32[]{:S(2)}) copy-start(f32[2,1024]{1,0:T(2,128)} %shift.1) | copy-start | bytes 24580
  178.1 0.8 copy-start.10
  178.9 102.6 %copy-start.6 = (bf16[256,1024]{1,0:T(8,128)(2,1)}, bf16[256,1024]{1,0:T(8,128)(2,1)S(1)}, u32[]{:S(2)}) copy-start(bf16[256,1024]{1,0:T(8,128)(2,1)S(1)} %get-tuple-element.48.low) | copy-start | bytes 1572868
  178.9 1.2 copy-start.11
  281.6 0.8 copy-start.8
  282.4 1.0 copy-start.7
  283.4 1.0 copy-start.9

commit v5 on v4

--- a/solution.py
+++ b/solution.py
@@ -25,17 +25,6 @@
     return jnp.dot(a, b, preferred_element_type=jnp.float32)
 
 
-def block_range(seg_s, start, size, blk, n):
-    first = seg_s[0, start]
-    last = seg_s[0, start + size - 1]
-    lo = jnp.int32(0)
-    hi = jnp.int32(0)
-    for j in range(n):
-        lo = lo + (seg_s[0, j * blk + blk - 1] < first).astype(jnp.int32)
-        hi = hi + (seg_s[0, j * blk] <= last).astype(jnp.int32)
-    return lo, hi
-
-
 def head_lanes(shape, half):
     return lax.broadcasted_iota(jnp.int32, shape, 1) < half
 
@@ -55,102 +44,6 @@
 
 def wide(column, lanes):
     return jnp.concatenate([column] * (lanes // 128), axis=1)
-
-
-def attn_fwd_body(scale, seg_s, seg_v, q_ref, k_ref, v_ref, o_ref, a_ref, lse_ref, vt, seg_c):
-    length, width = q_ref.shape
-    half = width // 2
-    n = length // BQ
-    first = head_lanes((BQ, width), half)
-    seg_columns(seg_v, seg_c)
-
-    @pl.loop(0, n)
-    def _(i):
-        rows = rows_of(i, BQ)
-        t = jnp.transpose(v_ref[rows, :])
-        for h in range(2):
-            vt[h, 0:half, rows] = t[h * half : (h + 1) * half]
-            vt[h, half : half + 16, rows] = jnp.ones((16, BQ), jnp.bfloat16)
-
-    sides = []
-    heads = (lax.broadcasted_iota(jnp.int32, (16, width), 1) < half) == (lax.broadcasted_iota(jnp.int32, (16, width), 0) < 8)
-    heads = heads.astype(jnp.float32).astype(jnp.bfloat16)
-    for ref in (q_ref, k_ref):
-        squares = nt(heads, ref[...] * ref[...])
-        sides.append((jnp.max(squares[0:8]), jnp.max(squares[8:16])))
-    bound = (40.0 / scale) ** 2
-    small = jnp.logical_and(sides[0][0] * sides[1][0] <= bound, sides[0][1] * sides[1][1] <= bound)
-
-    @pl.loop(0, n)
-    def _(i):
-        lo, hi = block_range(seg_s, i * BQ, BQ, BK, length // BK)
-        rows = rows_of(i, BQ)
-        q = q_ref[rows, :] * jnp.bfloat16(scale)
-        zero = jnp.zeros_like(q)
-        qs = (jnp.where(first, q, zero), jnp.where(first, zero, q))
-        seg_q = seg_v[:, rows].astype(jnp.float32)
-
-
-        def masked(cols, h):
-            same = wide(seg_c[cols, :], BQ) == seg_q
-            return jnp.where(same, nt(k_ref[cols, :], qs[h]), NEGATIVE)
-
-        def store(tops, accs):
-            o = []
-            for h in range(2):
-                total = accs[h][half : half + 1]
-                o.append(accs[h][0:half] / total)
-                lse_ref[h : h + 1, rows] = tops[h] + jnp.log(total)
-            o = jnp.transpose(jnp.concatenate(o, axis=0))
-            o_ref[rows, :] = o
-            a_ref[rows, :] = o.astype(jnp.bfloat16)
-
-        def direct(count):
-            base = jnp.minimum(lo, length // BK - count)
-            accs = [jnp.zeros((half + 16, BQ), jnp.float32)] * 2
-            for j in range(count):
-                cols = rows_of(base + j, BK)
-                for h in range(2):
-                    accs[h] = accs[h] + nn(vt[h, :, cols], jnp.exp(masked(cols, h)).astype(jnp.bfloat16))
-            store([jnp.zeros((1, BQ), jnp.float32)] * 2, accs)
-
-        def running():
-            def step(j, state):
-                cols = rows_of(j, BK)
-                out = []
-                for h in range(2):
-                    m, acc = state[h]
-                    s = masked(cols, h)
-                    top = jnp.maximum(m, jnp.max(s, axis=0, keepdims=True))
-                    p = jnp.exp(s - top).astype(jnp.bfloat16)
-                    out.append((top, acc * jnp.exp(m - top) + nn(vt[h, :, cols], p)))
-                return tuple(out)
-
-            one = (jnp.full((1, BQ), NEGATIVE, jnp.float32), jnp.zeros((half + 16, BQ), jnp.float32))
-            state = lax.fori_loop(lo, hi, step, (one, one))
-            store([state[h][0] for h in range(2)], [state[h][1] for h in range(2)])
-
-        for count in range(1, length // BK + 1):
-            pl.when(jnp.logical_and(small, hi - lo == count))(functools.partial(direct, count))
-        pl.when(jnp.logical_not(small))(running)
-
-
-def attn_fwd(scale, seg, q, k, v):
-    length, width = q.shape
-    return pl.pallas_call(
-        functools.partial(attn_fwd_body, scale),
-        name="attn_fwd",
-        out_shape=(
-            jax.ShapeDtypeStruct((length, width), jnp.float32),
-            jax.ShapeDtypeStruct((length, width), jnp.bfloat16),
-            jax.ShapeDtypeStruct((8, length), jnp.float32),
-        ),
-        in_specs=[SM, VM, VM, VM, VM],
-        out_specs=(VM, VM, VM),
-        scratch_shapes=[pltpu.VMEM((2, width // 2 + 16, length), jnp.bfloat16), pltpu.VMEM((length, 128), jnp.float32)],
-        compiler_params=pltpu.CompilerParams(vmem_limit_bytes=32 << 20),
-        cost_estimate=pl.CostEstimate(flops=4 * length * length * width, bytes_accessed=6 * length * width, transcendentals=2 * length * length),
-    )(seg, seg, q, k, v)
 
 
 MESH = pl.DeviceIdType.MESH
@@ -202,16 +95,21 @@
             pl.semaphore_signal(barrier, inc=1, device_id=(rep, peer), device_id_type=MESH)
         pl.semaphore_wait(barrier, len(peers))
 
+    def drain(self, copies):
+        for copy in copies:
+            copy.wait_send()
+            self.sent = [other for other in self.sent if other is not copy]
+
     def finish(self):
         for copy in self.sent:
             copy.wait_send()
 
 
 class Line:
-    def __init__(self, wires, own, land, far, count):
+    def __init__(self, wires, own, land, far, count, size=None):
         self.own, self.land, self.far = own, land, far
         rep, dev = wires.rep, wires.own
-        size = own.shape[0] // count
+        size = own.shape[0] // count if size is None else size
         self.rows = [pl.ds(i * size, size) for i in range(count)]
         self.inner = jnp.logical_or(rep == 1, rep == 2)
         self.outer = jnp.logical_not(self.inner)
@@ -367,6 +265,11 @@
         add(self.cx, self.half, 3)
         self.x_last = self.wires.send(self.part.at[self.cx, self.b], self.last.at[1], self.x)
 
+    def drain(self):
+        for copy in (self.x_own, self.y_own, self.x_far, self.y_far, self.x_last, self.y_last):
+            copy.wait_send()
+            self.wires.sent = [other for other in self.wires.sent if other is not copy]
+
     def wait_first(self):
         self.x_own.wait_recv()
         self.y_last.wait_recv()
@@ -381,60 +284,179 @@
         return self.part[self.chip, rows, :].astype(F32) + self.side[which, here, :].astype(F32) + self.last[which, here, :].astype(F32)
 
 
-def middle_body(
-    heads, x, cot, upout, down_w, proj_bias, hidden_bias, gain, shift,
-    output, branch_grad, grad_heads, vec, down_grad, keep, to_x, to_y, to_d,
-    att, out_full, up_full, down_full, h1, z1, r1, gs, fl, act, slope, part, side, last, sl, pre, part2, side2, last2,
-    branch_low, agl, acc, d_send, d_recv, d_keep, u_send, u_recv, u_keep, o_send, o_recv, o_keep,
+def layer_body(
+    scale, seg, x, cot, qkv_w, up_w, out_w, down_w, proj_bias, hidden_bias, gain, shift,
+    h_output, h_input_grad, h_qkv, h_upout, h_down, h_vec,
+    q_out, k_out, v_out, o_out, lse, xs, w_full, output, branch_grad, grad_heads, vec, down_grad, sends,
+    stage, vt, seg_c, low, att, out_full, up_full, down_full, h1, z1, r1, fl, act, slope, part, side, last, sl, pre,
+    branch_low, agl, acc, d_send, d_recv, d_far, down_sum, u_send, u_recv, o_send, o_recv,
+    corr, dv_acc, dqt, q_send, q_recv, q_piece, l_own, l_far, got, y_own, y_far, upout_sum, qkv_sum, input_grad, v_sum, v_recv, vec_sum,
     send_sems, recv_sems, local_sems,
 ):
     w = Wires(send_sems, recv_sems, local_sems)
-    own = w.own
+    own, rep = w.own, w.rep
     core, chip = lax.rem(own, 2), own // 2
     mate = lax.bitwise_xor(own, 1)
     cx, cy, cd = (lax.bitwise_xor(chip, m) for m in (1, 2, 3))
+    others = (cd, cx, cy)
     toks, width = x.shape
     ff = up_full.shape[1]
-    head_width = heads.shape[1]
+    share = width // 4
+    head_width = share // 2
     half = toks // 2
-    piece = upout.shape[2]
+    piece = up_w.shape[0]
+    quarter = piece // 4
     tile = 256
     w.greet(
-        [(w.rep, lax.bitwise_xor(own, m)) for m in range(1, 8)] + [(lax.rem(w.rep + 1, 4), own), (lax.rem(w.rep + 3, 4), own)]
-    )
-
-    swaps = []
-    for m in (6, 2, 4, 1, 3, 5, 7):
-        peer = lax.bitwise_xor(own, m)
-        swaps.append(w.send(heads.at[rows_of(peer, toks)], att.at[:, rows_of(own, head_width)], peer))
-    quarter = piece // 4
-    some = rows_of(w.rep, quarter)
-
-    def up_piece(k, r):
-        return up_full.at[pl.ds(pl.multiple_of((2 * k + core) * piece + r * quarter, quarter), quarter)]
-
-    others = (cd, cx, cy)
-    seeds = [w.local(upout.at[k, 0, some], up_piece(k, w.rep)) for k in others]
-    hops = Hops(w, lambda r: [up_piece(k, r) for k in others])
-    weights = []
-    for k in range(4):
-        dst = rows_of(2 * k + core, piece)
-        weights.append((w.local(upout.at[k, 1], out_full.at[dst]), w.send(upout.at[k, 1], out_full.at[dst], mate)))
-    dst = rows_of(own, piece)
-    weights.append((w.local(upout.at[chip, 0], up_full.at[dst]), w.send(upout.at[chip, 0], up_full.at[dst], mate)))
-    dst = rows_of(core, ff // 2)
-    weights.append((w.local(down_w, down_full.at[dst]), w.send(down_w, down_full.at[dst], mate)))
-    for copy in seeds:
+        [(rep, lax.bitwise_xor(own, m)) for m in range(1, 8)]
+        + [(lax.bitwise_xor(rep, m), own) for m in (1, 2, 3)]
+    )
+
+    mine, some = rows_of(own, piece), rows_of(rep, quarter)
+
+    def quarter_of(full, k, r, cols=slice(None)):
+        return full.at[pl.ds(pl.multiple_of((2 * k + core) * piece + r * quarter, quarter), quarter), cols]
+
+    def qkv_cols(p, to_chip):
+        return pl.ds(pl.multiple_of(p * width + to_chip * share, share), share)
+
+    first_fetch = []
+    for mask in (6, 2, 4):
+        peer, to_chip = lax.bitwise_xor(own, mask), lax.bitwise_xor(chip, mask // 2)
+        for p in range(3):
+            first_fetch.append(w.send(qkv_w.at[some, qkv_cols(p, to_chip)], quarter_of(w_full, chip, rep, pl.ds(p * share, share)), peer))
+    xs[chip] = x[...]
+    spread0 = Spread(w, xs, half)
+    spread0.first_half()
+    spread0.second_half()
+    fetch = []
+    for mask in (6, 2, 4):
+        peer, to_chip = lax.bitwise_xor(own, mask), lax.bitwise_xor(chip, mask // 2)
+        fetch.append(w.send(up_w.at[some, rows_of(to_chip, ff)], quarter_of(up_full, chip, rep), peer))
+        fetch.append(w.send(out_w.at[some], quarter_of(out_full, chip, rep), peer))
+    here, there = [], []
+    for p in range(3):
+        src, dst = qkv_w.at[:, qkv_cols(p, chip)], w_full.at[mine, pl.ds(p * share, share)]
+        here.append(w.local(src, dst))
+        there.append(w.send(src, dst, mate))
+    kept = []
+    for src, dst in ((up_w.at[:, rows_of(chip, ff)], up_full.at[mine]), (out_w, out_full.at[mine]), (down_w, down_full.at[rows_of(core, ff // 2)])):
+        kept.append((w.local(src, dst), w.send(src, dst, mate)))
+    qkv_hops = Hops(w, lambda r: [quarter_of(w_full, k, r) for k in others])
+    hops = Hops(w, lambda r: [quarter_of(full, k, r) for full in (up_full, out_full) for k in others])
+    for copy in first_fetch:
+        copy.wait_recv()
+    qkv_hops.start(1)
+    seg_columns(seg, seg_c)
+    qkv_hops.wait(1)
+    qkv_hops.start(2)
+    spread0.relay()
+    qkv_hops.wait(2)
+    qkv_hops.start(3)
+    for copy in fetch:
+        copy.wait_recv()
+    hops.start(1)
+    qkv_hops.wait(3)
+    for k in others:
+        rows = rows_of(2 * k + core, piece)
+        there.append(w.send(w_full.at[rows], w_full.at[rows], mate))
+    for copy in here:
         copy.wait()
-    hops.start(1)
-    att[:, rows_of(own, head_width)] = heads[rows_of(own, toks), :]
+    for copy in there:
+        copy.wait_recv()
+
+    outs = (q_out, k_out, v_out)
+    trades = []
+
+    def block(k):
+        rows = rows_of(2 * k + core, toks)
+        for p in range(3):
+            r = nn(xs[k], w_full[:, pl.ds(p * share, share)])
+            if p != 1:
+                r = r + proj_bias[p // 2 : p // 2 + 1, rows_of(chip, share)]
+            stage[k, :, pl.ds(p * share, share)] = r.astype(BF16)
+            theirs = pl.ds(pl.multiple_of(p * share + (1 - core) * head_width, head_width), head_width)
+            trades.append(w.send(stage.at[k, :, theirs], outs[p].at[rows], mate))
+            outs[p][rows, :] = stage[k, :, pl.ds(pl.multiple_of(p * share + core * head_width, head_width), head_width)]
+
+    block(chip)
+    spread0.wait_sides()
+    block(cx)
+    block(cy)
     hops.wait(1)
     hops.start(2)
-    for copy in swaps:
+    spread0.wait_diagonal()
+    block(cd)
+    for copy in trades:
         copy.wait_recv()
-    for here, there in weights:
-        here.wait()
-        there.wait_recv()
+    w.drain(trades)
+
+    headd = head_width // 2
+    blocks = q_out.shape[0] // BQ
+    first = head_lanes((BQ, head_width), headd)
+
+    @pl.loop(0, blocks)
+    def _(i):
+        rows = rows_of(i, BQ)
+        t = jnp.transpose(v_out[rows, :])
+        for h in range(2):
+            vt[h, 0:headd, rows] = t[h * headd : (h + 1) * headd]
+            vt[h, headd : headd + 16, rows] = jnp.ones((16, BQ), BF16)
+
+    swaps = {}
+    for mask in range(1, 8):
+        peer = lax.bitwise_xor(own, mask)
+        swaps[mask] = w.remote(low.at[rows_of(peer, toks)], att.at[:, rows_of(own, head_width)], peer)
+
+    @pl.loop(0, blocks)
+    def _(t):
+        i = lax.bitwise_xor(own, 7 - t)
+        rows = rows_of(i, BQ)
+        qb = q_out[rows, :] * jnp.bfloat16(scale)
+        zero = jnp.zeros_like(qb)
+        qs = (jnp.where(first, qb, zero), jnp.where(first, zero, qb))
+        seg_q = seg[:, rows].astype(F32)
+        both = []
+        for h in range(2):
+            scores = []
+            for j in range(blocks):
+                cols = pl.ds(j * BQ, BQ)
+                same = wide(seg_c[cols, :], BQ) == seg_q
+                scores.append(jnp.where(same, nt(k_out[cols, :], qs[h]), NEGATIVE))
+            top = functools.reduce(jnp.maximum, [jnp.max(s, axis=0, keepdims=True) for s in scores])
+            total = jnp.zeros((headd + 16, BQ), F32)
+            for j in range(blocks):
+                total = total + nn(vt[h, :, pl.ds(j * BQ, BQ)], jnp.exp(scores[j] - top).astype(BF16))
+            norm = total[headd : headd + 1]
+            both.append(total[0:headd] / norm)
+            lse[h : h + 1, rows] = top + jnp.log(norm)
+        out = jnp.transpose(jnp.concatenate(both, axis=0))
+        o_out[rows, :] = out
+        low[rows, :] = out.astype(BF16)
+        for mask in range(1, 8):
+
+            @pl.when(t == 7 - mask)
+            def _(mask=mask):
+                swaps[mask].start()
+
+        @pl.when(t == 2)
+        def _():
+            hops.wait(2)
+            hops.start(3)
+
+    w.sent.extend(swaps.values())
+    att[:, rows_of(own, head_width)] = low[rows_of(own, toks), :]
+    hops.wait(3)
+    for k in others:
+        rows = rows_of(2 * k + core, piece)
+        for full in (out_full, up_full):
+            kept.append((None, w.send(full.at[rows], full.at[rows], mate)))
+    for local, remote in kept:
+        if local is not None:
+            local.wait()
+        remote.wait_recv()
+    for copy in swaps.values():
+        copy.wait_recv()
 
     @pl.loop(0, width // tile)
     def _(n):
@@ -443,8 +465,6 @@
 
     step = 32
     acc[...] = jnp.zeros_like(acc)
-    hops.wait(2)
-    hops.start(3)
 
     def first_rows(t):
         rows = rows_of(t, step)
@@ -467,21 +487,15 @@
         def _(n):
             cols = rows_of(n, tile)
             hidden = nn(fl[k], up_full[:, cols]) + hidden_bias[:, pl.ds(pl.multiple_of(chip * ff + n * tile, tile), tile)]
-            slope[k, :, cols] = hidden
-            act[k, :, cols] = (hidden * (0.5 * (1.0 + lax.erf(hidden * (2.0**-0.5))))).astype(BF16)
+            cdf = 0.5 * (1.0 + lax.erf(hidden * (2.0**-0.5)))
+            act[k, :, cols] = (hidden * cdf).astype(BF16)
+            slope[k, :, cols] = (cdf + hidden * (jnp.exp(-0.5 * hidden * hidden) * ((2.0 * math.pi) ** -0.5))).astype(BF16)
 
         @pl.loop(0, width // tile)
         def _(n):
             cols = rows_of(n, tile)
             part[k, :, cols] = nn(act[k], down_full[:, cols]).astype(BF16)
 
-    hops.wait(3)
-    passed = []
-    for k in others:
-        dst = rows_of(2 * k + core, piece)
-        passed.append(w.send(up_full.at[dst], up_full.at[dst], mate))
-    for copy in passed:
-        copy.wait_recv()
     forward(chip)
     gather = Gather(w, part, side, last, half)
     spread.relay()
@@ -494,19 +508,7 @@
     forward(cd)
     gather.send_diagonal()
 
-    def slopes(k):
-        @pl.loop(0, toks // 32)
-        def _(t):
-            rows = rows_of(t, 32)
-            hidden = slope[k, rows, :]
-            cdf = 0.5 * (1.0 + lax.erf(hidden * (2.0**-0.5)))
-            slope[k, rows, :] = cdf + hidden * (jnp.exp(-0.5 * hidden * hidden) * ((2.0 * math.pi) ** -0.5))
-
-    slopes(0)
-    slopes(1)
     gather.relay()
-    slopes(2)
-    slopes(3)
 
     def second_rows(which, t):
         rows = pl.ds(pl.multiple_of(which * half + t * step, step), step)
@@ -518,7 +520,7 @@
         c = cot[rows, :].astype(F32)
         e = c * gain[1:2, :]
         grad = inv * (e - jnp.mean(e, axis=1, keepdims=True) - z * jnp.mean(e * z, axis=1, keepdims=True))
-        gs[rows, :] = grad
+        h1[rows, :] = grad
         low = grad.astype(BF16)
         sl[chip, rows, :] = low
         acc[0] += fold_rows(c * z)
@@ -537,7 +539,7 @@
         @pl.loop(0, ff // tile)
         def _(n):
             cols = rows_of(n, tile)
-            grad = nt(sl[k], down_full[cols, :]) * slope[k, :, cols]
+            grad = nt(sl[k], down_full[cols, :]) * slope[k, :, cols].astype(F32)
             low = grad.astype(BF16)
             pre[k, :, cols] = low
             acc[3, :, cols] += fold_rows(low.astype(F32))
@@ -545,10 +547,11 @@
         @pl.loop(0, width // tile)
         def _(n):
             cols = rows_of(n, tile)
-            part2[k, :, cols] = nt(pre[k], up_full[cols, :]).astype(BF16)
-
+            part[k, :, cols] = nt(pre[k], up_full[cols, :]).astype(BF16)
+
+    gather.drain()
     backward(chip)
-    gather2 = Gather(w, part2, side2, last2, half)
+    gather2 = Gather(w, part, side, last, half)
     spread2.relay()
     spread2.wait_sides()
     backward(cx)
@@ -569,18 +572,16 @@
         d_send[rows_of(n, tile), :] = down_rows(1 - core, n).astype(BF16)
 
     d_copy = w.send(d_send, d_recv, mate)
+    d_copy.wait_recv()
 
     @pl.loop(0, ff // 2 // tile)
     def _(n):
-        d_keep[rows_of(n, tile), :] = down_rows(core, n)
-
+        rows = rows_of(n, tile)
+        down_grad[rows, :] = (down_rows(core, n) + d_recv[rows, :].astype(F32)).astype(BF16)
+
+    down_line = Line(w, down_grad, down_sum, d_far, 8)
+    down_line.start()
     gather2.relay()
-    d_copy.wait_recv()
-
-    @pl.loop(0, ff // 2 // 64)
-    def _(t):
-        rows = rows_of(t, 64)
-        down_grad[rows, :] = (d_keep[rows, :] + d_recv[rows, :].astype(F32)).astype(BF16)
 
     def up_rows(which, k):
         cols = pl.ds(pl.multiple_of((2 * k + which) * piece, piece), piece)
@@ -592,10 +593,11 @@
         u_send[k] = up_rows(1 - core, k).astype(BF16)
 
     u_copy = w.send(u_send, u_recv, mate)
+    down_line.collect((0,))
 
     def branch_rows(which, t):
         rows = pl.ds(pl.multiple_of(which * half + t * step, step), step)
-        grad = gs[rows, :] + gather2.total(which, t * step, step)
+        grad = h1[rows, :] + gather2.total(which, t * step, step)
         z = z1[rows, :]
         e = grad * gain[0:1, :]
         out = r1[rows, 0:1] * (e - jnp.mean(e, axis=1, keepdims=True) - z * jnp.mean(e * z, axis=1, keepdims=True))
@@ -608,6 +610,7 @@
 
     gather2.wait_first()
     pl.loop(0, half // step)(functools.partial(branch_rows, 0))
+    down_line.collect((1,))
     gather2.wait_second()
     pl.loop(0, half // step)(functools.partial(branch_rows, 1))
 
@@ -622,6 +625,25 @@
         backs.append(w.send(agl.at[:, rows_of(peer, head_width)], grad_heads.at[rows_of(own, toks)], peer))
     grad_heads[rows_of(own, toks), :] = agl[:, rows_of(own, head_width)]
 
+    down_line.collect((2,))
+    down_line.total((0,))
+    u_copy.wait_recv()
+    spread_up, spread_out = [], []
+
+    def up_piece(m):
+        k = lax.bitwise_xor(chip, m)
+        return (up_rows(core, k) + u_recv[k].astype(F32)).astype(BF16)
+
+    y_own[0:piece, :] = up_piece(0)
+    y_own[piece : 2 * piece, :] = up_piece(3)
+    up_line = Line(w, y_own.at[pl.ds(0, 2 * piece)], upout_sum.at[pl.ds(0, 2 * piece)], y_far.at[pl.ds(0, 2 * piece)], 4)
+    up_line.start()
+    for i, m in ((1, 1), (2, 2)):
+        sends[i, 0] = up_piece(m)
+        spread_up.append(w.send(sends.at[i, 0], got.at[i, 0], lax.bitwise_xor(own, 2 * m)))
+    down_line.collect((3,))
+    down_line.total((1,))
+
     def out_rows(which, k):
         cols = pl.ds(pl.multiple_of((2 * k + which) * piece, piece), piece)
         return tn(att[:, cols], branch_low[...])
@@ -631,18 +653,15 @@
         o_send[k] = out_rows(1 - core, k).astype(BF16)
 
     o_copy = w.send(o_send, o_recv, mate)
-
-    @pl.loop(0, 4)
-    def _(k):
-        u_keep[k] = up_rows(core, k)
-        o_keep[k] = out_rows(core, k)
-
-    u_copy.wait_recv()
     o_copy.wait_recv()
-    for m, ref in enumerate((keep, to_x, to_y, to_d)):
+    for i, m in enumerate((3, 1, 2, 0)):
         k = lax.bitwise_xor(chip, m)
-        ref[0] = (u_keep[k] + u_recv[k].astype(F32)).astype(BF16)
-        ref[1] = (o_keep[k] + o_recv[k].astype(F32)).astype(BF16)
+        sends[i, 1] = (out_rows(core, k) + o_recv[k].astype(F32)).astype(BF16)
+        if m:
+            spread_out.append(w.send(sends.at[i, 1], got.at[i, 1], lax.bitwise_xor(own, 2 * m)))
+    down_line.collect((4, 5))
+    down_line.total((2, 3))
+
     vec[...] = jnp.zeros_like(vec)
     for row, slot in ((2, 6), (3, 2), (4, 4), (5, 0), (6, 5), (7, 1)):
         vec[row : row + 1, :] = jnp.sum(acc[slot], axis=0, keepdims=True)
@@ -651,201 +670,43 @@
         vec[8 + k : 9 + k, :] = jnp.where(chip == k, hidden_sum, jnp.zeros_like(hidden_sum))
     for copy in backs:
         copy.wait_recv()
-    hops.finish()
-    w.finish()
-
-
-def middle(heads, x, cot, upout, down_w, proj_bias, hidden_bias, gain, shift):
-    toks, width = x.shape
-    piece = upout.shape[2]
-    ff = 2 * down_w.shape[0]
-    half = toks // 2
-    shape = jax.ShapeDtypeStruct
-    vm = pltpu.VMEM
-    return pl.pallas_call(
-        middle_body,
-        name="middle",
-        out_shape=(
-            shape((toks, width), BF16),
-            shape((toks, width), F32),
-            shape(heads.shape, BF16),
-            shape((16, width), F32),
-            shape((ff // 2, width), BF16),
-        )
-        + (shape((2, piece, width), BF16),) * 4,
-        in_specs=[VM, VM, VM, HBM, HBM] + [VM] * 4,
-        out_specs=(VM,) * 9,
-        scratch_shapes=[
-            vm((toks, width), BF16), vm((width, width), BF16), vm((width, ff), BF16), vm((ff, width), BF16),
-            vm((toks, width), F32), vm((toks, width), F32), vm((toks, 128), F32), vm((toks, width), F32),
-            vm((4, toks, width), BF16), vm((4, toks, ff), BF16), vm((4, toks, ff), F32),
-            vm((4, toks, width), BF16), vm((4, half, width), BF16), vm((2, half, width), BF16),
-            vm((4, toks, width), BF16), vm((4, toks, ff), BF16),
-            vm((4, toks, width), BF16), vm((4, half, width), BF16), vm((2, half, width), BF16),
-            vm((toks, width), BF16), vm((toks, width), BF16), vm((8, 8, width), F32),
-            vm((ff // 2, width), BF16), vm((ff // 2, width), BF16), vm((ff // 2, width), F32),
-            vm((4, piece, ff), BF16), vm((4, piece, ff), BF16), vm((4, piece, ff), F32),
-            vm((4, piece, width), BF16), vm((4, piece, width), BF16), vm((4, piece, width), F32),
-            pltpu.SemaphoreType.DMA((96,)), pltpu.SemaphoreType.DMA((96,)), pltpu.SemaphoreType.DMA((16,)),
-        ],
-        compiler_params=pltpu.CompilerParams(collective_id=1, has_side_effects=True, vmem_limit_bytes=44 << 20),
-    )(heads, x, cot, upout, down_w, proj_bias, hidden_bias, gain, shift)
-
-
-def project_body(x, qkv_w, up_w, out_w, proj_bias, q_out, k_out, v_out, xs, w_full, upout, stage, send_sems, recv_sems, local_sems):
-    w = Wires(send_sems, recv_sems, local_sems)
-    own = w.own
-    core, chip = lax.rem(own, 2), own // 2
-    mate = lax.bitwise_xor(own, 1)
-    toks, width = x.shape
-    piece = qkv_w.shape[0]
-    share = width // 4
-    head_width = share // 2
-    rep = w.rep
-    reps = 4
-    w.greet([(rep, lax.bitwise_xor(own, m)) for m in (1, 2, 4, 6)] + [(lax.rem(rep + 1, reps), own), (lax.rem(rep + reps - 1, reps), own)])
-    mine = rows_of(own, piece)
-    quarter = piece // reps
-
-    def source(part, to_chip):
-        return qkv_w.at[:, pl.ds(pl.multiple_of(part * width + to_chip * share, share), share)]
-
-    arrivals = []
-    for m in (6, 2, 4):
-        peer = lax.bitwise_xor(own, m)
-        copies = [w.send(source(p, lax.bitwise_xor(chip, m // 2)), w_full.at[mine, pl.ds(p * share, share)], peer) for p in range(3)]
-        arrivals.append((peer, copies))
-    fetched = []
-    for m in (6, 2, 4):
-        peer, to_chip = lax.bitwise_xor(own, m), lax.bitwise_xor(chip, m // 2)
-        some = rows_of(rep, quarter)
-        fetched.append(w.send(up_w.at[some, rows_of(to_chip, width)], upout.at[chip, 0, some], peer))
-        fetched.append(w.send(out_w.at[some], upout.at[chip, 1, some], peer))
-    kept = [w.local(up_w.at[:, rows_of(chip, width)], upout.at[chip, 0]), w.local(out_w, upout.at[chip, 1])]
-    others = [lax.bitwise_xor(chip, m) for m in (3, 1, 2)]
-    hops = Hops(w, lambda r: [upout.at[c, 1, rows_of(r, quarter)] for c in others])
-    xs[chip] = x[...]
-    spread = Spread(w, xs, toks // 2)
-    spread.first_half()
-    spread.second_half()
-    here = [w.local(source(p, chip), w_full.at[mine, pl.ds(p * share, share)]) for p in range(3)]
-    theirs = [w.send(source(p, chip), w_full.at[mine, pl.ds(p * share, share)], mate) for p in range(3)]
-    for peer, copies in arrivals:
-        for copy in copies:
+
+    got_up, got_out = spread_up, spread_out
+    side_line = Line(w, y_own.at[pl.ds(2 * piece, 2 * piece)], upout_sum.at[pl.ds(2 * piece, 2 * piece)], y_far.at[pl.ds(2 * piece, 2 * piece)], 4)
+    out_line = Line(w, y_own.at[pl.ds(4 * piece, piece)], upout_sum.at[pl.ds(4 * piece, piece)], y_far.at[pl.ds(4 * piece, piece)], 2)
+    lines = [Line(w, l_own.at[p], qkv_sum.at[p], l_far.at[p], 4) for p in range(3)]
+
+    def side_start():
+        for copy in got_up:
             copy.wait_recv()
-        rows = rows_of(peer, piece)
-        theirs.append(w.send(w_full.at[rows], w_full.at[rows], mate))
-    for copy in fetched:
-        copy.wait_recv()
-    hops.start(1)
-    for copy in here:
-        copy.wait()
-    for copy in theirs:
-        copy.wait_recv()
-    outs = (q_out, k_out, v_out)
-    swaps = []
-
-    def block(k):
-        rows = rows_of(2 * k + core, toks)
-        for p in range(3):
-            r = nn(xs[k], w_full[:, pl.ds(p * share, share)])
-            if p != 1:
-                r = r + proj_bias[p // 2 : p // 2 + 1, rows_of(chip, share)]
-            stage[k, :, pl.ds(p * share, share)] = r.astype(BF16)
-            swaps.append(w.send(stage.at[k, :, pl.ds(pl.multiple_of(p * share + (1 - core) * head_width, head_width), head_width)], outs[p].at[rows], mate))
-            outs[p][rows, :] = stage[k, :, pl.ds(pl.multiple_of(p * share + core * head_width, head_width), head_width)]
-
-    block(chip)
-    spread.relay()
-    hops.wait(1)
-    hops.start(2)
-    spread.wait_sides()
-    block(spread.cx)
-    block(spread.cy)
-    hops.wait(2)
-    hops.start(3)
-    spread.wait_diagonal()
-    block(spread.cd)
-    for copy in swaps:
-        copy.wait_recv()
-    hops.wait(3)
-    for copy in kept:
-        copy.wait()
-    hops.finish()
-    w.finish()
-
-
-def project(x, qkv_w, up_w, out_w, proj_bias):
-    toks, width = x.shape
-    piece = qkv_w.shape[0]
-    shape = jax.ShapeDtypeStruct
-    vm = pltpu.VMEM
-    heads = shape((8 * toks, width // 8), BF16)
-    return pl.pallas_call(
-        project_body,
-        name="project",
-        out_shape=(heads, heads, heads, shape((4, toks, width), BF16), shape((8 * piece, 3 * width // 4), BF16), shape((4, 2, piece, width), BF16)),
-        in_specs=[VM, VM, HBM, HBM, VM],
-        out_specs=(VM,) * 5 + (HBM,),
-        scratch_shapes=[
-            vm((4, toks, 3 * width // 4), BF16),
-            pltpu.SemaphoreType.DMA((72,)), pltpu.SemaphoreType.DMA((72,)), pltpu.SemaphoreType.DMA((8,)),
-        ],
-        compiler_params=pltpu.CompilerParams(collective_id=0, has_side_effects=True, vmem_limit_bytes=40 << 20),
-    )(x, qkv_w, up_w, out_w, proj_bias)
-
-
-def backward_body(
-    scale, seg, q, k, v, g, o, lse, xs, w_full, branch_grad, vec, down, keep, to_x, to_y, to_d,
-    input_grad, qkv_sum, upout_sum, down_sum, vec_sum,
-    corr, kt, dk_acc, dv_acc, dqt, seg_c, heads, grads, part, side, last, q_send, q_recv, q_keep, q_piece, l_own, l_far,
-    d_own, d_far, got, y_own, y_far, v_sum, v_recv,
-    send_sems, recv_sems, local_sems,
-):
-    w = Wires(send_sems, recv_sems, local_sems)
-    own, rep = w.own, w.rep
-    core, chip = lax.rem(own, 2), own // 2
-    mate = lax.bitwise_xor(own, 1)
-    toks, width = branch_grad.shape
-    share = width // 4
-    head_width = share // 2
-    piece = keep.shape[1]
-    half = toks // 2
-    tile = 256
-    z1, z2, z3 = (lax.bitwise_xor(rep, m) for m in (1, 2, 3))
-    w.greet([(rep, lax.bitwise_xor(own, m)) for m in (1, 2, 4, 6)] + [(z1, own), (z2, own), (z3, own)])
-
-    spread = [w.send(ref, got.at[i], lax.bitwise_xor(own, m)) for i, (m, ref) in enumerate(((6, to_d), (2, to_x), (4, to_y)))]
-    d_own[...] = down[...]
-    down_line = Line(w, d_own, down_sum, d_far, 8)
-    down_line.start()
-    upout_line = Line(w, y_own, upout_sum, y_far, 10)
-    lines = [Line(w, l_own.at[p], qkv_sum.at[p], l_far.at[p], 4) for p in range(3)]
-
-    def upout_start():
-        for copy in spread:
+        for row, i in ((2, 1), (3, 2)):
+            y_own[row * piece : (row + 1) * piece, :] = got[i, 0]
+        side_line.start()
+
+    def out_start():
+        for copy in got_out:
             copy.wait_recv()
-        for i, ref in enumerate((keep, got.at[1], got.at[2], got.at[0])):
-            y_own[i * piece : (i + 1) * piece, :] = ref[0]
-        y_own[4 * piece :, :] = (keep[1].astype(F32) + got[0, 1].astype(F32) + got[1, 1].astype(F32) + got[2, 1].astype(F32)).astype(BF16)
-        upout_line.start()
+        y_own[4 * piece :, :] = (sends[3, 1].astype(F32) + got[0, 1].astype(F32) + got[1, 1].astype(F32) + got[2, 1].astype(F32)).astype(BF16)
+        out_line.start()
 
     hooks = {
-        0: lambda: down_line.collect((0,)),
-        1: lambda: (down_line.collect((1,)), down_line.total((0,))),
-        2: lambda: (down_line.collect((2, 3)), down_line.total((1,))),
-        3: lambda: (down_line.collect((4,)), down_line.total((2, 3))),
-        4: lambda: (down_line.collect((5, 6)), down_line.total((4,))),
-        5: lambda: (upout_start(), down_line.collect((7,)), down_line.total((5, 6))),
-        6: lambda: (down_line.total((7,)), upout_line.collect((0,))),
-        7: lambda: (upout_line.collect((1,)), upout_line.total((0,))),
+        0: lambda: (down_line.collect((6, 7)), down_line.total((4, 5))),
+        1: lambda: down_line.total((6,)),
+        2: lambda: up_line.collect((0,)),
+        3: lambda: (side_start(), down_line.total((7,))),
+        4: lambda: (up_line.collect((1,)), up_line.total((0,))),
+        6: lambda: (up_line.collect((2,)), up_line.total((1,))),
+        7: lambda: (up_line.collect((3,)), up_line.total((2,))),
     }
 
-    length, head_cols = q.shape
-    headd = head_cols // 2
-    blocks = length // BQ
-    first = head_lanes((BQ, head_cols), headd)
-    seg_columns(seg, seg_c)
+    grads = stage
+
+    def head_cols_of(p, core_index):
+        return pl.ds(pl.multiple_of((2 * p + core_index) * head_width, head_width), head_width)
+
+    length, head_cols = q_out.shape
+    q, k, v, g, o = q_out, k_out, v_out, grad_heads, o_out
+    dk_acc = o_out
 
     @pl.loop(0, blocks)
     def _(i):
@@ -853,7 +714,9 @@
         prod = jnp.transpose(g[rows, :].astype(F32) * o[rows, :])
         corr[0:1, rows] = jnp.sum(prod[:headd], axis=0, keepdims=True)
         corr[1:2, rows] = jnp.sum(prod[headd:], axis=0, keepdims=True)
-        kt[:, rows] = jnp.transpose(k[rows, :])
+        t = jnp.transpose(k[rows, :])
+        for h in range(2):
+            vt[h, 0:headd, rows] = t[h * headd : (h + 1) * headd]
         dk_acc[rows, :] = jnp.zeros((BQ, head_cols), F32)
         dv_acc[rows, :] = jnp.zeros((BQ, head_cols), F32)
 
@@ -882,12 +745,12 @@
                 dscore = (p * (dp - corr[h : h + 1, rows])).astype(BF16)
                 ps.append(p.astype(BF16))
                 ds.append(dscore)
-                dq[h] = dq[h] + nn(kt[h * headd : (h + 1) * headd, cols], dscore)
+                dq[h] = dq[h] + nn(vt[h, 0:headd, cols], dscore)
             dv_acc[cols, :] += nn(jnp.concatenate(ps, axis=1), gz)
             dk_acc[cols, :] += nn(jnp.concatenate(ds, axis=1), qz)
         dqt[0:headd, :] = dq[0]
         dqt[headd:, :] = dq[1]
-        heads[0, lax.rem(i, 2), i // 2] = (jnp.transpose(dqt[...]) * scale).astype(BF16)
+        act[i // 2, :, head_cols_of(0, lax.rem(i, 2))] = (jnp.transpose(dqt[...]) * scale).astype(BF16)
         for at, hook in hooks.items():
 
             @pl.when(i == at)
@@ -897,20 +760,21 @@
     @pl.loop(0, blocks)
     def _(i):
         rows = rows_of(i, BQ)
-        heads[1, lax.rem(i, 2), i // 2] = dk_acc[rows, :].astype(BF16)
-        heads[2, lax.rem(i, 2), i // 2] = dv_acc[rows, :].astype(BF16)
-
+        act[i // 2, :, head_cols_of(1, lax.rem(i, 2))] = dk_acc[rows, :].astype(BF16)
+        act[i // 2, :, head_cols_of(2, lax.rem(i, 2))] = dv_acc[rows, :].astype(BF16)
+
+    gather2.drain()
     swaps = []
     for p in range(3):
         cols = pl.ds(pl.multiple_of(p * share + core * head_width, head_width), head_width)
-        swaps.append(w.send(heads.at[p, 1 - core], grads.at[:, :, cols], mate))
-        grads[:, :, cols] = heads[p, core]
-    upout_line.collect((2,))
+        swaps.append(w.send(act.at[:, :, head_cols_of(p, 1 - core)], grads.at[:, :, cols], mate))
+        grads[:, :, cols] = act[:, :, head_cols_of(p, core)]
     v_sum[...] = vec[...]
     for row, p in ((0, 0), (1, 2)):
-        total = jnp.sum(heads[p].reshape(8 * toks, head_width).astype(F32), axis=0, keepdims=True)
+        total = jnp.sum(act[:, :, 2 * p * head_width : 2 * (p + 1) * head_width].reshape(4 * toks, 2 * head_width).astype(F32), axis=0, keepdims=True)
+        total = total[:, 0:head_width] + total[:, head_width:]
         v_sum[row : row + 1, rows_of(own, head_width)] = total
-    rounds = [(None, mate), (None, lax.bitwise_xor(own, 2)), (None, lax.bitwise_xor(own, 4)), (z1, own), (z2, own)]
+    rounds = [(None, mate), (None, lax.bitwise_xor(own, 2)), (None, lax.bitwise_xor(own, 4)), (lax.bitwise_xor(rep, 1), own), (lax.bitwise_xor(rep, 2), own)]
     flying = []
 
     def vec_start(i):
@@ -941,19 +805,14 @@
 
         return w.send(q_send.at[p], q_recv.at[p], mate)
 
-    def ours(p):
+    moved = []
+
+    def pieces(p, copy):
+        copy.wait_recv()
+
         @pl.loop(0, 4)
         def _(kk):
-            q_keep[p, kk] = qkv_rows(core, kk, p)
-
-    moved = []
-
-    def pieces(p, copy):
-        copy.wait_recv()
-
-        @pl.loop(0, 4)
-        def _(kk):
-            q_piece[p, kk] = (q_keep[p, kk] + q_recv[p, kk].astype(F32)).astype(BF16)
+            q_piece[p, kk] = (qkv_rows(core, kk, p) + q_recv[p, kk].astype(F32)).astype(BF16)
 
         cols = rows_of(chip, share)
         moved.append([w.send(q_piece.at[p, lax.bitwise_xor(chip, m // 2)], l_own.at[p, :, cols], lax.bitwise_xor(own, m)) for m in (6, 2, 4)])
@@ -966,24 +825,22 @@
 
     swaps[0].wait_recv()
     copies = [theirs(0)]
-    ours(0)
-    upout_line.collect((3,))
-    upout_line.total((1,))
+    up_line.total((3,))
+    side_line.collect((0,))
     swaps[1].wait_recv()
     copies.append(theirs(1))
     pieces(0, copies[0])
-    upout_line.collect((4,))
-    upout_line.total((2,))
-    ours(1)
+    out_start()
     swaps[2].wait_recv()
     copies.append(theirs(2))
-    upout_line.collect((5,))
-    upout_line.total((3,))
     pieces(1, copies[1])
-    ours(2)
-    upout_line.collect((6,))
-    upout_line.total((4,))
+    side_line.collect((1,))
+    side_line.total((0,))
+    up_line.arrive(range(4))
+    far_copy = w.send(upout_sum.at[pl.ds(piece, piece)], got.at[0, 0], lax.bitwise_xor(own, 6))
     pieces(2, copies[2])
+    side_line.collect((2,))
+    side_line.total((1,))
     vec_step(0)
 
     def partial(kk):
@@ -995,22 +852,23 @@
     gather = Gather(w, part, side, last, half)
     partial(gather.cd)
     gather.send_diagonal()
-    line_start(0)
+    side_line.collect((3,))
+    side_line.total((2,))
     partial(gather.cx)
     gather.send_x()
-    line_start(1)
-    upout_line.collect((7,))
-    upout_line.total((5, 6))
+    line_start(0)
     partial(gather.cy)
     gather.send_y()
+    line_start(1)
+    out_line.collect((0,))
+    side_line.total((3,))
+    partial(chip)
     line_start(2)
-    partial(chip)
-    upout_line.collect((8,))
-    upout_line.total((7,))
+    out_line.collect((1,))
+    out_line.total((0,))
     vec_step(1)
-    upout_line.collect((9,))
+    out_line.total((1,))
     gather.relay()
-    upout_line.total((8, 9))
     vec_step(2)
     step = 32
 
@@ -1039,60 +897,87 @@
     for at in range(8, len(order) + 2):
         hop(at)
     down_line.arrive(range(8))
-    upout_line.arrive(range(10))
-    for line in lines:
-        line.arrive(range(4))
-    for line in [down_line, upout_line] + lines:
+    spill = [w.local(down_sum, h_down)]
+    side_line.arrive(range(4))
+    out_line.arrive(range(2))
+    far_copy.wait_recv()
+    for to, src_ref in ((0, upout_sum.at[pl.ds(0, piece)]), (1, got.at[0, 0])):
+        spill.append(w.local(src_ref, h_upout.at[pl.ds(to * piece, piece)]))
+    spill.append(w.local(upout_sum.at[pl.ds(2 * piece, 3 * piece)], h_upout.at[pl.ds(2 * piece, 3 * piece)]))
+    for p in range(3):
+        lines[p].arrive(range(4))
+        spill.append(w.local(qkv_sum.at[p], h_qkv.at[p]))
+    spill += [w.local(s, d) for s, d in ((output, h_output), (input_grad, h_input_grad), (vec_sum, h_vec))]
+    for line in [down_line, up_line, side_line, out_line] + lines:
         line.finish()
+    for copy in spill:
+        copy.wait()
+    qkv_hops.finish()
+    hops.finish()
     w.finish()
 
 
-def backward(scale, seg, q, k, v, g, o, lse, xs, w_full, branch_grad, vec, down, keep, to_x, to_y, to_d):
-    toks, width = branch_grad.shape
-    length, head_cols = q.shape
-    piece = keep.shape[1]
+def layer(scale, seg, x, cot, qkv_w, up_w, out_w, down_w, proj_bias, hidden_bias, gain, shift):
+    toks, width = x.shape
+    piece = up_w.shape[0]
+    ff = 2 * down_w.shape[0]
+    half = toks // 2
     share = width // 4
-    half = toks // 2
+    head_width = width // 8
+    length = 8 * toks
     shape = jax.ShapeDtypeStruct
     vm = pltpu.VMEM
+    five = (5 * piece, width)
     small = vm((3, 4, piece, share), BF16)
-    five = vm((5 * piece, width), BF16)
-    line = vm((3, piece, width), BF16)
+    three = (3, piece, width)
+    rows4 = vm((4, toks, width), BF16)
+    block = vm((toks, width), BF16)
+    block32 = vm((toks, width), F32)
+    pieces = vm((4, piece, width), BF16)
+    halfff = vm((ff // 2, width), BF16)
+    heads = vm((length, head_width), BF16)
+    heads32 = vm((length, head_width), F32)
     return pl.pallas_call(
-        functools.partial(backward_body, scale),
-        name="backward",
+        functools.partial(layer_body, scale),
+        name="layer",
         out_shape=(
-            shape((toks, width), BF16), shape((3, piece, width), BF16), shape((5 * piece, width), BF16), shape(down.shape, BF16), shape(vec.shape, F32),
+            shape((toks, width), BF16), shape((toks, width), BF16), shape(three, BF16), shape(five, BF16), shape((ff // 2, width), BF16), shape((16, width), F32),
         ),
-        in_specs=[VM] * 16,
-        out_specs=(VM,) * 5,
+        in_specs=[VM, VM, VM, VM, HBM, HBM, HBM] + [VM] * 4,
+        out_specs=(HBM,) * 6,
         scratch_shapes=[
-            vm((8, length), F32), vm((head_cols, length), BF16), vm((length, head_cols), F32), vm((length, head_cols), F32),
-            vm((head_cols, BQ), F32), vm((length, 128), F32), vm((3, 2, 4, toks, head_cols), BF16),
-            vm((4, toks, 3 * share), BF16),
-            vm((4, toks, width), BF16), vm((4, half, width), BF16), vm((2, half, width), BF16),
-            small, small, vm((3, 4, piece, share), F32), small, line, line,
-            vm(down.shape, BF16), vm(down.shape, BF16), vm((3, 2, piece, width), BF16), five, five,
-            vm(vec.shape, F32), vm((9,) + vec.shape, F32),
-            pltpu.SemaphoreType.DMA((160,)), pltpu.SemaphoreType.DMA((160,)), pltpu.SemaphoreType.DMA((8,)),
+            heads, heads, heads, heads32, vm((8, length), F32), rows4, vm((8 * piece, 3 * share), BF16), block, block32, heads, vm((16, width), F32), halfff,
+            vm((4, 2, piece, width), BF16),
+            vm((4, toks, 3 * share), BF16), vm((2, head_width // 2 + 16, length), BF16), heads32, heads, block,
+            vm((width, width), BF16), vm((width, ff), BF16), vm((ff, width), BF16), block32, block32, vm((toks, 128), F32),
+            rows4, vm((4, toks, ff), BF16), vm((4, toks, ff), BF16), rows4, vm((4, half, width), BF16), vm((2, half, width), BF16), rows4, vm((4, toks, ff), BF16),
+            block, block, vm((8, 8, width), F32), halfff, halfff, halfff, halfff, pieces, pieces, pieces, pieces,
+            vm((8, length), F32), heads32, vm((head_width, BQ), F32), small, small, small, vm(three, BF16), vm(three, BF16), vm((3, 2, piece, width), BF16),
+            vm(five, BF16), vm(five, BF16), vm(five, BF16), vm(three, BF16), block, vm((16, width), F32), vm((9, 16, width), F32), vm((16, width), F32),
+            pltpu.SemaphoreType.DMA((320,)), pltpu.SemaphoreType.DMA((320,)), pltpu.SemaphoreType.DMA((40,)),
         ],
-        compiler_params=pltpu.CompilerParams(collective_id=2, has_side_effects=True, vmem_limit_bytes=34 << 20),
-    )(seg, q, k, v, g, o, lse, xs, w_full, branch_grad, vec, down, keep, to_x, to_y, to_d)
+        compiler_params=pltpu.CompilerParams(collective_id=1, has_side_effects=True, vmem_limit_bytes=63 << 20),
+    )(seg, x, cot, qkv_w, up_w, out_w, down_w, proj_bias, hidden_bias, gain, shift)
 
 
 def emit_body(
-    grad_scale, who, low, grad, qkv_sum, upout_sum, down_sum, vec_sum,
+    grad_scale, who, h_low, h_grad, h_qkv, h_upout, h_down, h_vec,
     output, input_grad, qkv_total, out_total, up_total, down_total, bias_total, hidden_total, gain_total, shift_total,
+    qkv_sum, upout_sum, down_sum, vec_sum, sems,
 ):
-    width = low.shape[1]
+    width = h_low.shape[1]
     piece = qkv_sum.shape[1]
-    output[...] = low[...]
-    input_grad[...] = grad[...]
+    pairs = ((h_down, down_sum), (h_upout, upout_sum), (h_qkv, qkv_sum), (h_vec, vec_sum), (h_low, output), (h_grad, input_grad))
+    copies = [pltpu.make_async_copy(src, dst, sems.at[i]) for i, (src, dst) in enumerate(pairs)]
+    for copy in copies:
+        copy.start()
+    for copy in copies:
+        copy.wait()
     for p in range(3):
         qkv_total[:, p * width : (p + 1) * width] = qkv_sum[p].astype(F32) * grad_scale
     chip = who[0]
-    for m in range(4):
-        up_total[:, rows_of(lax.bitwise_xor(chip, m), width)] = upout_sum[m * piece : (m + 1) * piece, :].astype(F32) * grad_scale
+    for at, m in enumerate((0, 3, 1, 2)):
+        up_total[:, rows_of(lax.bitwise_xor(chip, m), width)] = upout_sum[at * piece : (at + 1) * piece, :].astype(F32) * grad_scale
     out_total[...] = upout_sum[4 * piece :, :].astype(F32) * grad_scale
     down_total[...] = down_sum[...].astype(F32) * grad_scale
     bias_total[...] = vec_sum[0:4] * grad_scale
@@ -1113,9 +998,13 @@
             shape((toks, width), BF16), shape((toks, width), BF16), shape((piece, 3 * width), F32), shape((piece, width), F32), shape((piece, 4 * width), F32),
             shape(down_sum.shape, F32), shape((4, width), F32), shape((1, 4 * width), F32), shape((2, width), F32), shape((2, width), F32),
         ),
-        in_specs=[SM] + [VM] * 6,
+        in_specs=[SM] + [HBM] * 6,
         out_specs=(VM,) * 10,
-        compiler_params=pltpu.CompilerParams(vmem_limit_bytes=32 << 20),
+        scratch_shapes=[
+            pltpu.VMEM(qkv_sum.shape, BF16), pltpu.VMEM(upout_sum.shape, BF16), pltpu.VMEM(down_sum.shape, BF16), pltpu.VMEM(vec_sum.shape, F32),
+            pltpu.SemaphoreType.DMA((6,)),
+        ],
+        compiler_params=pltpu.CompilerParams(vmem_limit_bytes=62 << 20),
     )(who, low, grad, qkv_sum, upout_sum, down_sum, vec_sum)
 
 
@@ -1124,13 +1013,8 @@
     toks, width = inputs.shape
     scale = (width // HEADS) ** (-0.5)
     grad_scale = (toks * lax.axis_size("fsdp") * lax.axis_size("rep")) ** (-0.5)
-    queries, key_rows, value_rows, xs, w_full, upout = project(inputs, qkv_weight, up_weight, out_weight, proj_bias)
-    attended, attended_low, lse = attn_fwd(scale, segment_ids, queries, key_rows, value_rows)
-    low, branch_grad, grad_heads, vec, down, keep, to_x, to_y, to_d = middle(
-        attended_low, inputs, cotangent[0], upout, down_weight, proj_bias, hidden_bias[None], norm_gain, norm_shift
-    )
-    grad, qkv_sum, upout_sum, down_sum, vec_sum = backward(
-        scale, segment_ids, queries, key_rows, value_rows, grad_heads, attended, lse, xs, w_full, branch_grad, vec, down, keep, to_x, to_y, to_d
+    low, grad, qkv_sum, upout_sum, down_sum, vec_sum = layer(
+        scale, segment_ids, inputs, cotangent[0], qkv_weight, up_weight, out_weight, down_weight, proj_bias, hidden_bias[None], norm_gain, norm_shift
     )
     output, input_grad, qkv_total, out_total, up_total, down_total, bias_total, hidden_total, gain_total, shift_total = emit(
         grad_scale, (lax.axis_index("fsdp") // 2).reshape(1), low, grad, qkv_sum, upout_sum, down_sum, vec_sum

time: 287 us -> 260 us (0.906)
  Pallas kernels: 277 us -> 259 us
  local copies, waits for them, and re-layouts: 10 us -> 0 us
    pallas_call x4 -> x1, Pallas kernels: 274 us -> 253 us  [layer(): pl.pallas_call(functools.partial(layer_body, scale), name='layer', out_sh...]
    unnamed x38 -> x0, local copies, waits for them, and re-layouts: 10 us -> none
where the time goes in v5:
time: 260 us; the launch traced here: 259 us
  Pallas kernels  259 us (100%)
    pallas_call x1, Pallas kernels, layer(): pl.pallas_call(functools.partial(layer_body, scale), name='layer', out_sh...  253 us
    pallas_call x1, Pallas kernels, emit(): pl.pallas_call(functools.partial(emit_body, grad_scale), name='emit', out...  5.69 us

profile of v5, /device:TPU:0, one launch (start us, length us, event | category | flops | bytes accessed | tf_op | source)
XLA Modules:
  0.0 259.4 jit_solution(17266025417828676367)
XLA Ops:
  0.7 252.9 %layer.1 = (bf16[256,1024]{1,0:T(8,128)(2,1)}, bf16[256,1024]{1,0:T(8,128)(2,1)}, bf16[3,128,1024]{2,1,0:T(8,128)(2,1)}, bf16[640,1024]{1,0:T(8,128)(2,1)}, bf16...) custom-call(s32[1,2048]{1,0:T(1,128)} %seg.1, bf16[256,1024]{1,0:T(8,128)(2,1)} %bitcast.7, bf16[256,1024]{1,0:T(8,128)(2,1)} %bitcast.8, ...), custom_call_target="tpu_custom_call" | custom-call | tf_op jit(solution)/shard_map/layer/pallas_call | solution.py:940
  253.5 5.7 %emit.1 = (bf16[256,1024]{1,0:T(8,128)(2,1)}, bf16[256,1024]{1,0:T(8,128)(2,1)}, f32[128,3072]{1,0:T(8,128)}, f32[128,1024]{1,0:T(8,128)}, f32[128,4096]{1,0:T(8...) custom-call(s32[1]{0:T(128)} %bitcast.who, ...), custom_call_target="tpu_custom_call" | custom-call | tf_op jit(solution)/shard_map/emit/pallas_call | solution.py:994

commit v6 on v5

--- a/solution.py
+++ b/solution.py
@@ -674,7 +674,7 @@
     got_up, got_out = spread_up, spread_out
     side_line = Line(w, y_own.at[pl.ds(2 * piece, 2 * piece)], upout_sum.at[pl.ds(2 * piece, 2 * piece)], y_far.at[pl.ds(2 * piece, 2 * piece)], 4)
     out_line = Line(w, y_own.at[pl.ds(4 * piece, piece)], upout_sum.at[pl.ds(4 * piece, piece)], y_far.at[pl.ds(4 * piece, piece)], 2)
-    lines = [Line(w, l_own.at[p], qkv_sum.at[p], l_far.at[p], 4) for p in range(3)]
+    lines = [Line(w, l_own.at[p], qkv_sum.at[p], l_far.at[p], 2) for p in range(3)]
 
     def side_start():
         for copy in got_up:
@@ -851,50 +851,51 @@
 
     gather = Gather(w, part, side, last, half)
     partial(gather.cd)
-    gather.send_diagonal()
     side_line.collect((3,))
     side_line.total((2,))
+    line_start(0)
     partial(gather.cx)
+    line_start(1)
+    partial(gather.cy)
+    line_start(2)
+    gather.send_diagonal()
     gather.send_x()
-    line_start(0)
-    partial(gather.cy)
     gather.send_y()
-    line_start(1)
     out_line.collect((0,))
     side_line.total((3,))
     partial(chip)
-    line_start(2)
     out_line.collect((1,))
     out_line.total((0,))
     vec_step(1)
-    out_line.total((1,))
-    gather.relay()
-    vec_step(2)
     step = 32
 
     def final_rows(which, t):
         rows = pl.ds(pl.multiple_of(which * half + t * step, step), step)
         input_grad[rows, :] = (branch_grad[rows, :] + gather.total(which, t * step, step)).astype(BF16)
 
-    order = [(p, i) for p in range(3) for i in range(4)]
+    order = [(p, i) for p in range(3) for i in range(2)]
 
     def hop(at):
         if at < len(order):
             lines[order[at][0]].collect((order[at][1],))
-        if at >= 2:
-            lines[order[at - 2][0]].total((order[at - 2][1],))
-
-    for at in range(5):
+        if at >= 1:
+            lines[order[at - 1][0]].total((order[at - 1][1],))
+
+    hop(0)
+    out_line.total((1,))
+    hop(1)
+    gather.relay()
+    vec_step(2)
+    for at in range(2, 4):
         hop(at)
     vec_step(3)
     gather.wait_first()
     pl.loop(0, half // step)(functools.partial(final_rows, 0))
-    for at in range(5, 8):
-        hop(at)
+    hop(4)
     vec_step(4)
     gather.wait_second()
     pl.loop(0, half // step)(functools.partial(final_rows, 1))
-    for at in range(8, len(order) + 2):
+    for at in range(5, len(order) + 1):
         hop(at)
     down_line.arrive(range(8))
     spill = [w.local(down_sum, h_down)]
@@ -905,7 +906,7 @@
         spill.append(w.local(src_ref, h_upout.at[pl.ds(to * piece, piece)]))
     spill.append(w.local(upout_sum.at[pl.ds(2 * piece, 3 * piece)], h_upout.at[pl.ds(2 * piece, 3 * piece)]))
     for p in range(3):
-        lines[p].arrive(range(4))
+        lines[p].arrive(range(2))
         spill.append(w.local(qkv_sum.at[p], h_qkv.at[p]))
     spill += [w.local(s, d) for s, d in ((output, h_output), (input_grad, h_input_grad), (vec_sum, h_vec))]
     for line in [down_line, up_line, side_line, out_line] + lines:
@@ -962,8 +963,8 @@
 
 def emit_body(
     grad_scale, who, h_low, h_grad, h_qkv, h_upout, h_down, h_vec,
-    output, input_grad, qkv_total, out_total, up_total, down_total, bias_total, hidden_total, gain_total, shift_total,
-    qkv_sum, upout_sum, down_sum, vec_sum, sems,
+    output, input_grad, h_qkv_total, h_out_total, h_up_total, h_down_total, bias_total, hidden_total, gain_total, shift_total,
+    qkv_sum, upout_sum, down_sum, vec_sum, qkv_total, out_total, up_total, down_total, sems,
 ):
     width = h_low.shape[1]
     piece = qkv_sum.shape[1]
@@ -971,20 +972,35 @@
     copies = [pltpu.make_async_copy(src, dst, sems.at[i]) for i, (src, dst) in enumerate(pairs)]
     for copy in copies:
         copy.start()
-    for copy in copies:
-        copy.wait()
+    chip = who[0]
+    sent = []
+
+    def leave(src, dst):
+        copy = pltpu.make_async_copy(src, dst, sems.at[6 + len(sent)])
+        copy.start()
+        sent.append(copy)
+
+    copies[0].wait()
+    down_total[...] = down_sum[...].astype(F32) * grad_scale
+    leave(down_total, h_down_total)
+    copies[1].wait()
+    for at, m in enumerate((0, 3, 1, 2)):
+        up_total[:, rows_of(lax.bitwise_xor(chip, m), width)] = upout_sum[at * piece : (at + 1) * piece, :].astype(F32) * grad_scale
+    leave(up_total, h_up_total)
+    out_total[...] = upout_sum[4 * piece :, :].astype(F32) * grad_scale
+    leave(out_total, h_out_total)
+    copies[2].wait()
     for p in range(3):
         qkv_total[:, p * width : (p + 1) * width] = qkv_sum[p].astype(F32) * grad_scale
-    chip = who[0]
-    for at, m in enumerate((0, 3, 1, 2)):
-        up_total[:, rows_of(lax.bitwise_xor(chip, m), width)] = upout_sum[at * piece : (at + 1) * piece, :].astype(F32) * grad_scale
-    out_total[...] = upout_sum[4 * piece :, :].astype(F32) * grad_scale
-    down_total[...] = down_sum[...].astype(F32) * grad_scale
+    leave(qkv_total, h_qkv_total)
+    copies[3].wait()
     bias_total[...] = vec_sum[0:4] * grad_scale
     gain_total[...] = vec_sum[4:6] * grad_scale
     shift_total[...] = vec_sum[6:8] * grad_scale
     for kk in range(4):
         hidden_total[:, kk * width : (kk + 1) * width] = vec_sum[8 + kk : 9 + kk] * grad_scale
+    for copy in copies[4:] + sent:
+        copy.wait()
 
 
 def emit(grad_scale, who, low, grad, qkv_sum, upout_sum, down_sum, vec_sum):
@@ -999,10 +1015,11 @@
             shape(down_sum.shape, F32), shape((4, width), F32), shape((1, 4 * width), F32), shape((2, width), F32), shape((2, width), F32),
         ),
         in_specs=[SM] + [HBM] * 6,
-        out_specs=(VM,) * 10,
+        out_specs=(VM, VM) + (HBM,) * 4 + (VM,) * 4,
         scratch_shapes=[
             pltpu.VMEM(qkv_sum.shape, BF16), pltpu.VMEM(upout_sum.shape, BF16), pltpu.VMEM(down_sum.shape, BF16), pltpu.VMEM(vec_sum.shape, F32),
-            pltpu.SemaphoreType.DMA((6,)),
+            pltpu.VMEM((piece, 3 * width), F32), pltpu.VMEM((piece, width), F32), pltpu.VMEM((piece, 4 * width), F32), pltpu.VMEM(down_sum.shape, F32),
+            pltpu.SemaphoreType.DMA((10,)),
         ],
         compiler_params=pltpu.CompilerParams(vmem_limit_bytes=62 << 20),
     )(who, low, grad, qkv_sum, upout_sum, down_sum, vec_sum)

time: 260 us -> 256 us (0.985)
  Pallas kernels: 259 us -> 255 us
    pallas_call x1, Pallas kernels: 253 us -> 250 us  [layer(): pl.pallas_call(functools.partial(layer_body, scale), name='layer', out_sh...]
where the time goes in v6:
time: 256 us
  Pallas kernels  255 us (100%)
    pallas_call x1, Pallas kernels, layer(): pl.pallas_call(functools.partial(layer_body, scale), name='layer', out_sh...  250 us
    pallas_call x1, Pallas kernels, emit(): pl.pallas_call(functools.partial(emit_body, grad_scale), name='emit', out...  5.13 us

profile of v6, /device:TPU:0, one launch (start us, length us, event | category | flops | bytes accessed | tf_op | source)
XLA Modules:
  0.0 255.5 jit_solution(3055855568454825779)
XLA Ops:
  0.7 249.5 %layer.1 = (bf16[256,1024]{1,0:T(8,128)(2,1)}, bf16[256,1024]{1,0:T(8,128)(2,1)}, bf16[3,128,1024]{2,1,0:T(8,128)(2,1)}, bf16[640,1024]{1,0:T(8,128)(2,1)}, bf16...) custom-call(s32[1,2048]{1,0:T(1,128)} %seg.1, bf16[256,1024]{1,0:T(8,128)(2,1)} %bitcast.7, bf16[256,1024]{1,0:T(8,128)(2,1)} %bitcast.8, ...), custom_call_target="tpu_custom_call" | custom-call | tf_op jit(solution)/shard_map/layer/pallas_call | solution.py:941
  250.2 5.1 %emit.1 = (bf16[256,1024]{1,0:T(8,128)(2,1)}, bf16[256,1024]{1,0:T(8,128)(2,1)}, f32[128,3072]{1,0:T(8,128)}, f32[128,1024]{1,0:T(8,128)}, f32[128,4096]{1,0:T(8...) custom-call(s32[1]{0:T(128)} %bitcast.who, ...), custom_call_target="tpu_custom_call" | custom-call | tf_op jit(solution)/shard_map/emit/pallas_call | solution.py:1010

commit v7 on v6

--- a/solution.py
+++ b/solution.py
@@ -439,7 +439,7 @@
             def _(mask=mask):
                 swaps[mask].start()
 
-        @pl.when(t == 2)
+        @pl.when(t == 1)
         def _():
             hops.wait(2)
             hops.start(3)
@@ -447,14 +447,20 @@
     w.sent.extend(swaps.values())
     att[:, rows_of(own, head_width)] = low[rows_of(own, toks), :]
     hops.wait(3)
-    for k in others:
-        rows = rows_of(2 * k + core, piece)
-        for full in (out_full, up_full):
-            kept.append((None, w.send(full.at[rows], full.at[rows], mate)))
-    for local, remote in kept:
-        if local is not None:
-            local.wait()
-        remote.wait_recv()
+    later = kept[:1] + kept[2:]
+    soon = kept[1:2]
+    for full, group in ((out_full, soon), (up_full, later)):
+        for k in others:
+            rows = rows_of(2 * k + core, piece)
+            group.append((None, w.send(full.at[rows], full.at[rows], mate)))
+
+    def settle(group):
+        for local, remote in group:
+            if local is not None:
+                local.wait()
+            remote.wait_recv()
+
+    settle(soon)
     for copy in swaps.values():
         copy.wait_recv()
 
@@ -496,6 +502,7 @@
             cols = rows_of(n, tile)
             part[k, :, cols] = nn(act[k], down_full[:, cols]).astype(BF16)
 
+    settle(later)
     forward(chip)
     gather = Gather(w, part, side, last, half)
     spread.relay()

time: 256 us -> 254 us (level)
  no operation moved by 1% of the time
where the time goes in v7:
time: 254 us
  Pallas kernels  253 us (100%)
    pallas_call x1, Pallas kernels, layer(): pl.pallas_call(functools.partial(layer_body, scale), name='layer', out_sh...  248 us
    pallas_call x1, Pallas kernels, emit(): pl.pallas_call(functools.partial(emit_body, grad_scale), name='emit', out...  5.13 us

profile of v7, /device:TPU:0, one launch (start us, length us, event | category | flops | bytes accessed | tf_op | source)
XLA Modules:
  0.0 253.7 jit_solution(1329009972721403696)
XLA Ops:
  0.7 247.7 %layer.1 = (bf16[256,1024]{1,0:T(8,128)(2,1)}, bf16[256,1024]{1,0:T(8,128)(2,1)}, bf16[3,128,1024]{2,1,0:T(8,128)(2,1)}, bf16[640,1024]{1,0:T(8,128)(2,1)}, bf16...) custom-call(s32[1,2048]{1,0:T(1,128)} %seg.1, bf16[256,1024]{1,0:T(8,128)(2,1)} %bitcast.7, bf16[256,1024]{1,0:T(8,128)(2,1)} %bitcast.8, ...), custom_call_target="tpu_custom_call" | custom-call | tf_op jit(solution)/shard_map/layer/pallas_call | solution.py:948
  248.4 5.1 %emit.1 = (bf16[256,1024]{1,0:T(8,128)(2,1)}, bf16[256,1024]{1,0:T(8,128)(2,1)}, f32[128,3072]{1,0:T(8,128)}, f32[128,1024]{1,0:T(8,128)}, f32[128,4096]{1,0:T(8...) custom-call(s32[1]{0:T(128)} %bitcast.who, ...), custom_call_target="tpu_custom_call" | custom-call | tf_op jit(solution)/shard_map/emit/pallas_call | solution.py:1017
